TPU v7x, 128 devices: a whole 4x4x4 slice. The times are simulated.
128 devices in a mesh: bin: 16 (over z_lo, x, core), trk: 8 (over y, z_hi).
Axes of the slice: x: 4, y: 4, z: 4 (z_hi: 2, z_lo: 2; z = z_hi * 2 + z_lo), core: 2. Of those that a mesh axis runs over, the one named last changes fastest.
Arguments:
- trunk: bfloat16 [8192, 1536], P(('bin', 'trk')), may hold values from -6 to 6
- norm_gain: float32 [1536], replicated, may hold values from 0.1 to 1.9
- w_query: bfloat16 [1536, 1024], replicated, may hold values from -0.4375 to 0.4375
- w_kv: bfloat16 [1536, 256], replicated, may hold values from -0.15625 to 0.15625
- w_out: bfloat16 [1024, 1536], replicated, may hold values from -0.1875 to 0.1875
- w_up: bfloat16 [1536, 768], replicated, may hold values from -0.15625 to 0.15625
- skip: bfloat16 [32768, 768], P(('bin', 'trk')), may hold values from -6 to 6
- conv_w: bfloat16 [5, 768, 768], replicated, may hold values from -0.09375 to 0.09375
- head_w: bfloat16 [768, 6144], P(None, 'trk'), may hold values from -0.21875 to 0.21875
- head_bias: float32 [6144], P('trk'), may hold values from -4 to 4
- targets: bfloat16 [32768, 6144], P('bin', 'trk'), may hold values from 0.049804688 to 4
- missing: int32 [8192], P('bin'), may hold values 0 or 1
- group_ids: int32 [6144, 1], replicated, may hold values from 0 to 10
- group_weight: float32 [11], replicated, may hold values from 0.25 to 4
Outputs:
- prediction: bfloat16 [32768, 6144], P('bin', 'trk')
- head_grad: float32 [768, 6144], P('bin', 'trk')
- feature_grad: bfloat16 [32768, 768], P(('bin', 'trk'))
Inputs may be any that keep to these rules, and one draw needn't show every extreme that they name: `group_ids`: every group id is held by at least one track.
All inputs are finite; a program needn't handle non-finite values. No bound on the sum of `missing` on one device may be relied on, other than what follows from the above.
Results may differ from a plain program's by a relative error of at most 0.019.
Values may be sent and summed in bfloat16 or wider, within the bound.
No kernel may reach another device: no remote copies, remote signals or barrier semaphores. Data moves between devices by JAX's collectives and lax.ppermute only.
A program may use at most 128 MiB of HBM per device.

v0:
```python
import math

import jax
import jax.numpy as jnp
from jax import lax
from jax.sharding import PartitionSpec as P

logit_cap = 20.0


def padded_2(value, sides, width):
    for axis, dim in sides:
        size, length = (lax.axis_size(axis), value.shape[dim])
        up = [(i, (i + 1) % size) for i in range(size - 1)]
        down = [(j, i) for i, j in up]
        last = lax.slice_in_dim(value, length - width, length, axis=dim)
        initial = lax.slice_in_dim(value, 0, width, axis=dim)
        before = lax.ppermute(last, axis, up)
        after = lax.ppermute(initial, axis, down)
        value = jnp.concatenate([before, value, after], axis=dim)
    return value


def attend_block(state_pair, queries, key_block, value_block, score_scale):
    numerator, denominator = state_pair
    scores = (
        jnp.einsum("rhd,nd->rhn", queries, key_block, preferred_element_type=jnp.float32)
        * score_scale
    )
    scores = logit_cap * jnp.tanh(scores / logit_cap)
    exp_weights = jnp.exp(scores)
    numerator = numerator + jnp.einsum(
        "rhn,nd->rhd",
        exp_weights.astype(jnp.bfloat16),
        value_block,
        preferred_element_type=jnp.float32,
    )
    denominator = denominator + jnp.sum(exp_weights, axis=2)
    return (numerator, denominator)


def make_folder(queries, head_dim):
    score_scale = 1.0 / math.sqrt(head_dim)

    def fold(accum, key_piece, offset):
        piece_rows = key_piece.shape[0]
        block_rows = math.gcd(piece_rows, 2048)
        stacked = key_piece.reshape(piece_rows // block_rows, block_rows, key_piece.shape[1])

        def fold_step(running, one_block):
            updated = attend_block(
                running, queries, one_block[:, :head_dim], one_block[:, head_dim:], score_scale
            )
            return (updated, None)

        result, _ = lax.scan(fold_step, accum, stacked)
        return result

    return fold


def body(
    trunk,
    norm_gain,
    w_query,
    w_kv,
    w_out,
    w_up,
    skip,
    conv_w,
    head_w,
    head_bias,
    targets,
    missing,
    group_ids,
    group_weight,
):
    row_count = trunk.shape[0]
    head_dim = w_kv.shape[1] // 2
    head_count = w_query.shape[1] // head_dim
    widened = trunk.astype(jnp.float32)
    meansq = jnp.mean(widened * widened, axis=1, keepdims=True)
    normed = (widened * lax.rsqrt(meansq + 1e-06) * norm_gain).astype(jnp.bfloat16)
    queries = (
        jnp.dot(normed, w_query, preferred_element_type=jnp.float32)
        .astype(jnp.bfloat16)
        .reshape(row_count, head_count, head_dim)
    )
    keyvals = jnp.dot(normed, w_kv, preferred_element_type=jnp.float32).astype(jnp.bfloat16)
    start_pair = (
        jnp.zeros((row_count, head_count, head_dim), jnp.float32),
        jnp.zeros((row_count, head_count), jnp.float32),
    )
    folder = make_folder(queries, head_dim)
    numerator, denominator = folder(
        start_pair, lax.all_gather(keyvals, ("bin", "trk"), axis=0, tiled=True), jnp.int32(0)
    )
    attended = (
        (numerator / denominator[:, :, None])
        .astype(jnp.bfloat16)
        .reshape(row_count, head_count * head_dim)
    )
    hidden = (widened + jnp.dot(attended, w_out, preferred_element_type=jnp.float32)).astype(
        jnp.bfloat16
    )
    upward = jnp.dot(hidden, w_up, preferred_element_type=jnp.float32)
    factor = skip.shape[0] // row_count
    upsampled = (jnp.repeat(upward, factor, axis=0) + skip.astype(jnp.float32)).astype(jnp.bfloat16)
    tap_count = conv_w.shape[0]
    rim_width = tap_count // 2
    padded = padded_2(upsampled, ((("bin", "trk"), 0),), rim_width)
    pos_count = upsampled.shape[0]
    windows = jnp.concatenate([padded[tap : tap + pos_count] for tap in range(tap_count)], axis=1)
    kernel_flat = conv_w.reshape(tap_count * conv_w.shape[1], conv_w.shape[2])
    conved = jnp.dot(windows, kernel_flat, preferred_element_type=jnp.float32)
    feature = (upsampled.astype(jnp.float32) + jax.nn.gelu(conved)).astype(jnp.bfloat16)
    panel_feat = lax.all_gather(feature, "trk", axis=0, tiled=True)
    logits = jnp.dot(panel_feat, head_w, preferred_element_type=jnp.float32) + head_bias
    smooth = jax.nn.softplus(logits)
    prediction = smooth.astype(jnp.bfloat16)
    tile_width = head_w.shape[1]
    groups = group_weight.shape[0]
    total_tracks = group_ids.shape[0]
    labels = jnp.arange(groups, dtype=jnp.int32)
    counts = jnp.sum((group_ids == labels[None, :]).astype(jnp.int32), axis=0)
    per_group = group_weight * total_tracks / (groups * counts.astype(jnp.float32))
    local_ids = lax.dynamic_slice_in_dim(
        group_ids, lax.axis_index("trk") * tile_width, tile_width, 0
    )
    track_scale = jnp.sum(jnp.where(local_ids == labels[None, :], per_group[None, :], 0.0), axis=1)
    keep_mask = 1.0 - jnp.repeat(missing.astype(jnp.float32), factor)[:, None]
    misfit = smooth - targets.astype(jnp.float32)
    slope_grad = (keep_mask * track_scale[None, :] * misfit * jax.nn.sigmoid(logits)).astype(
        jnp.bfloat16
    )
    positions = panel_feat.shape[0] * lax.axis_size("bin")
    product = lax.dot_general(
        panel_feat, slope_grad, (((0,), (0,)), ((), ())), preferred_element_type=jnp.float32
    )
    head_grad = lax.psum_scatter(
        (product / positions).astype(jnp.bfloat16), "bin", scatter_dimension=0, tiled=True
    ).astype(jnp.float32)
    partial_value = lax.dot_general(
        slope_grad, head_w, (((1,), (1,)), ((), ())), preferred_element_type=jnp.float32
    )
    feature_grad = lax.psum_scatter(
        partial_value.astype(jnp.bfloat16), "trk", scatter_dimension=0, tiled=True
    )
    return (prediction, head_grad, feature_grad)


def solution(mesh):
    in_specs = (
        P(("bin", "trk"), None),
        P(),
        P(),
        P(),
        P(),
        P(),
        P(("bin", "trk"), None),
        P(),
        P(None, "trk"),
        P("trk"),
        P("bin", "trk"),
        P("bin"),
        P(),
        P(),
    )
    out_specs = (P("bin", "trk"), P("bin", "trk"), P(("bin", "trk"), None))
    return jax.shard_map(body, mesh=mesh, in_specs=in_specs, out_specs=out_specs, check_vma=False)
```

profile of v0, /device:TPU:0, one launch (start us, length us, event | category | flops | bytes accessed | tf_op | source)
XLA Modules:
  0.0 599.8 jit_solution(18380595523179321211)
XLA Ops:
  8.5 2.2 convolution_convert_fusion.2
  12.4 306.4 %all-gather.3.cloned.1.call-done = bf16[8192,256]{1,0:T(8,128)(2,1)} async-done(((bf16[64,256]{1,0:T(8,128)(2,1)}), bf16[8192,256]{1,0:T(8,128)(2,1)}) %all-gather.3.cloned.1.call-update) | async-done | bytes 4194320 | tf_op jit(solution)/shard_map/all_gather | solution.py:96
  318.8 22.4 %while.15 = (s32[]{:T(128)}, f32[64,8,128]{2,0,1:T(8,128)S(1)}, f32[64,8]{0,1:T(8,128)S(1)}, bf16[4,2048,256]{2,1,0:T(8,128)(2,1)}, bf16[64,8,128]{2,0,1:T(8,128)(2,1)S(1)}, /*index=5*/s32[]{:T(128)}, s32[]{:T(128)}) while((s32[]{:T(128)}, f32[64,8,128]{2,0,1:T(8,128)S(1)}, f32[64,8]{0,1:T(8,128)S(1)}, ...), condition=%wide.region_3.4_spmd.clone, body=%wide.region_1.3_spmd.clone.sunk | while | flops 541196800 | bytes 12198016 | solution.py:56
  318.8 2.3 dynamic-slice_bitcast_fusion.2
  321.1 2.5 bitcast_reduce_fusion.2
  324.4 2.3 dynamic-slice_bitcast_fusion.2
  326.7 2.5 bitcast_reduce_fusion.2
  330.0 2.3 dynamic-slice_bitcast_fusion.2
  332.3 2.5 bitcast_reduce_fusion.2
  335.6 2.3 dynamic-slice_bitcast_fusion.2
  337.9 2.5 bitcast_reduce_fusion.2
  341.2 4.4 fusion.4
  345.7 1.9 broadcast_in_dim.34
  347.6 2.3 reshape.46
  351.2 4.5 collective-permute-start
  357.3 5.4 collective-permute-done.1
  363.0 5.3 fusion.14
  369.2 65.0 %all-gather.5.cloned.1.call-done = bf16[2048,768]{1,0:T(8,128)(2,1)} async-done(((bf16[256,768]{1,0:T(8,128)(2,1)}), bf16[2048,768]{1,0:T(8,128)(2,1)}) %all-gather.5.cloned.1.call-update) | async-done | bytes 3145744 | tf_op jit(solution)/shard_map/all_gather | solution.py:117
  434.2 10.5 %multiply_convert_fusion = (bf16[2048,768]{1,0:T(8,128)(2,1)S(1)}, bf16[2048,768]{1,0:T(8,128)(2,1)}) fusion(bf16[2048,768]{1,0:T(8,128)(2,1)} %param.26, f32[768]{0:T(1024)S(1)} %select_reduce_fusion, f32[2048]{0:T(1024)S(1)} %sub.20, f32[768]{0:T(1024)S(1)} %copy-done.5, bf16[2048,768]{1,0:T(8,128)(2,1)} %all-gather.5.cloned.1.call-done, ...), kind=kOutput, calls=%fused_computation.10 | convolution fusion | flops 2442657792 | bytes 13776896 | tf_op jit(solution)/shard_map/dot_general | solution.py:118
  444.7 1.7 copy-done.7
  446.4 3.7 multiply_convert_fusion.1
  450.2 6.5 %convolution_convert_fusion = bf16[2048,768]{1,0:T(8,128)(2,1)} fusion(bf16[2048,768]{1,0:T(8,128)(2,1)} %copy-done.7, bf16[768,768]{1,0:T(8,128)(2,1)} %param.24), kind=kOutput, calls=%fused_computation.12 | convolution fusion | flops 2417491968 | bytes 7471104 | tf_op jit(solution)/shard_map/dot_general | solution.py:143
  456.7 53.6 %reduce-scatter.3.cloned.1.call-done = bf16[48,768]{1,0:T(8,128)(2,1)} async-done(((bf16[768,768]{1,0:T(8,128)(2,1)}), bf16[48,768]{1,0:T(8,128)(2,1)}) %reduce-scatter.3.cloned.1.call-update) | async-done | bytes 73744 | tf_op jit(solution)/shard_map/reduce_scatter | solution.py:140
  511.9 81.4 %reduce-scatter.5.cloned.1.call-done = bf16[256,768]{1,0:T(8,128)(2,1)} async-done(((bf16[2048,768]{1,0:T(8,128)(2,1)}), bf16[256,768]{1,0:T(8,128)(2,1)}) %reduce-scatter.5.cloned.1.call-update) | async-done | bytes 393232 | tf_op jit(solution)/shard_map/reduce_scatter | solution.py:146
  (60 shorter events, 11.6 us)
Async XLA Ops:
  7.2 3.6 copy-start
  7.2 311.6 %all-gather.3.cloned.1.call-start = ((), (), s32[]{:S(2)}) async-start(), calls=%async_computation.2 | async-start | bytes 4227072 | tf_op jit(solution)/shard_map/all_gather | solution.py:96
  10.7 423.5 %all-gather.5.cloned.1.call-start = ((), (), s32[]{:S(2)}) async-start(), calls=%async_computation.3 | async-start | bytes 3538944 | tf_op jit(solution)/shard_map/all_gather | solution.py:117
  321.1 2.5 copy-start.1
  326.7 2.5 copy-start.1
  332.3 2.5 copy-start.1
  337.9 2.5 copy-start.1
  351.2 5.8 collective-permute-start
  355.7 7.0 %collective-permute-start.1 = (bf16[2,768]{1,0:T(2,128)(2,1)S(1)}, bf16[2,768]{1,0:T(2,128)(2,1)S(1)}, u32[]{:S(2)}, u32[]{:S(2)}) collective-permute-start(bf16[2,768]{1,0:T(2,128)(2,1)S(1)} %get-tuple-element.123), channel_id=1, source_target_pairs={{1,0},{2,1},{3,2},{4,3},{5,4},{6,5},{7,6},{8,7},{9,8},{10,9},{11,1... | collective-permute-start | bytes 9224 | tf_op jit(solution)/shard_map/ppermute | solution.py:19
  363.0 5.6 copy-start.3
  363.0 5.9 copy-start.2
  363.0 6.1 %copy-start.6 = (f32[11]{0:T(128)S(1)}, f32[11]{0:T(128)}, u32[]{:S(2)}) copy-start(f32[11]{0:T(128)} %param.29) | copy-start | bytes 136
  363.0 71.2 %copy-start.5 = (f32[768]{0:T(1024)S(1)}, f32[768]{0:T(1024)}, u32[]{:S(2)}) copy-start(f32[768]{0:T(1024)} %param.25) | copy-start | bytes 9220
  368.3 142.1 %reduce-scatter.3.cloned.1.call-start = ((), (), s32[]{:S(2)}) async-start(), calls=%async_computation.4 | async-start | bytes 1253376 | tf_op jit(solution)/shard_map/reduce_scatter | solution.py:140
  434.2 12.2 %copy-start.4 = (bf16[2048,768]{1,0:T(8,128)(2,1)S(1)}, bf16[2048,768]{1,0:T(8,128)(2,1)}, u32[]{:S(2)}) copy-start(bf16[2048,768]{1,0:T(8,128)(2,1)} %all-gather.5.cloned.1.call-done) | copy-start | bytes 9437188
  444.7 1.7 copy-start.7
  450.1 143.2 %reduce-scatter.5.cloned.1.call-start = ((), (), s32[]{:S(2)}) async-start(), calls=%async_computation.5 | async-start | bytes 3538944 | tf_op jit(solution)/shard_map/reduce_scatter | solution.py:146
Sparse Core Ops, SparseCore 0:
  10.8 307.9 all-gather.2
  368.4 65.7 all-gather.4
  450.2 60.0 reduce-scatter.2
  514.7 78.5 reduce-scatter.4
where the time goes:
time: 600 us
  waiting for transfers between devices  512 us (85%)
  matrix products  47.5 us (8%)
  local copies, waits for them, and re-layouts  15.4 us (3%)
  between operations  14 us (2%)
  starting transfers between devices  6.16 us (1%)
    all_gather x1, waiting for transfers between devices, body(): lax.all_gather(keyvals, ('bin', 'trk'), axis=0, tiled=True)  306 us
    reduce_scatter x1, waiting for transfers between devices, body(): lax.psum_scatter(partial_value.astype(jnp.bfloat16), 'trk', scatter_dimen...  81.4 us
    all_gather x1, waiting for transfers between devices, body(): panel_feat = lax.all_gather(feature, 'trk', axis=0, tiled=True)  65 us
    reduce_scatter x1, waiting for transfers between devices, body(): lax.psum_scatter((product / positions).astype(jnp.bfloat16), 'bin', scatt...  53.6 us
  transfers between devices with their start and end apart: 6, of which 5 were waited for; matrix products, arithmetic and copies ran while one was open for 2% of the time, Pallas kernels for 0%

commit v1 on v0

v1 whole, which is shorter than its diff:
```python
import functools
import math

import jax
import jax.numpy as jnp
import numpy as np
from jax import lax
from jax.experimental import pallas as pl
from jax.experimental.pallas import tpu as pltpu
from jax.sharding import Mesh, PartitionSpec as P

logit_cap = 20.0
BIN = ("bz", "core")
TRK = ("y", "zh")
ALL = BIN + TRK


def place(index):
    bz, rest = divmod(index, 16)
    core, rest = divmod(rest, 8)
    y, zh = divmod(rest, 2)
    zlo, x = divmod(bz, 4)
    return (x, y, zh * 2 + zlo, core)


def number(x, y, z, core):
    zh, zlo = divmod(z, 2)
    return ((zlo * 4 + x) * 2 + core) * 8 + y * 2 + zh


def moved(value, dim, step):
    sizes = (4, 4, 4, 2)
    pairs = []
    for index in range(128):
        target = list(place(index))
        target[dim] = (target[dim] + step) % sizes[dim]
        pairs.append((index, number(*target)))
    return lax.ppermute(value, ALL, pairs)


def whole(array):
    return pl.BlockSpec(array.shape, lambda *_: (0,) * array.ndim, pipeline_mode=pl.Buffered(1))


def attend_kernel(head_dim, first, *refs):
    q_ref, refs = refs[0], refs[1:]
    num_ref, den_ref = refs[-2:]
    pieces = refs[:-2] if first else refs[:-4]
    f32, bf16 = jnp.float32, jnp.bfloat16
    heads = q_ref.shape[1] // head_dim
    queries = jnp.concatenate(
        [q_ref[:, h * head_dim : (h + 1) * head_dim] for h in range(heads)], 0
    )
    inner = 1.0 / (math.sqrt(head_dim) * logit_cap)
    outer = logit_cap * math.log2(math.e)
    num = jnp.zeros(num_ref.shape, f32) if first else refs[-4][...]
    den = jnp.zeros(den_ref.shape, f32) if first else refs[-3][...]
    step = 256
    for piece in pieces:
        for start in range(0, piece.shape[0], step):
            keys = piece[start : start + step, :head_dim]
            values = piece[start : start + step, head_dim:]
            scores = lax.dot_general(
                queries, keys, (((1,), (1,)), ((), ())), preferred_element_type=f32
            )
            weights = jnp.exp2(outer * jnp.tanh(scores * inner))
            num = num + jnp.dot(weights.astype(bf16), values, preferred_element_type=f32)
            for lane in range(0, step, 128):
                den = den + weights[:, lane : lane + 128]
    num_ref[...] = num
    den_ref[...] = den


def attend(state, queries, pieces, head_dim):
    rows = queries.shape[0] * queries.shape[1] // head_dim
    operands = [queries, *pieces, *(state or ())]
    keys = sum(piece.shape[0] for piece in pieces)
    return pl.pallas_call(
        functools.partial(attend_kernel, head_dim, state is None),
        grid=(1,),
        in_specs=[whole(operand) for operand in operands],
        out_specs=[pl.BlockSpec((rows, head_dim), lambda i: (0, 0))] * 2,
        out_shape=[jax.ShapeDtypeStruct((rows, head_dim), jnp.float32)] * 2,
        cost_estimate=pl.CostEstimate(
            flops=8 * rows * keys * head_dim,
            transcendentals=2 * rows * keys,
            bytes_accessed=1 << 20,
        ),
        compiler_params=pltpu.CompilerParams(vmem_limit_bytes=24 << 20),
        name="attend",
    )(*operands)


def project_kernel(num_ref, den_ref, trunk_ref, out_ref, up_ref, upward_ref):
    f32, bf16 = jnp.float32, jnp.bfloat16
    rows = trunk_ref.shape[0]
    total = jnp.sum(den_ref[...], axis=1, keepdims=True)
    ratio = (num_ref[...] / total).astype(bf16)
    heads = ratio.shape[0] // rows
    attended = jnp.concatenate([ratio[h * rows : (h + 1) * rows] for h in range(heads)], 1)
    hidden = (
        trunk_ref[...].astype(f32)
        + jnp.dot(attended, out_ref[...], preferred_element_type=f32)
    ).astype(bf16)
    upward_ref[...] = jnp.dot(hidden, up_ref[...], preferred_element_type=f32).astype(bf16)


def project(state, trunk, w_out, w_up):
    operands = (*state, trunk, w_out, w_up)
    out = jax.ShapeDtypeStruct((trunk.shape[0], w_up.shape[1]), jnp.bfloat16)
    return pl.pallas_call(
        project_kernel,
        grid=(1,),
        in_specs=[whole(operand) for operand in operands],
        out_specs=whole(out),
        out_shape=out,
        cost_estimate=pl.CostEstimate(
            flops=2 * trunk.shape[0] * (w_out.size + w_up.size),
            transcendentals=0,
            bytes_accessed=2 * (w_out.size + w_up.size),
        ),
        compiler_params=pltpu.CompilerParams(vmem_limit_bytes=24 << 20),
        name="project",
    )(*operands)


def head_kernel(
    positions, core_ref, up_ref, skip_ref, before_ref, after_ref, conv_ref, head_ref, bias_ref,
    scale_ref, keep_ref, target_ref, pred_ref, partial_ref, mine_ref, theirs_ref, wide, near, total,
):
    f32, bf16 = jnp.float32, jnp.bfloat16
    step = pl.program_id(0)
    rows, channels = pred_ref.shape[0], up_ref.shape[1]
    segments = skip_ref.shape[0] // rows
    bins = up_ref.shape[0] // segments
    factor = rows // bins
    taps = conv_ref.shape[0]
    rim = taps // 2

    @pl.when(step == 0)
    def _():
        wide[0:8, :] = jnp.zeros((8, channels), f32)
        wide[8 - rim : 8, :] = before_ref[...].astype(f32)
        wide[8 + segments * rows : 16 + segments * rows, :] = jnp.zeros((8, channels), f32)
        wide[8 + segments * rows : 8 + segments * rows + rim, :] = after_ref[...].astype(f32)
        row = lax.broadcasted_iota(jnp.int32, (rows, bins), 0)
        col = lax.broadcasted_iota(jnp.int32, (rows, bins), 1) * factor
        spread = jnp.where((row >= col) & (row < col + factor), 1.0, 0.0).astype(bf16)

        def expand(segment, carry):
            at = pl.multiple_of(segment * rows, rows)
            source = pl.multiple_of(segment * bins, bins)
            tall = jnp.dot(spread, up_ref[pl.ds(source, bins), :], preferred_element_type=f32)
            tall = (tall + skip_ref[pl.ds(at, rows), :].astype(f32)).astype(bf16)
            wide[pl.ds(at + 8, rows), :] = tall.astype(f32)
            return carry

        lax.fori_loop(0, segments, expand, 0)
        total[...] = jnp.zeros(total.shape, f32)

    near[...] = wide[pl.ds(pl.multiple_of(step * rows, rows), rows + 16), :]
    conved = jnp.zeros((rows, channels), f32)
    for tap in range(taps):
        begin = 8 - rim + tap
        conved = conved + jnp.dot(
            near[begin : begin + rows, :].astype(bf16), conv_ref[tap], preferred_element_type=f32
        )
    cubic = math.sqrt(2.0 / math.pi) * (conved + 0.044715 * (conved * conved * conved))
    feature = (near[8 : 8 + rows, :] + 0.5 * conved * (1.0 + jnp.tanh(cubic))).astype(bf16)
    logits = jnp.dot(feature, head_ref[...], preferred_element_type=f32) + bias_ref[...]
    decay = jnp.exp(-jnp.abs(logits))
    smooth = jnp.maximum(logits, 0.0) + jnp.log1p(decay)
    sigmoid = jnp.where(logits >= 0.0, 1.0, decay) / (1.0 + decay)
    pred_ref[...] = smooth.astype(bf16)
    misfit = smooth - target_ref[...].astype(f32)
    slope = (keep_ref[...] * scale_ref[...] * misfit * sigmoid).astype(bf16)
    partial_ref[...] = lax.dot_general(
        slope, head_ref[...], (((1,), (1,)), ((), ())), preferred_element_type=f32
    ).astype(bf16)
    total[...] += lax.dot_general(
        feature, slope, (((0,), (0,)), ((), ())), preferred_element_type=f32
    )

    @pl.when(step == segments - 1)
    def _():
        core = core_ref[0]
        pairs, height = 8, channels // 16
        for pair in range(pairs):
            at = pl.multiple_of((2 * pair + core) * height, height)
            other = pl.multiple_of((2 * pair + 1 - core) * height, height)
            into = slice(pair * height, (pair + 1) * height)
            mine_ref[into, :] = total[pl.ds(at, height), :] / positions
            theirs_ref[into, :] = (total[pl.ds(other, height), :] / positions).astype(bf16)


def head_pass(core, up, skip, before, after, conv_w, head_w, bias, scale, keep, targets, positions):
    f32, bf16 = jnp.float32, jnp.bfloat16
    count, channels = skip.shape
    segments = 8
    rows = count // segments
    tracks = head_w.shape[1]
    by_rows = pl.BlockSpec((rows, tracks), lambda i, core: (i, 0))
    operands = (up, skip, before, after, conv_w, head_w, bias, scale)
    half = (channels // 2, tracks)
    return pl.pallas_call(
        functools.partial(head_kernel, positions),
        grid_spec=pltpu.PrefetchScalarGridSpec(
            num_scalar_prefetch=1,
            grid=(segments,),
            in_specs=[whole(operand) for operand in operands]
            + [pl.BlockSpec((rows, 1), lambda i, core: (i, 0)), by_rows],
            out_specs=[
                by_rows,
                pl.BlockSpec((rows, channels), lambda i, core: (i, 0)),
                pl.BlockSpec(half, lambda i, core: (0, 0)),
                pl.BlockSpec(half, lambda i, core: (0, 0)),
            ],
            scratch_shapes=[
                pltpu.VMEM((count + 16, channels), f32),
                pltpu.VMEM((rows + 16, channels), f32),
                pltpu.VMEM((channels, tracks), f32),
            ],
        ),
        out_shape=[
            jax.ShapeDtypeStruct((count, tracks), bf16),
            jax.ShapeDtypeStruct((count, channels), bf16),
            jax.ShapeDtypeStruct(half, f32),
            jax.ShapeDtypeStruct(half, bf16),
        ],
        cost_estimate=pl.CostEstimate(
            flops=2 * count * (conv_w.size + 3 * head_w.size),
            transcendentals=4 * count * tracks,
            bytes_accessed=24 << 20,
        ),
        compiler_params=pltpu.CompilerParams(vmem_limit_bytes=44 << 20),
        name="head_pass",
    )(core, *operands, keep, targets)


def body(
    trunk,
    norm_gain,
    w_query,
    w_kv,
    w_out,
    w_up,
    skip,
    conv_w,
    head_w,
    head_bias,
    targets,
    missing,
    group_ids,
    group_weight,
):
    f32, bf16 = jnp.float32, jnp.bfloat16
    row_count = trunk.shape[0]
    head_dim = w_kv.shape[1] // 2
    head_count = w_query.shape[1] // head_dim
    skip_all = lax.all_gather(skip, TRK, axis=0, tiled=True)
    widened = trunk.astype(f32)
    meansq = jnp.mean(widened * widened, axis=1, keepdims=True)
    normed = (widened * lax.rsqrt(meansq + 1e-06) * norm_gain).astype(bf16)
    keyvals = jnp.dot(normed, w_kv, preferred_element_type=f32).astype(bf16)
    for dim in (2, 1):
        keyvals = jnp.concatenate([keyvals] + [moved(keyvals, dim, step) for step in (1, 3, 2)], 0)
    queries = jnp.dot(normed, w_query, preferred_element_type=f32).astype(bf16)
    crossed = moved(keyvals, 3, 1)
    pieces = [moved(keyvals, 0, step) for step in (1, 3, 2)]
    state = attend(None, queries, [keyvals], head_dim)
    for piece in pieces:
        state = attend(state, queries, [crossed, piece], head_dim)
        crossed = moved(piece, 3, 1)
    state = attend(state, queries, [crossed], head_dim)
    upward = project(state, trunk, w_out, w_up)
    n_trk = lax.axis_size(TRK)
    upward_all = lax.all_to_all(
        jnp.broadcast_to(upward[None], (n_trk,) + upward.shape), TRK, 0, 0, tiled=True
    ).reshape(n_trk * row_count, upward.shape[1])
    factor = skip.shape[0] // row_count
    tap_count, channels = conv_w.shape[:2]
    rim = tap_count // 2
    pos_count = skip_all.shape[0]
    n_bin = lax.axis_size(BIN)
    up_pairs = [(i, i + 1) for i in range(n_bin - 1)]
    last = upward_all[-1:].astype(f32) + skip_all[pos_count - rim :].astype(f32)
    first = upward_all[:1].astype(f32) + skip_all[:rim].astype(f32)
    before = lax.ppermute(last.astype(bf16), BIN, up_pairs)
    after = lax.ppermute(first.astype(bf16), BIN, [(j, i) for i, j in up_pairs])
    tile_width = head_w.shape[1]
    groups = group_weight.shape[0]
    total_tracks = group_ids.shape[0]
    labels = jnp.arange(groups, dtype=jnp.int32)
    counts = jnp.sum((group_ids == labels[None, :]).astype(jnp.int32), axis=0)
    per_group = group_weight * total_tracks / (groups * counts.astype(f32))
    local_ids = lax.dynamic_slice_in_dim(group_ids, lax.axis_index(TRK) * tile_width, tile_width, 0)
    track_scale = jnp.sum(jnp.where(local_ids == labels[None, :], per_group[None, :], 0.0), axis=1)
    keep_mask = 1.0 - jnp.repeat(missing.astype(f32), factor)[:, None]
    core = lax.axis_index("core")
    prediction, partial_value, mine, theirs = head_pass(
        core[None].astype(jnp.int32),
        upward_all,
        skip_all,
        before,
        after,
        conv_w,
        head_w,
        head_bias[None, :],
        track_scale[None, :],
        keep_mask,
        targets,
        pos_count * n_bin,
    )
    arrived = lax.all_to_all(
        partial_value.reshape(n_trk, pos_count // n_trk, channels), TRK, 0, 0, tiled=True
    )
    feature_grad = jnp.sum(arrived.astype(f32), axis=0).astype(bf16)
    pair_sum = (mine + lax.ppermute(theirs, "core", [(0, 1), (1, 0)]).astype(f32)).astype(bf16)
    pair_sum = pair_sum.reshape(lax.axis_size("bz"), channels // n_bin, tile_width)
    gathered = lax.all_to_all(pair_sum, "bz", 0, 0, tiled=True)
    head_grad = jnp.sum(gathered.astype(f32), axis=0)
    return (prediction, head_grad, feature_grad)


def solution(mesh):
    inner = Mesh(np.asarray(mesh.devices).reshape(8, 2, 4, 2), ALL)
    in_specs = (
        P(ALL, None),
        P(),
        P(),
        P(),
        P(),
        P(),
        P(ALL, None),
        P(),
        P(None, TRK),
        P(TRK),
        P(BIN, TRK),
        P(BIN),
        P(),
        P(),
    )
    out_specs = (P(BIN, TRK), P(BIN, TRK), P(ALL, None))
    return jax.shard_map(body, mesh=inner, in_specs=in_specs, out_specs=out_specs, check_vma=False)
```

time: 600 us -> 216 us (0.36)
  waiting for transfers between devices: 512 us -> 92.1 us
  Pallas kernels: 0 us -> 44.5 us
  matrix products: 47.5 us -> 3.2 us
  starting transfers between devices: 6.16 us -> 30.7 us
  blocking collectives: 0 us -> 17 us
  local copies, waits for them, and re-layouts: 15.4 us -> 5.36 us
    all_gather x2 -> x1, waiting for transfers between devices: 371 us -> 0.02 us  [body(): skip_all = lax.all_gather(skip, TRK, axis=0, tiled=True)]
    reduce_scatter x2 -> x0, waiting for transfers between devices: 135 us -> none  [the longest x1 81.4 us: body(): lax.psum_scatter(partial_value.astype(jnp.bfloat16), 'trk', scatter_dimen...]
    all_to_all x0 -> x2, waiting for transfers between devices: none -> 57.6 us  [the longest x1 43.5 us: body(): lax.all_to_all(partial_value.reshape(n_trk, pos_count // n_trk, channels)...]
    pallas_call x0 -> x7, Pallas kernels: none -> 44.5 us  [the longest x1 37.6 us: head_pass(): pl.pallas_call(functools.partial(head_kernel, positions), grid_spec=pltpu...]
    dot_general x15 -> x2, matrix products: 47.5 us -> 3.2 us  [the longest x1 1.63 us: body(): queries = jnp.dot(normed, w_query, preferred_element_type=f32).astype(bf16)]
    ppermute x2 -> x16, waiting for transfers between devices: 5.44 us -> 33.8 us  [the longest x13 32.1 us: moved(): return lax.ppermute(value, ALL, pairs)]
    all_to_all x0 -> x1, blocking collectives: none -> 17 us  [body(): gathered = lax.all_to_all(pair_sum, 'bz', 0, 0, tiled=True)]
    ppermute x2 -> x16, starting transfers between devices: 5.82 us -> 22 us  [the longest x13 16.5 us: moved(): return lax.ppermute(value, ALL, pairs)]
  transfers between devices with their start and end apart: 6 -> 19, of which waited for: 5 -> 9; matrix products, arithmetic and copies ran while one was open for 2% -> 4% of each run, Pallas kernels for 0% -> 3%
where the time goes in v1:
time: 216 us; the launch traced here: 215 us
  waiting for transfers between devices  92.1 us (43%)
  Pallas kernels  44.5 us (21%)
  starting transfers between devices  30.7 us (14%)
  blocking collectives  17 us (8%)
  between operations  14.3 us (7%)
  other arithmetic  8.12 us (4%)
  local copies, waits for them, and re-layouts  5.36 us (2%)
  matrix products  3.2 us (1%)
    all_to_all x1, waiting for transfers between devices, body(): lax.all_to_all(partial_value.reshape(n_trk, pos_count // n_trk, channels)...  43.5 us
    pallas_call x1, Pallas kernels, head_pass(): pl.pallas_call(functools.partial(head_kernel, positions), grid_spec=pltpu...  37.6 us
    ppermute x13, waiting for transfers between devices, moved(): return lax.ppermute(value, ALL, pairs)  32.1 us
    all_to_all x1, blocking collectives, body(): gathered = lax.all_to_all(pair_sum, 'bz', 0, 0, tiled=True)  17 us
    ppermute x13, starting transfers between devices, moved(): return lax.ppermute(value, ALL, pairs)  16.5 us
    all_to_all x1, waiting for transfers between devices, body(): lax.all_to_all(jnp.broadcast_to(upward[None], (n_trk,) + upward.shape), T...  14.1 us
    pallas_call x5, Pallas kernels, attend(): pl.pallas_call(functools.partial(attend_kernel, head_dim, state is None),...  5.91 us
    all_to_all x1, starting transfers between devices, body(): lax.all_to_all(partial_value.reshape(n_trk, pos_count // n_trk, channels)...  4.48 us
  transfers between devices with their start and end apart: 19, of which 9 were waited for; matrix products, arithmetic and copies ran while one was open for 4% of the time, Pallas kernels for 3%

profile of v1, /device:TPU:0, one launch (start us, length us, event | category | flops | bytes accessed | tf_op | source)
XLA Modules:
  0.0 215.4 jit_solution(11873296151881161900)
XLA Ops:
  9.2 1.6 constant_dynamic-update-slice_fusion.6
  10.8 4.0 %collective-permute-start.2 = (bf16[64,256]{1,0:T(8,128)(2,1)S(1)}, bf16[64,256]{1,0:T(8,128)(2,1)S(1)}, u32[]{:S(2)}, u32[]{:S(2)}) collective-permute-start(bf16[64,256]{1,0:T(8,128)(2,1)S(1)} %get-tuple-element.36), channel_id=1, source_target_pairs={{0,1},{1,0},{2,3},{3,2},{4,5},{5,4},{6,7},{7,6},{8,9},{9,8},{10,11... | collective-permute-start | bytes 98312 | tf_op jit(solution)/shard_map/ppermute | solution.py:38
  16.8 1.9 collective-permute-done.1
  18.7 1.9 collective-permute-done
  20.7 3.3 %collective-permute-start.5 = (bf16[256,256]{1,0:T(8,128)(2,1)S(1)}, bf16[256,256]{1,0:T(8,128)(2,1)S(1)}, u32[]{:S(2)}, u32[]{:S(2)}) collective-permute-start(bf16[256,256]{1,0:T(8,128)(2,1)S(1)} %pad_maximum_fusion), channel_id=1, source_target_pairs={{0,4},{1,5},{2,6},{3,7},{4,0},{5,1},{6,2},{7,3},{8,12},{9,13},{10,... | collective-permute-start | bytes 393224 | tf_op jit(solution)/shard_map/ppermute | solution.py:38
  26.0 7.2 %collective-permute-done.3 = bf16[256,256]{1,0:T(8,128)(2,1)S(1)} collective-permute-done((bf16[256,256]{1,0:T(8,128)(2,1)S(1)}, bf16[256,256]{1,0:T(8,128)(2,1)S(1)}, u32[]{:S(2)}, u32[]{:S(2)}) %collective-permute-start.3) | collective-permute-done | bytes 131104 | tf_op jit(solution)/shard_map/ppermute | solution.py:38
  33.2 1.6 collective-permute-start.10
  34.8 1.7 collective-permute-start.8
  36.5 1.8 collective-permute-start.6
  38.4 9.9 %collective-permute-done.10.refs_2_ = bf16[1024,256]{1,0:T(8,128)(2,1)S(1)} collective-permute-done((bf16[1024,256]{1,0:T(8,128)(2,1)S(1)}, bf16[1024,256]{1,0:T(8,128)(2,1)S(1)}, u32[]{:S(2)}, u32[]{:S(2)}) %collective-permute-start.10) | collective-permute-done | bytes 524320 | tf_op jit(solution)/shard_map/ppermute | solution.py:38
  48.2 1.4 collective-permute-done.8.refs_2_
  49.7 9.8 %collective-permute-done.6.refs_2_ = bf16[1024,256]{1,0:T(8,128)(2,1)S(1)} collective-permute-done((bf16[1024,256]{1,0:T(8,128)(2,1)S(1)}, bf16[1024,256]{1,0:T(8,128)(2,1)S(1)}, u32[]{:S(2)}, u32[]{:S(2)}) %collective-permute-start.6) | collective-permute-done | bytes 524320 | tf_op jit(solution)/shard_map/ppermute | solution.py:38
  59.5 1.6 convolution_convert_fusion.refs_0_
  69.6 4.2 %all-to-all-start = ((bf16[8,64,768]{2,1,0:T(8,128)(2,1)}), bf16[8,64,768]{2,1,0:T(8,128)(2,1)}, u32[]{:S(2)}, u32[]{:S(2)}) async-start(bf16[8,64,768]{2,1,0:T(8,128)(2,1)} %broadcast_in_dim.36), calls=%async_computation | async-start | bytes 1572864 | tf_op jit(solution)/shard_map/all_to_all | solution.py:277
  74.1 14.1 %all-to-all-done = bf16[8,64,768]{2,1,0:T(8,128)(2,1)} async-done(((bf16[8,64,768]{2,1,0:T(8,128)(2,1)}), bf16[8,64,768]{2,1,0:T(8,128)(2,1)}, u32[]{:S(2)}, u32[]{:S(2)}) %all-to-all-start) | async-done | bytes 786464 | tf_op jit(solution)/shard_map/all_to_all | solution.py:277
  89.7 1.5 collective-permute-start.14
  91.2 3.0 %collective-permute-start.13 = (bf16[2,768]{1,0:T(2,128)(2,1)S(1)}, bf16[2,768]{1,0:T(2,128)(2,1)S(1)}, u32[]{:S(2)}, u32[]{:S(2)}) collective-permute-start(bf16[2,768]{1,0:T(2,128)(2,1)S(1)} %get-tuple-element.34), channel_id=1, source_target_pairs={{0,8},{8,16},{16,24},{24,32},{32,40},{40,48},{48,56},{56,64},{64,7... | collective-permute-start | bytes 9224 | tf_op jit(solution)/shard_map/ppermute | solution.py:288
  98.2 37.6 %head_pass.1 = (bf16[2048,768]{1,0:T(8,128)(2,1)}, bf16[2048,768]{1,0:T(8,128)(2,1)S(1)}, f32[384,768]{1,0:T(8,128)S(1)}, bf16[384,768]{1,0:T(8,128)(2,1)S(1)}) custom-call(s32[1]{0:T(128)} %bitcast.core_ref, bf16[512,768]{1,0:T(8,128)(2,1)} %bitcast.1.up_ref, bf16[2048,768]{1,0:T(8,128)(2,1)} %all-gather.2.cloned.1.call-done.skip_ref, ...), custom_call_target="tpu_custom_call" | custom-call | flops 19327352832 | bytes 25165824 | tf_op jit(solution)/shard_map/head_pass/pallas_call | solution.py:205
  136.8 1.6 collective-permute-done.15
  138.6 17.0 %all_to_all.15 = bf16[8,48,768]{2,1,0:T(8,128)(2,1)} all-to-all(bf16[8,48,768]{2,1,0:T(8,128)(2,1)S(1)} %bitcast.8), channel_id=1, replica_groups=mesh['bz'=8,'core'=2,'y'=4,'zh'=2] {'bz'}, dimensions={0} | all-to-all | bytes 1179648 | tf_op jit(solution)/shard_map/all_to_all | solution.py:320
  155.5 4.5 %all-to-all-start.2 = ((bf16[8,256,768]{2,1,0:T(8,128)(2,1)}), bf16[8,256,768]{2,1,0:T(8,128)(2,1)}, u32[]{:S(2)}, u32[]{:S(2)}) async-start(bf16[8,256,768]{2,1,0:T(8,128)(2,1)} %bitcast.7), calls=%async_computation.2 | async-start | bytes 6291456 | tf_op jit(solution)/shard_map/all_to_all | solution.py:314
  160.0 1.8 convert_reduce_fusion
  161.8 43.5 %all-to-all-done.2 = bf16[8,256,768]{2,1,0:T(8,128)(2,1)} async-done(((bf16[8,256,768]{2,1,0:T(8,128)(2,1)}), bf16[8,256,768]{2,1,0:T(8,128)(2,1)}, u32[]{:S(2)}, u32[]{:S(2)}) %all-to-all-start.2) | async-done | bytes 3145760 | tf_op jit(solution)/shard_map/all_to_all | solution.py:314
  205.4 3.2 %reduce_sum.52 = bf16[256,768]{1,0:T(8,128)(2,1)} reduce(bf16[8,256,768]{2,1,0:T(8,128)(2,1)} %all-to-all-done.2, bf16[]{:T(256)} %constant.33.clone.1), dimensions={0}, to_apply=%region_4.5 | reduce | flops 1376256 | bytes 3538946 | tf_op jit(solution)/shard_map/reduce_sum | solution.py:317
  (71 shorter events, 21.3 us)
Async XLA Ops:
  7.2 52.3 %copy-start = (bf16[1536,1024]{1,0:T(8,128)(2,1)S(1)}, bf16[1536,1024]{1,0:T(8,128)(2,1)}, u32[]{:S(2)}) copy-start(bf16[1536,1024]{1,0:T(8,128)(2,1)} %param.16) | copy-start | bytes 9437188
  7.2 81.8 %all-gather.2.cloned.1.call-start = ((), (), s32[]{:S(2)}) async-start(), calls=%async_computation.3 | async-start | bytes 3538944 | tf_op jit(solution)/shard_map/all_gather | solution.py:260
  10.8 6.1 %collective-permute-start.2 = (bf16[64,256]{1,0:T(8,128)(2,1)S(1)}, bf16[64,256]{1,0:T(8,128)(2,1)S(1)}, u32[]{:S(2)}, u32[]{:S(2)}) collective-permute-start(bf16[64,256]{1,0:T(8,128)(2,1)S(1)} %get-tuple-element.36), channel_id=1, source_target_pairs={{0,1},{1,0},{2,3},{3,2},{4,5},{5,4},{6,7},{7,6},{8,9},{9,8},{10,11... | collective-permute-start | bytes 98312 | tf_op jit(solution)/shard_map/ppermute | solution.py:38
  14.8 3.9 %collective-permute-start.1 = (bf16[64,256]{1,0:T(8,128)(2,1)S(1)}, bf16[64,256]{1,0:T(8,128)(2,1)S(1)}, u32[]{:S(2)}, u32[]{:S(2)}) collective-permute-start(bf16[64,256]{1,0:T(8,128)(2,1)S(1)} %get-tuple-element.36), channel_id=1, source_target_pairs={{0,65},{1,64},{2,67},{3,66},{4,69},{5,68},{6,71},{7,70},{8,73},{9,... | collective-permute-start | bytes 98312 | tf_op jit(solution)/shard_map/ppermute | solution.py:38
  15.5 5.1 %collective-permute-start = (bf16[64,256]{1,0:T(8,128)(2,1)S(1)}, bf16[64,256]{1,0:T(8,128)(2,1)S(1)}, u32[]{:S(2)}, u32[]{:S(2)}) collective-permute-start(bf16[64,256]{1,0:T(8,128)(2,1)S(1)} %get-tuple-element.36), channel_id=1, source_target_pairs={{0,64},{1,65},{2,66},{3,67},{4,68},{5,69},{6,70},{7,71},{8,72},{9,... | collective-permute-start | bytes 98312 | tf_op jit(solution)/shard_map/ppermute | solution.py:38
  20.7 12.6 %collective-permute-start.5 = (bf16[256,256]{1,0:T(8,128)(2,1)S(1)}, bf16[256,256]{1,0:T(8,128)(2,1)S(1)}, u32[]{:S(2)}, u32[]{:S(2)}) collective-permute-start(bf16[256,256]{1,0:T(8,128)(2,1)S(1)} %pad_maximum_fusion), channel_id=1, source_target_pairs={{0,4},{1,5},{2,6},{3,7},{4,0},{5,1},{6,2},{7,3},{8,12},{9,13},{10,... | collective-permute-start | bytes 393224 | tf_op jit(solution)/shard_map/ppermute | solution.py:38
  23.9 9.3 %collective-permute-start.4 = (bf16[256,256]{1,0:T(8,128)(2,1)S(1)}, bf16[256,256]{1,0:T(8,128)(2,1)S(1)}, u32[]{:S(2)}, u32[]{:S(2)}) collective-permute-start(bf16[256,256]{1,0:T(8,128)(2,1)S(1)} %pad_maximum_fusion), channel_id=1, source_target_pairs={{0,6},{1,7},{2,0},{3,1},{4,2},{5,3},{6,4},{7,5},{8,14},{9,15},{10,... | collective-permute-start | bytes 393224 | tf_op jit(solution)/shard_map/ppermute | solution.py:38
  25.0 8.2 %collective-permute-start.3 = (bf16[256,256]{1,0:T(8,128)(2,1)S(1)}, bf16[256,256]{1,0:T(8,128)(2,1)S(1)}, u32[]{:S(2)}, u32[]{:S(2)}) collective-permute-start(bf16[256,256]{1,0:T(8,128)(2,1)S(1)} %pad_maximum_fusion), channel_id=1, source_target_pairs={{0,2},{1,3},{2,4},{3,5},{4,6},{5,7},{6,0},{7,1},{8,10},{9,11},{10,... | collective-permute-start | bytes 393224 | tf_op jit(solution)/shard_map/ppermute | solution.py:38
  33.2 15.0 %collective-permute-start.10 = (bf16[1024,256]{1,0:T(8,128)(2,1)S(1)}, bf16[1024,256]{1,0:T(8,128)(2,1)S(1)}, u32[]{:S(2)}, u32[]{:S(2)}) collective-permute-start(bf16[1024,256]{1,0:T(8,128)(2,1)S(1)} %constant_dynamic-update-slice_fusion.refs_1_), channel_id=1, source_target_pairs={{0,16},{1,17},{2,18},{3,19},{4,20},{5,21},{6,22},{7,23},{8,24},{9,... | collective-permute-start | bytes 1572872 | tf_op jit(solution)/shard_map/ppermute | solution.py:38
  34.8 14.9 %collective-permute-start.8 = (bf16[1024,256]{1,0:T(8,128)(2,1)S(1)}, bf16[1024,256]{1,0:T(8,128)(2,1)S(1)}, u32[]{:S(2)}, u32[]{:S(2)}) collective-permute-start(bf16[1024,256]{1,0:T(8,128)(2,1)S(1)} %constant_dynamic-update-slice_fusion.refs_1_), channel_id=1, source_target_pairs={{0,48},{1,49},{2,50},{3,51},{4,52},{5,53},{6,54},{7,55},{8,56},{9,... | collective-permute-start | bytes 1572872 | tf_op jit(solution)/shard_map/ppermute | solution.py:38
  36.5 22.9 %collective-permute-start.6 = (bf16[1024,256]{1,0:T(8,128)(2,1)S(1)}, bf16[1024,256]{1,0:T(8,128)(2,1)S(1)}, u32[]{:S(2)}, u32[]{:S(2)}) collective-permute-start(bf16[1024,256]{1,0:T(8,128)(2,1)S(1)} %constant_dynamic-update-slice_fusion.refs_1_), channel_id=1, source_target_pairs={{0,32},{1,33},{2,34},{3,35},{4,36},{5,37},{6,38},{7,39},{8,40},{9,... | collective-permute-start | bytes 1572872 | tf_op jit(solution)/shard_map/ppermute | solution.py:38
  38.4 23.7 %collective-permute-start.12 = (bf16[1024,256]{1,0:T(8,128)(2,1)S(1)}, bf16[1024,256]{1,0:T(8,128)(2,1)S(1)}, u32[]{:S(2)}, u32[]{:S(2)}) collective-permute-start(bf16[1024,256]{1,0:T(8,128)(2,1)S(1)} %constant_dynamic-update-slice_fusion.refs_1_), channel_id=1, source_target_pairs={{0,8},{1,9},{2,10},{3,11},{4,12},{5,13},{6,14},{7,15},{8,0},{9,1},... | collective-permute-start | bytes 1572872 | tf_op jit(solution)/shard_map/ppermute | solution.py:38
  48.2 15.3 %collective-permute-start.11 = (bf16[1024,256]{1,0:T(8,128)(2,1)S(1)}, bf16[1024,256]{1,0:T(8,128)(2,1)S(1)}, u32[]{:S(2)}, u32[]{:S(2)}) collective-permute-start(bf16[1024,256]{1,0:T(8,128)(2,1)S(1)} %collective-permute-done.10.refs_2_), channel_id=1, source_target_pairs={{0,8},{1,9},{2,10},{3,11},{4,12},{5,13},{6,14},{7,15},{8,0},{9,1},... | collective-permute-start | bytes 1572872 | tf_op jit(solution)/shard_map/ppermute | solution.py:38
  49.7 15.2 %collective-permute-start.9 = (bf16[1024,256]{1,0:T(8,128)(2,1)S(1)}, bf16[1024,256]{1,0:T(8,128)(2,1)S(1)}, u32[]{:S(2)}, u32[]{:S(2)}) collective-permute-start(bf16[1024,256]{1,0:T(8,128)(2,1)S(1)} %collective-permute-done.8.refs_2_), channel_id=1, source_target_pairs={{0,8},{1,9},{2,10},{3,11},{4,12},{5,13},{6,14},{7,15},{8,0},{9,1},... | collective-permute-start | bytes 1572872 | tf_op jit(solution)/shard_map/ppermute | solution.py:38
  59.5 6.8 %collective-permute-start.7 = (bf16[1024,256]{1,0:T(8,128)(2,1)S(1)}, bf16[1024,256]{1,0:T(8,128)(2,1)S(1)}, u32[]{:S(2)}, u32[]{:S(2)}) collective-permute-start(bf16[1024,256]{1,0:T(8,128)(2,1)S(1)} %collective-permute-done.6.refs_2_), channel_id=1, source_target_pairs={{0,8},{1,9},{2,10},{3,11},{4,12},{5,13},{6,14},{7,15},{8,0},{9,1},... | collective-permute-start | bytes 1572872 | tf_op jit(solution)/shard_map/ppermute | solution.py:38
  67.6 6.4 %copy-start.10 = (f32[11]{0:T(128)S(1)}, f32[11]{0:T(128)}, u32[]{:S(2)}) copy-start(f32[11]{0:T(128)} %param.27) | copy-start | bytes 136
  67.6 6.4 %copy-start.9 = (s32[512]{0:T(512)S(1)}, s32[512]{0:T(512)}, u32[]{:S(2)}) copy-start(s32[512]{0:T(512)} %param.25) | copy-start | bytes 6148
  67.6 26.7 %copy-start.8 = (f32[768]{0:T(1024)S(1)}, f32[768]{0:T(1024)}, u32[]{:S(2)}) copy-start(f32[768]{0:T(1024)} %param.23) | copy-start | bytes 9220
  69.6 18.6 %all-to-all-start = ((bf16[8,64,768]{2,1,0:T(8,128)(2,1)}), bf16[8,64,768]{2,1,0:T(8,128)(2,1)}, u32[]{:S(2)}, u32[]{:S(2)}) async-start(bf16[8,64,768]{2,1,0:T(8,128)(2,1)} %broadcast_in_dim.36), calls=%async_computation | async-start | bytes 1572864 | tf_op jit(solution)/shard_map/all_to_all | solution.py:277
  89.7 6.0 %collective-permute-start.14 = (bf16[2,768]{1,0:T(2,128)(2,1)S(1)}, bf16[2,768]{1,0:T(2,128)(2,1)S(1)}, u32[]{:S(2)}, u32[]{:S(2)}) collective-permute-start(bf16[2,768]{1,0:T(2,128)(2,1)S(1)} %get-tuple-element.33), channel_id=1, source_target_pairs={{8,0},{16,8},{24,16},{32,24},{40,32},{48,40},{56,48},{64,56},{72,6... | collective-permute-start | bytes 9224 | tf_op jit(solution)/shard_map/ppermute | solution.py:289
  91.2 4.5 %collective-permute-start.13 = (bf16[2,768]{1,0:T(2,128)(2,1)S(1)}, bf16[2,768]{1,0:T(2,128)(2,1)S(1)}, u32[]{:S(2)}, u32[]{:S(2)}) collective-permute-start(bf16[2,768]{1,0:T(2,128)(2,1)S(1)} %get-tuple-element.34), channel_id=1, source_target_pairs={{0,8},{8,16},{16,24},{24,32},{32,40},{40,48},{48,56},{56,64},{64,7... | collective-permute-start | bytes 9224 | tf_op jit(solution)/shard_map/ppermute | solution.py:288
  135.8 19.8 %copy-start.3 = (bf16[2048,768]{1,0:T(8,128)(2,1)}, bf16[2048,768]{1,0:T(8,128)(2,1)S(1)}, u32[]{:S(2)}) copy-start(bf16[2048,768]{1,0:T(8,128)(2,1)S(1)} %get-tuple-element.30) | copy-start | bytes 9437188
  135.8 2.7 %collective-permute-start.15 = (bf16[384,768]{1,0:T(8,128)(2,1)S(1)}, bf16[384,768]{1,0:T(8,128)(2,1)S(1)}, u32[]{:S(2)}, u32[]{:S(2)}) collective-permute-start(bf16[384,768]{1,0:T(8,128)(2,1)S(1)} %get-tuple-element.29), channel_id=1, source_target_pairs={{0,8},{8,0},{1,9},{9,1},{2,10},{10,2},{3,11},{11,3},{4,12},{12,4},... | collective-permute-start | bytes 1769480 | tf_op jit(solution)/shard_map/ppermute | solution.py:318
  155.5 49.8 %all-to-all-start.2 = ((bf16[8,256,768]{2,1,0:T(8,128)(2,1)}), bf16[8,256,768]{2,1,0:T(8,128)(2,1)}, u32[]{:S(2)}, u32[]{:S(2)}) async-start(bf16[8,256,768]{2,1,0:T(8,128)(2,1)} %bitcast.7), calls=%async_computation.2 | async-start | bytes 6291456 | tf_op jit(solution)/shard_map/all_to_all | solution.py:314
  (6 other events, 15.9 us)
Sparse Core Ops, SparseCore 0:
  10.3 65.7 all-gather.1

commit v2 on v1

v2 whole, which is shorter than its diff:
```python
import functools
import math

import jax
import jax.numpy as jnp
import numpy as np
from jax import lax
from jax.experimental import pallas as pl
from jax.experimental.pallas import tpu as pltpu
from jax.sharding import Mesh, PartitionSpec as P

logit_cap = 20.0
PARTS = 2
BIN = ("bz", "core")
TRK = ("y", "zh")
ALL = BIN + TRK


def place(index):
    bz, rest = divmod(index, 16)
    core, rest = divmod(rest, 8)
    y, zh = divmod(rest, 2)
    zlo, x = divmod(bz, 4)
    return (x, y, zh * 2 + zlo, core)


def number(x, y, z, core):
    zh, zlo = divmod(z, 2)
    return ((zlo * 4 + x) * 2 + core) * 8 + y * 2 + zh


def moved(value, dim, step):
    sizes = (4, 4, 4, 2)
    pairs = []
    for index in range(128):
        target = list(place(index))
        target[dim] = (target[dim] + step) % sizes[dim]
        pairs.append((index, number(*target)))
    return lax.ppermute(value, ALL, pairs)


def whole(array):
    return pl.BlockSpec(array.shape, lambda *_: (0,) * array.ndim, pipeline_mode=pl.Buffered(1))


def attend_kernel(head_dim, first, *refs):
    q_ref, refs = refs[0], refs[1:]
    num_ref, den_ref = refs[-2:]
    pieces = refs[:-2] if first else refs[:-4]
    f32, bf16 = jnp.float32, jnp.bfloat16
    heads = q_ref.shape[1] // head_dim
    queries = jnp.concatenate(
        [q_ref[:, h * head_dim : (h + 1) * head_dim] for h in range(heads)], 0
    )
    inner = 1.0 / (math.sqrt(head_dim) * logit_cap)
    outer = logit_cap * math.log2(math.e)
    num = jnp.zeros(num_ref.shape, f32) if first else refs[-4][...]
    den = jnp.zeros(den_ref.shape, f32) if first else refs[-3][...]
    step = 512
    for piece in pieces:

        def block(index, pair, piece=piece):
            num, den = pair
            rows = pl.ds(pl.multiple_of(index * step, step), step)
            scores = lax.dot_general(
                queries, piece[rows, :head_dim], (((1,), (1,)), ((), ())), preferred_element_type=f32
            )
            weights = jnp.exp2(outer * jnp.tanh(scores * inner))
            num = num + jnp.dot(
                weights.astype(bf16), piece[rows, head_dim:], preferred_element_type=f32
            )
            for lane in range(0, step, 128):
                den = den + weights[:, lane : lane + 128]
            return num, den

        num, den = lax.fori_loop(0, piece.shape[0] // step, block, (num, den))
    num_ref[...] = num
    den_ref[...] = den


def attend(state, queries, pieces, head_dim):
    rows = queries.shape[0] * queries.shape[1] // head_dim
    operands = [queries, *pieces, *(state or ())]
    keys = sum(piece.shape[0] for piece in pieces)
    return pl.pallas_call(
        functools.partial(attend_kernel, head_dim, state is None),
        grid=(1,),
        in_specs=[whole(operand) for operand in operands],
        out_specs=[pl.BlockSpec((rows, head_dim), lambda i: (0, 0))] * 2,
        out_shape=[jax.ShapeDtypeStruct((rows, head_dim), jnp.float32)] * 2,
        cost_estimate=pl.CostEstimate(
            flops=8 * rows * keys * head_dim,
            transcendentals=2 * rows * keys,
            bytes_accessed=1 << 20,
        ),
        compiler_params=pltpu.CompilerParams(vmem_limit_bytes=24 << 20),
        name="attend",
    )(*operands)


def project_kernel(num_ref, den_ref, trunk_ref, out_ref, up_ref, upward_ref):
    f32, bf16 = jnp.float32, jnp.bfloat16
    rows = trunk_ref.shape[0]
    total = jnp.sum(den_ref[...], axis=1, keepdims=True)
    ratio = (num_ref[...] / total).astype(bf16)
    heads = ratio.shape[0] // rows
    attended = jnp.concatenate([ratio[h * rows : (h + 1) * rows] for h in range(heads)], 1)
    hidden = (
        trunk_ref[...].astype(f32)
        + jnp.dot(attended, out_ref[...], preferred_element_type=f32)
    ).astype(bf16)
    upward_ref[...] = jnp.dot(hidden, up_ref[...], preferred_element_type=f32).astype(bf16)


def project(state, trunk, w_out, w_up):
    operands = (*state, trunk, w_out, w_up)
    out = jax.ShapeDtypeStruct((trunk.shape[0], w_up.shape[1]), jnp.bfloat16)
    return pl.pallas_call(
        project_kernel,
        grid=(1,),
        in_specs=[whole(operand) for operand in operands],
        out_specs=whole(out),
        out_shape=out,
        cost_estimate=pl.CostEstimate(
            flops=2 * trunk.shape[0] * (w_out.size + w_up.size),
            transcendentals=0,
            bytes_accessed=2 * (w_out.size + w_up.size),
        ),
        compiler_params=pltpu.CompilerParams(vmem_limit_bytes=24 << 20),
        name="project",
    )(*operands)


def expand_kernel(at_ref, *refs):
    f32, bf16 = jnp.float32, jnp.bfloat16
    ups, skips, wide = refs[:4], refs[4:8], refs[8]
    bins, channels = ups[0].shape[0] // 2, ups[0].shape[1]
    rows = skips[0].shape[0] // 2
    factor = rows // bins
    row = lax.broadcasted_iota(jnp.int32, (rows, bins), 0)
    col = lax.broadcasted_iota(jnp.int32, (rows, bins), 1) * factor
    spread = jnp.where((row >= col) & (row < col + factor), 1.0, 0.0).astype(bf16)
    wide[0:8, :] = jnp.zeros((8, channels), f32)
    wide[8 * rows + 8 : 8 * rows + 16, :] = jnp.zeros((8, channels), f32)
    y, zh = at_ref[0], at_ref[1]
    for step in range(4):
        for half in range(2):
            other = zh if half == 0 else 1 - zh
            segment = 2 * lax.rem(y + 4 - step, 4) + other
            tall = jnp.dot(
                spread, ups[step][half * bins : (half + 1) * bins, :], preferred_element_type=f32
            )
            tall = tall + skips[step][half * rows : (half + 1) * rows, :].astype(f32)
            start = pl.multiple_of(segment * rows + 8, 8)
            wide[pl.ds(start, rows), :] = tall.astype(bf16).astype(f32)


def expand(at, ups, skips):
    operands = (*ups, *skips)
    channels = skips[0].shape[1]
    out = jax.ShapeDtypeStruct((4 * skips[0].shape[0] + 16, channels), jnp.float32)
    return pl.pallas_call(
        expand_kernel,
        grid_spec=pltpu.PrefetchScalarGridSpec(
            num_scalar_prefetch=1,
            grid=(1,),
            in_specs=[whole(operand) for operand in operands],
            out_specs=whole(out),
        ),
        out_shape=out,
        cost_estimate=pl.CostEstimate(
            flops=2 * out.size * 64, transcendentals=0, bytes_accessed=10 << 20
        ),
        compiler_params=pltpu.CompilerParams(vmem_limit_bytes=24 << 20),
        name="expand",
    )(at, *operands)


def head_kernel(
    first, last, positions, at_ref, wide_ref, before_ref, after_ref, conv_ref, head_ref, bias_ref,
    scale_ref, keep_ref, target_ref, *refs,
):
    f32, bf16 = jnp.float32, jnp.bfloat16
    if first:
        near, total = refs[-1], None
        pred_ref, partial_ref, total_ref = refs[:3]
    else:
        near, old_ref = refs[-1], refs[1]
        pred_ref, partial_ref, total_ref = refs[2:5]
    part = pl.program_id(0)
    segment = at_ref[0] * PARTS + part
    rows, channels = partial_ref.shape
    taps = conv_ref.shape[0]
    rim = taps // 2
    near[...] = wide_ref[pl.ds(pl.multiple_of(segment * rows, rows), rows + 16), :]

    @pl.when(segment == 0)
    def _():
        near[8 - rim : 8, :] = before_ref[...].astype(f32)

    @pl.when(segment == 4 * PARTS - 1)
    def _():
        near[rows + 8 : rows + 8 + rim, :] = after_ref[...].astype(f32)

    conved = jnp.zeros((rows, channels), f32)
    for tap in range(taps):
        begin = 8 - rim + tap
        conved = conved + jnp.dot(
            near[begin : begin + rows, :].astype(bf16), conv_ref[tap], preferred_element_type=f32
        )
    cubic = math.sqrt(2.0 / math.pi) * (conved + 0.044715 * (conved * conved * conved))
    feature = (near[8 : 8 + rows, :] + 0.5 * conved * (1.0 + jnp.tanh(cubic))).astype(bf16)
    logits = jnp.dot(feature, head_ref[...], preferred_element_type=f32) + bias_ref[...]
    decay = jnp.exp(-jnp.abs(logits))
    smooth = jnp.maximum(logits, 0.0) + jnp.log1p(decay)
    sigmoid = jnp.where(logits >= 0.0, 1.0, decay) / (1.0 + decay)
    pred_ref[...] = smooth.astype(bf16)
    misfit = smooth - target_ref[...].astype(f32)
    slope = (keep_ref[...] * scale_ref[...] * misfit * sigmoid).astype(bf16)
    partial_ref[...] = lax.dot_general(
        slope, head_ref[...], (((1,), (1,)), ((), ())), preferred_element_type=f32
    ).astype(bf16)
    product = lax.dot_general(
        feature, slope, (((0,), (0,)), ((), ())), preferred_element_type=f32
    )
    scale = 1.0 / positions if last else 1.0

    @pl.when(part == 0)
    def _():
        total_ref[...] = product if first else product + old_ref[...]

    @pl.when(part > 0)
    def _():
        total_ref[...] = (total_ref[...] + product) * scale


def head_pass(at, carried, wide, before, after, conv_w, head_w, bias, scale, keep, targets, last, positions):
    f32, bf16 = jnp.float32, jnp.bfloat16
    count, tracks = targets.shape
    channels = head_w.shape[0]
    rows = count // (4 * PARTS)
    first = carried is None
    by_rows = pl.BlockSpec((rows, tracks), lambda i, at: (at[0] * PARTS + i, 0))
    operands = (wide, before, after, conv_w, head_w, bias, scale)
    totals = jax.ShapeDtypeStruct((channels, tracks), f32)
    extra = [] if first else [pl.BlockSpec(memory_space=pl.ANY), whole(totals)]
    at_input = 1 + len(operands) + 2
    return pl.pallas_call(
        functools.partial(head_kernel, first, last, positions),
        grid_spec=pltpu.PrefetchScalarGridSpec(
            num_scalar_prefetch=1,
            grid=(PARTS,),
            in_specs=[whole(operand) for operand in operands]
            + [pl.BlockSpec((rows, 1), lambda i, at: (at[0] * PARTS + i, 0)), by_rows]
            + extra,
            out_specs=[by_rows, pl.BlockSpec((rows, channels), lambda i, at: (i, 0)), whole(totals)],
            scratch_shapes=[pltpu.VMEM((rows + 16, channels), f32)],
        ),
        out_shape=[
            jax.ShapeDtypeStruct((count, tracks), bf16),
            jax.ShapeDtypeStruct((PARTS * rows, channels), bf16),
            totals,
        ],
        input_output_aliases={} if first else {at_input: 0, at_input + 1: 2},
        cost_estimate=pl.CostEstimate(
            flops=2 * PARTS * rows * (conv_w.size + 3 * head_w.size),
            transcendentals=4 * PARTS * rows * tracks,
            bytes_accessed=16 << 20,
        ),
        compiler_params=pltpu.CompilerParams(vmem_limit_bytes=36 << 20),
        name="head_pass",
    )(at, *operands, keep, targets, *(carried or ()))


def body(
    trunk,
    norm_gain,
    w_query,
    w_kv,
    w_out,
    w_up,
    skip,
    conv_w,
    head_w,
    head_bias,
    targets,
    missing,
    group_ids,
    group_weight,
):
    f32, bf16 = jnp.float32, jnp.bfloat16
    row_count = trunk.shape[0]
    head_dim = w_kv.shape[1] // 2
    head_count = w_query.shape[1] // head_dim
    widened = trunk.astype(f32)
    meansq = jnp.mean(widened * widened, axis=1, keepdims=True)
    normed = (widened * lax.rsqrt(meansq + 1e-06) * norm_gain).astype(bf16)
    keyvals = jnp.dot(normed, w_kv, preferred_element_type=f32).astype(bf16)
    skip_pair = jnp.concatenate([skip, moved(skip, 2, 2)], 0)
    for dim in (2, 1):
        keyvals = jnp.concatenate([keyvals] + [moved(keyvals, dim, step) for step in (1, 3, 2)], 0)
    skip_pair, keyvals = lax.optimization_barrier((skip_pair, keyvals))
    queries = jnp.dot(normed, w_query, preferred_element_type=f32).astype(bf16)
    crossed = moved(keyvals, 3, 1)
    pieces = [moved(keyvals, 0, step) for step in (1, 3, 2)]
    skips = [skip_pair] + [moved(skip_pair, 1, step) for step in (1, 2, 3)]
    state = attend(None, queries, [keyvals], head_dim)
    for piece in pieces:
        state = attend(state, queries, [crossed, piece], head_dim)
        crossed = moved(piece, 3, 1)
    state = attend(state, queries, [crossed], head_dim)
    upward = project(state, trunk, w_out, w_up)
    up_pair = jnp.concatenate([upward, moved(upward, 2, 2)], 0)
    ups = [up_pair] + [moved(up_pair, 1, step) for step in (1, 2, 3)]
    y, zh, core = lax.axis_index("y"), lax.axis_index("zh"), lax.axis_index("core")
    wide = expand(jnp.stack([y, zh]).astype(jnp.int32), ups, skips)
    factor = skip.shape[0] // row_count
    tap_count, channels = conv_w.shape[:2]
    rim = tap_count // 2
    pos_count = targets.shape[0]
    n_bin = lax.axis_size(BIN)
    up_pairs = [(i, i + 1) for i in range(n_bin - 1)]
    before = lax.ppermute(wide[pos_count + 8 - rim : pos_count + 8].astype(bf16), BIN, up_pairs)
    after = lax.ppermute(wide[8 : 8 + rim].astype(bf16), BIN, [(j, i) for i, j in up_pairs])
    tile_width = head_w.shape[1]
    groups = group_weight.shape[0]
    total_tracks = group_ids.shape[0]
    labels = jnp.arange(groups, dtype=jnp.int32)
    counts = jnp.sum((group_ids == labels[None, :]).astype(jnp.int32), axis=0)
    per_group = group_weight * total_tracks / (groups * counts.astype(f32))
    local_ids = lax.dynamic_slice_in_dim(group_ids, lax.axis_index(TRK) * tile_width, tile_width, 0)
    track_scale = jnp.sum(jnp.where(local_ids == labels[None, :], per_group[None, :], 0.0), axis=1)
    keep_mask = 1.0 - jnp.repeat(missing.astype(f32), factor)[:, None]
    carried, received = None, []
    for step in (2, 1, 3, 0):
        prediction, partial, total = head_pass(
            jnp.stack([lax.rem(y + step, 4), core]).astype(jnp.int32),
            carried,
            wide,
            before,
            after,
            conv_w,
            head_w,
            head_bias[None, :],
            track_scale[None, :],
            keep_mask,
            targets,
            step == 0,
            pos_count * n_bin,
        )
        carried = (prediction, total)
        received.append(moved(partial, 1, step) if step else partial)
    summed = sum(part.astype(f32) for part in received)
    halves = summed.reshape(2, summed.shape[0] // 2, channels)
    away = lax.dynamic_index_in_dim(halves, 1 - zh, 0, keepdims=False).astype(bf16)
    here = lax.dynamic_index_in_dim(halves, zh, 0, keepdims=False)
    feature_grad = (here + moved(away, 2, 2).astype(f32)).astype(bf16)
    blocks = total.reshape(lax.axis_size("bz"), 2, channels // n_bin, tile_width)
    mine = lax.dynamic_index_in_dim(blocks, core, 1, keepdims=False)
    theirs = lax.dynamic_index_in_dim(blocks, 1 - core, 1, keepdims=False).astype(bf16)
    pair_sum = (mine + lax.ppermute(theirs, "core", [(0, 1), (1, 0)]).astype(f32)).astype(bf16)
    gathered = lax.all_to_all(pair_sum, "bz", 0, 0, tiled=True)
    head_grad = jnp.sum(gathered.astype(f32), axis=0)
    return (prediction, head_grad, feature_grad)


def solution(mesh):
    inner = Mesh(np.asarray(mesh.devices).reshape(8, 2, 4, 2), ALL)
    in_specs = (
        P(ALL, None),
        P(),
        P(),
        P(),
        P(),
        P(),
        P(ALL, None),
        P(),
        P(None, TRK),
        P(TRK),
        P(BIN, TRK),
        P(BIN),
        P(),
        P(),
    )
    out_specs = (P(BIN, TRK), P(BIN, TRK), P(ALL, None))
    return jax.shard_map(body, mesh=inner, in_specs=in_specs, out_specs=out_specs, check_vma=False)
```

time: 216 us -> 236 us (1.093); the launches traced: 215 us -> 233 us
  Pallas kernels: 44.5 us -> 69.9 us
  local copies, waits for them, and re-layouts: 5.36 us -> 23.3 us
  blocking collectives: 17 us -> 0 us
  starting transfers between devices: 30.7 us -> 45.1 us
  between operations: 14.3 us -> 0.97 us
  waiting for transfers between devices: 92.1 us -> 79.3 us
  other arithmetic: 8.12 us -> 11.5 us
    all_to_all x2 -> x1, waiting for transfers between devices: 57.6 us -> 0.01 us  [body(): gathered = lax.all_to_all(pair_sum, 'bz', 0, 0, tiled=True)]
    ppermute x13 -> x25, waiting for transfers between devices: 32.1 us -> 79.3 us  [moved(): return lax.ppermute(value, ALL, pairs)]
    ppermute x13 -> x25, starting transfers between devices: 16.5 us -> 33.9 us  [moved(): return lax.ppermute(value, ALL, pairs)]
    all_to_all x1 -> x0, blocking collectives: 17 us -> none  [body(): gathered = lax.all_to_all(pair_sum, 'bz', 0, 0, tiled=True)]
    pallas_call x1 -> x5, Pallas kernels: 37.6 us -> 52.7 us  [the longest x4 50 us: head_pass(): pl.pallas_call(functools.partial(head_kernel, first, last, positions), gr...]
    unnamed x27 -> x45, local copies, waits for them, and re-layouts: 3.02 us -> 18 us
    pallas_call x5, Pallas kernels: 5.91 us -> 16.1 us  [attend(): pl.pallas_call(functools.partial(attend_kernel, head_dim, state is None),...]
    reduce_sum x1 -> x0, other arithmetic: 3.17 us -> none  [body(): feature_grad = jnp.sum(arrived.astype(f32), axis=0).astype(bf16)]
  transfers between devices with their start and end apart: 19 -> 29, of which waited for: 9 -> 15; matrix products, arithmetic and copies ran while one was open for 4% -> 7% of each run, Pallas kernels for 3% -> 7%
where the time goes in v2:
time: 236 us; the launch traced here: 233 us
  waiting for transfers between devices  79.3 us (34%)
  Pallas kernels  69.9 us (30%)
  starting transfers between devices  45.1 us (19%)
  local copies, waits for them, and re-layouts  23.3 us (10%)
  other arithmetic  11.5 us (5%)
  matrix products  2.89 us (1%)
    ppermute x25, waiting for transfers between devices, moved(): return lax.ppermute(value, ALL, pairs)  79.3 us
    pallas_call x4, Pallas kernels, head_pass(): pl.pallas_call(functools.partial(head_kernel, first, last, positions), gr...  50 us
    ppermute x25, starting transfers between devices, moved(): return lax.ppermute(value, ALL, pairs)  33.9 us
    unnamed x45, local copies, waits for them, and re-layouts  18 us
    pallas_call x5, Pallas kernels, attend(): pl.pallas_call(functools.partial(attend_kernel, head_dim, state is None),...  16.1 us
    all_to_all x1, starting transfers between devices, body(): gathered = lax.all_to_all(pair_sum, 'bz', 0, 0, tiled=True)  5.84 us
  transfers between devices with their start and end apart: 29, of which 15 were waited for; matrix products, arithmetic and copies ran while one was open for 7% of the time, Pallas kernels for 7%

profile of v2, /device:TPU:0, one launch (start us, length us, event | category | flops | bytes accessed | tf_op | source)
XLA Modules:
  0.0 232.9 jit_solution(13417715321622297307)
XLA Ops:
  31.2 9.5 %collective-permute-done.11.refs_2_ = bf16[1024,256]{1,0:T(8,128)(2,1)} collective-permute-done((bf16[1024,256]{1,0:T(8,128)(2,1)}, bf16[1024,256]{1,0:T(8,128)(2,1)}, u32[]{:S(2)}, u32[]{:S(2)}) %collective-permute-start.11) | collective-permute-done | bytes 524320 | tf_op jit(solution)/shard_map/ppermute | solution.py:39
  40.9 7.7 %collective-permute-done.9.refs_2_ = bf16[1024,256]{1,0:T(8,128)(2,1)} collective-permute-done((bf16[1024,256]{1,0:T(8,128)(2,1)}, bf16[1024,256]{1,0:T(8,128)(2,1)}, u32[]{:S(2)}, u32[]{:S(2)}) %collective-permute-start.9) | collective-permute-done | bytes 524320 | tf_op jit(solution)/shard_map/ppermute | solution.py:39
  52.8 2.6 %collective-permute-start.19 = (bf16[512,768]{1,0:T(8,128)(2,1)}, bf16[512,768]{1,0:T(8,128)(2,1)S(1)}, u32[]{:S(2)}, u32[]{:S(2)}) collective-permute-start(bf16[512,768]{1,0:T(8,128)(2,1)} %pad_maximum_fusion.refs_4_), channel_id=1, source_target_pairs={{0,4},{1,5},{2,6},{3,7},{4,0},{5,1},{6,2},{7,3},{8,12},{9,13},{10,... | collective-permute-start | bytes 2359304 | tf_op jit(solution)/shard_map/ppermute | solution.py:39
  56.6 3.8 %attend.6 = (f32[512,128]{1,0:T(8,128)S(1)}, f32[512,128]{1,0:T(8,128)S(1)}) custom-call(bf16[64,1024]{1,0:T(8,128)(2,1)S(1)} %convolution_convert_fusion.refs_0_, bf16[1024,256]{1,0:T(8,128)(2,1)} %collective-permute-done.13.refs_1_, bf16[1024,256]{1,0:T(8,128)(2,1)} %collective-permute-done.11.refs_2_, f32[512,128]{1,0:T(8,128)S(1)} %get-tuple-element.28.refs_3_, ...), custom_call_target="tpu_custom_call" | custom-call | flops 1073741824 | bytes 1048576 | tf_op jit(solution)/shard_map/attend/pallas_call | solution.py:85
  60.4 3.8 %attend.7 = (f32[512,128]{1,0:T(8,128)S(1)}, f32[512,128]{1,0:T(8,128)S(1)}) custom-call(bf16[64,1024]{1,0:T(8,128)(2,1)S(1)} %convolution_convert_fusion.refs_0_, bf16[1024,256]{1,0:T(8,128)(2,1)} %collective-permute-done.12.refs_1_, bf16[1024,256]{1,0:T(8,128)(2,1)} %collective-permute-done.9.refs_2_, f32[512,128]{1,0:T(8,128)S(1)} %get-tuple-element.30.refs_3_, ...), custom_call_target="tpu_custom_call" | custom-call | flops 1073741824 | bytes 1048576 | tf_op jit(solution)/shard_map/attend/pallas_call | solution.py:85
  64.2 3.9 %attend.8 = (f32[512,128]{1,0:T(8,128)S(1)}, f32[512,128]{1,0:T(8,128)S(1)}) custom-call(bf16[64,1024]{1,0:T(8,128)(2,1)S(1)} %convolution_convert_fusion.refs_0_, bf16[1024,256]{1,0:T(8,128)(2,1)} %collective-permute-done.10.refs_1_, bf16[1024,256]{1,0:T(8,128)(2,1)} %collective-permute-done.7.refs_2_, f32[512,128]{1,0:T(8,128)S(1)} %get-tuple-element.32.refs_3_, ...), custom_call_target="tpu_custom_call" | custom-call | flops 1073741824 | bytes 1048576 | tf_op jit(solution)/shard_map/attend/pallas_call | solution.py:85
  73.5 4.3 %collective-permute-done.14 = bf16[64,768]{1,0:T(8,128)(2,1)S(1)} collective-permute-done((bf16[64,768]{1,0:T(8,128)(2,1)S(1)}, bf16[64,768]{1,0:T(8,128)(2,1)S(1)}, u32[]{:S(2)}, u32[]{:S(2)}) %collective-permute-start.14) | collective-permute-done | bytes 98336 | tf_op jit(solution)/shard_map/ppermute | solution.py:39
  81.5 5.7 %collective-permute-done.19.refs_6_ = bf16[512,768]{1,0:T(8,128)(2,1)S(1)} collective-permute-done((bf16[512,768]{1,0:T(8,128)(2,1)}, bf16[512,768]{1,0:T(8,128)(2,1)S(1)}, u32[]{:S(2)}, u32[]{:S(2)}) %collective-permute-start.19) | collective-permute-done | bytes 786464 | tf_op jit(solution)/shard_map/ppermute | solution.py:39
  87.2 3.8 %collective-permute-done.20.refs_7_ = bf16[512,768]{1,0:T(8,128)(2,1)S(1)} collective-permute-done((bf16[512,768]{1,0:T(8,128)(2,1)}, bf16[512,768]{1,0:T(8,128)(2,1)S(1)}, u32[]{:S(2)}, u32[]{:S(2)}) %collective-permute-start.20) | collective-permute-done | bytes 786464 | tf_op jit(solution)/shard_map/ppermute | solution.py:39
  91.5 3.8 %collective-permute-done.16.refs_2_ = bf16[128,768]{1,0:T(8,128)(2,1)S(1)} collective-permute-done((bf16[128,768]{1,0:T(8,128)(2,1)S(1)}, bf16[128,768]{1,0:T(8,128)(2,1)S(1)}, u32[]{:S(2)}, u32[]{:S(2)}) %collective-permute-start.16) | collective-permute-done | bytes 196640 | tf_op jit(solution)/shard_map/ppermute | solution.py:39
  95.3 3.6 %collective-permute-done.17.refs_3_ = bf16[128,768]{1,0:T(8,128)(2,1)S(1)} collective-permute-done((bf16[128,768]{1,0:T(8,128)(2,1)S(1)}, bf16[128,768]{1,0:T(8,128)(2,1)S(1)}, u32[]{:S(2)}, u32[]{:S(2)}) %collective-permute-start.17) | collective-permute-done | bytes 196640 | tf_op jit(solution)/shard_map/ppermute | solution.py:39
  98.9 2.7 %expand.1.wide_ref = f32[2064,768]{1,0:T(8,128)S(1)} custom-call(s32[2]{0:T(128)S(1)} %pad_add_fusion.1.at_ref, bf16[128,768]{1,0:T(8,128)(2,1)S(1)} %pad_maximum_fusion.1.refs_0_, bf16[128,768]{1,0:T(8,128)(2,1)S(1)} %collective-permute-done.15.refs_1_, bf16[128,768]{1,0:T(8,128)(2,1)S(1)} %collective-permute-done.16.refs_2_, ...), custom_call_target="tpu_custom_call" | custom-call | flops 202899456 | bytes 10485760 | tf_op jit(solution)/shard_map/expand/pallas_call | solution.py:162
  110.5 2.7 %copy-done.2 = bf16[5,768,768]{2,1,0:T(8,128)(2,1)S(1)} copy-done((bf16[5,768,768]{2,1,0:T(8,128)(2,1)S(1)}, bf16[5,768,768]{2,1,0:T(8,128)(2,1)}, u32[]{:S(2)}) %copy-start.2) | copy-done | bytes 5898264
  117.5 12.3 %head_pass.4 = (bf16[2048,768]{1,0:T(8,128)(2,1)}, bf16[512,768]{1,0:T(8,128)(2,1)}, f32[768,768]{1,0:T(8,128)S(1)}) custom-call(s32[2]{0:T(128)S(1)} %get-tuple-element.58.at_ref, f32[2064,768]{1,0:T(8,128)} %copy-done.1, bf16[2,768]{1,0:T(2,128)(2,1)S(1)} %collective-permute-done.21.before_ref, bf16[2,768]{1,0:T(2,128)(2,1)S(1)} %collective-permute-done.22.after_ref, ...), custom_call_target="tpu_custom_call" | custom-call | flops 4831838208 | bytes 16777216 | tf_op jit(solution)/shard_map/head_pass/pallas_call | solution.py:248
  129.8 2.7 %copy-done.3 = bf16[5,768,768]{2,1,0:T(8,128)(2,1)S(1)} copy-done((bf16[5,768,768]{2,1,0:T(8,128)(2,1)S(1)}, bf16[5,768,768]{2,1,0:T(8,128)(2,1)}, u32[]{:S(2)}) %copy-start.3) | copy-done | bytes 5898264
  132.5 12.5 %head_pass.5 = (bf16[2048,768]{1,0:T(8,128)(2,1)}, bf16[512,768]{1,0:T(8,128)(2,1)}, f32[768,768]{1,0:T(8,128)S(1)}) custom-call(s32[2]{0:T(128)S(1)} %get-tuple-element.57.at_ref, f32[2064,768]{1,0:T(8,128)} %copy-done.1, bf16[2,768]{1,0:T(2,128)(2,1)S(1)} %collective-permute-done.21.before_ref, ...), custom_call_target="tpu_custom_call", output_to_operand_aliasing={{0}: (10, {}), {2}: (11, {})} | custom-call | flops 4831838208 | bytes 16777216 | tf_op jit(solution)/shard_map/head_pass/pallas_call | solution.py:248
  145.0 12.5 %head_pass.6 = (bf16[2048,768]{1,0:T(8,128)(2,1)}, bf16[512,768]{1,0:T(8,128)(2,1)}, f32[768,768]{1,0:T(8,128)S(1)}) custom-call(s32[2]{0:T(128)S(1)} %get-tuple-element.56.at_ref, f32[2064,768]{1,0:T(8,128)} %copy-done.1, bf16[2,768]{1,0:T(2,128)(2,1)S(1)} %collective-permute-done.21.before_ref, ...), custom_call_target="tpu_custom_call", output_to_operand_aliasing={{0}: (10, {}), {2}: (11, {})} | custom-call | flops 4831838208 | bytes 16777216 | tf_op jit(solution)/shard_map/head_pass/pallas_call | solution.py:248
  157.6 12.6 %head_pass.7 = (bf16[2048,768]{1,0:T(8,128)(2,1)}, bf16[512,768]{1,0:T(8,128)(2,1)S(1)}, f32[768,768]{1,0:T(8,128)S(1)}) custom-call(s32[2]{0:T(128)S(1)} %get-tuple-element.55.at_ref, f32[2064,768]{1,0:T(8,128)} %copy-done.1, bf16[2,768]{1,0:T(2,128)(2,1)S(1)} %collective-permute-done.21.before_ref, ...), custom_call_target="tpu_custom_call", output_to_operand_aliasing={{0}: (10, {}), {2}: (11, {})} | custom-call | flops 4831838208 | bytes 16777216 | tf_op jit(solution)/shard_map/head_pass/pallas_call | solution.py:248
  174.8 2.6 %collective-permute-start.26 = (bf16[512,768]{1,0:T(8,128)(2,1)}, bf16[512,768]{1,0:T(8,128)(2,1)}, u32[]{:S(2)}, u32[]{:S(2)}) collective-permute-start(bf16[512,768]{1,0:T(8,128)(2,1)} %get-tuple-element.49), channel_id=1, source_target_pairs={{0,6},{1,7},{2,0},{3,1},{4,2},{5,3},{6,4},{7,5},{8,14},{9,15},{10,... | collective-permute-start | bytes 2359304 | tf_op jit(solution)/shard_map/ppermute | solution.py:39
  178.9 2.4 %fusion = bf16[8,48,768]{2,1,0:T(8,128)(2,1)} fusion(bf16[8,48,768]{2,1,0:T(8,128)(2,1)} %collective-permute-done.23, f32[8,2,48,768]{3,2,1,0:T(8,128)} %bitcast.25, s32[]{:T(128)S(6)} %select_n.23), kind=kLoop, calls=%fused_computation.2 | loop fusion | flops 884736 | bytes 2359300 | tf_op jit(solution)/shard_map/convert_element_type | solution.py:361
  181.3 5.8 %all-to-all-start = ((bf16[8,48,768]{2,1,0:T(8,128)(2,1)}), bf16[8,48,768]{2,1,0:T(8,128)(2,1)}, u32[]{:S(2)}, u32[]{:S(2)}) async-start(bf16[8,48,768]{2,1,0:T(8,128)(2,1)} %fusion), calls=%async_computation | async-start | bytes 1179648 | tf_op jit(solution)/shard_map/all_to_all | solution.py:362
  187.2 24.5 %collective-permute-done.26 = bf16[512,768]{1,0:T(8,128)(2,1)} collective-permute-done((bf16[512,768]{1,0:T(8,128)(2,1)}, bf16[512,768]{1,0:T(8,128)(2,1)}, u32[]{:S(2)}, u32[]{:S(2)}) %collective-permute-start.26) | collective-permute-done | bytes 786464 | tf_op jit(solution)/shard_map/ppermute | solution.py:39
  211.6 3.4 %collective-permute-done.25 = bf16[512,768]{1,0:T(8,128)(2,1)} collective-permute-done((bf16[512,768]{1,0:T(8,128)(2,1)}, bf16[512,768]{1,0:T(8,128)(2,1)}, u32[]{:S(2)}, u32[]{:S(2)}) %collective-permute-start.25) | collective-permute-done | bytes 786464 | tf_op jit(solution)/shard_map/ppermute | solution.py:39
  223.0 7.8 %collective-permute-done.27 = bf16[256,768]{1,0:T(8,128)(2,1)} collective-permute-done((bf16[256,768]{1,0:T(8,128)(2,1)}, bf16[256,768]{1,0:T(8,128)(2,1)}, u32[]{:S(2)}, u32[]{:S(2)}) %collective-permute-start.27) | collective-permute-done | bytes 393248 | tf_op jit(solution)/shard_map/ppermute | solution.py:39
  (118 shorter events, 75.0 us)
Async XLA Ops:
  4.1 7.7 %collective-permute-start.1 = (bf16[64,256]{1,0:T(8,128)(2,1)S(1)}, bf16[64,256]{1,0:T(8,128)(2,1)S(1)}, u32[]{:S(2)}, u32[]{:S(2)}) collective-permute-start(bf16[64,256]{1,0:T(8,128)(2,1)S(1)} %get-tuple-element.54), channel_id=1, source_target_pairs={{0,64},{1,65},{2,66},{3,67},{4,68},{5,69},{6,70},{7,71},{8,72},{9,... | collective-permute-start | bytes 98312 | tf_op jit(solution)/shard_map/ppermute | solution.py:39
  10.1 14.3 %collective-permute-start = (bf16[256,768]{1,0:T(8,128)(2,1)}, bf16[256,768]{1,0:T(8,128)(2,1)S(1)}, u32[]{:S(2)}, u32[]{:S(2)}) collective-permute-start(bf16[256,768]{1,0:T(8,128)(2,1)} %param.20), channel_id=1, source_target_pairs={{0,1},{1,0},{2,3},{3,2},{4,5},{5,4},{6,7},{7,6},{8,9},{9,8},{10,11... | collective-permute-start | bytes 1179656 | tf_op jit(solution)/shard_map/ppermute | solution.py:39
  13.9 7.7 %collective-permute-start.4 = (bf16[256,256]{1,0:T(8,128)(2,1)S(1)}, bf16[256,256]{1,0:T(8,128)(2,1)S(1)}, u32[]{:S(2)}, u32[]{:S(2)}) collective-permute-start(bf16[256,256]{1,0:T(8,128)(2,1)S(1)} %pad_maximum_fusion.2), channel_id=1, source_target_pairs={{0,2},{1,3},{2,4},{3,5},{4,6},{5,7},{6,0},{7,1},{8,10},{9,11},{10,... | collective-permute-start | bytes 393224 | tf_op jit(solution)/shard_map/ppermute | solution.py:39
  15.6 6.7 %collective-permute-start.5 = (bf16[256,256]{1,0:T(8,128)(2,1)S(1)}, bf16[256,256]{1,0:T(8,128)(2,1)S(1)}, u32[]{:S(2)}, u32[]{:S(2)}) collective-permute-start(bf16[256,256]{1,0:T(8,128)(2,1)S(1)} %pad_maximum_fusion.2), channel_id=1, source_target_pairs={{0,6},{1,7},{2,0},{3,1},{4,2},{5,3},{6,4},{7,5},{8,14},{9,15},{10,... | collective-permute-start | bytes 393224 | tf_op jit(solution)/shard_map/ppermute | solution.py:39
  17.2 6.5 %collective-permute-start.6 = (bf16[256,256]{1,0:T(8,128)(2,1)S(1)}, bf16[256,256]{1,0:T(8,128)(2,1)S(1)}, u32[]{:S(2)}, u32[]{:S(2)}) collective-permute-start(bf16[256,256]{1,0:T(8,128)(2,1)S(1)} %pad_maximum_fusion.2), channel_id=1, source_target_pairs={{0,4},{1,5},{2,6},{3,7},{4,0},{5,1},{6,2},{7,3},{8,12},{9,13},{10,... | collective-permute-start | bytes 393224 | tf_op jit(solution)/shard_map/ppermute | solution.py:39
  25.3 15.4 %collective-permute-start.11 = (bf16[1024,256]{1,0:T(8,128)(2,1)}, bf16[1024,256]{1,0:T(8,128)(2,1)}, u32[]{:S(2)}, u32[]{:S(2)}) collective-permute-start(bf16[1024,256]{1,0:T(8,128)(2,1)} %constant_dynamic-update-slice_fusion.refs_1_), channel_id=1, source_target_pairs={{0,16},{1,17},{2,18},{3,19},{4,20},{5,21},{6,22},{7,23},{8,24},{9,... | collective-permute-start | bytes 1572872 | tf_op jit(solution)/shard_map/ppermute | solution.py:39
  26.8 21.8 %collective-permute-start.9 = (bf16[1024,256]{1,0:T(8,128)(2,1)}, bf16[1024,256]{1,0:T(8,128)(2,1)}, u32[]{:S(2)}, u32[]{:S(2)}) collective-permute-start(bf16[1024,256]{1,0:T(8,128)(2,1)} %constant_dynamic-update-slice_fusion.refs_1_), channel_id=1, source_target_pairs={{0,48},{1,49},{2,50},{3,51},{4,52},{5,53},{6,54},{7,55},{8,56},{9,... | collective-permute-start | bytes 1572872 | tf_op jit(solution)/shard_map/ppermute | solution.py:39
  28.5 21.7 %collective-permute-start.7 = (bf16[1024,256]{1,0:T(8,128)(2,1)}, bf16[1024,256]{1,0:T(8,128)(2,1)}, u32[]{:S(2)}, u32[]{:S(2)}) collective-permute-start(bf16[1024,256]{1,0:T(8,128)(2,1)} %constant_dynamic-update-slice_fusion.refs_1_), channel_id=1, source_target_pairs={{0,32},{1,33},{2,34},{3,35},{4,36},{5,37},{6,38},{7,39},{8,40},{9,... | collective-permute-start | bytes 1572872 | tf_op jit(solution)/shard_map/ppermute | solution.py:39
  31.1 21.7 %collective-permute-start.13 = (bf16[1024,256]{1,0:T(8,128)(2,1)}, bf16[1024,256]{1,0:T(8,128)(2,1)}, u32[]{:S(2)}, u32[]{:S(2)}) collective-permute-start(bf16[1024,256]{1,0:T(8,128)(2,1)} %constant_dynamic-update-slice_fusion.refs_1_), channel_id=1, source_target_pairs={{0,8},{1,9},{2,10},{3,11},{4,12},{5,13},{6,14},{7,15},{8,0},{9,1},... | collective-permute-start | bytes 1572872 | tf_op jit(solution)/shard_map/ppermute | solution.py:39
  40.7 14.7 %collective-permute-start.12 = (bf16[1024,256]{1,0:T(8,128)(2,1)}, bf16[1024,256]{1,0:T(8,128)(2,1)}, u32[]{:S(2)}, u32[]{:S(2)}) collective-permute-start(bf16[1024,256]{1,0:T(8,128)(2,1)} %collective-permute-done.11.refs_2_), channel_id=1, source_target_pairs={{0,8},{1,9},{2,10},{3,11},{4,12},{5,13},{6,14},{7,15},{8,0},{9,1},... | collective-permute-start | bytes 1572872 | tf_op jit(solution)/shard_map/ppermute | solution.py:39
  48.5 15.6 %collective-permute-start.10 = (bf16[1024,256]{1,0:T(8,128)(2,1)}, bf16[1024,256]{1,0:T(8,128)(2,1)}, u32[]{:S(2)}, u32[]{:S(2)}) collective-permute-start(bf16[1024,256]{1,0:T(8,128)(2,1)} %collective-permute-done.9.refs_2_), channel_id=1, source_target_pairs={{0,8},{1,9},{2,10},{3,11},{4,12},{5,13},{6,14},{7,15},{8,0},{9,1},... | collective-permute-start | bytes 1572872 | tf_op jit(solution)/shard_map/ppermute | solution.py:39
  48.6 31.1 %collective-permute-start.18 = (bf16[512,768]{1,0:T(8,128)(2,1)}, bf16[512,768]{1,0:T(8,128)(2,1)}, u32[]{:S(2)}, u32[]{:S(2)}) collective-permute-start(bf16[512,768]{1,0:T(8,128)(2,1)} %pad_maximum_fusion.refs_4_), channel_id=1, source_target_pairs={{0,2},{1,3},{2,4},{3,5},{4,6},{5,7},{6,0},{7,1},{8,10},{9,11},{10,... | collective-permute-start | bytes 2359304 | tf_op jit(solution)/shard_map/ppermute | solution.py:39
  50.2 17.9 %collective-permute-start.8 = (bf16[1024,256]{1,0:T(8,128)(2,1)}, bf16[1024,256]{1,0:T(8,128)(2,1)}, u32[]{:S(2)}, u32[]{:S(2)}) collective-permute-start(bf16[1024,256]{1,0:T(8,128)(2,1)} %collective-permute-done.7.refs_2_), channel_id=1, source_target_pairs={{0,8},{1,9},{2,10},{3,11},{4,12},{5,13},{6,14},{7,15},{8,0},{9,1},... | collective-permute-start | bytes 1572872 | tf_op jit(solution)/shard_map/ppermute | solution.py:39
  52.8 34.4 %collective-permute-start.19 = (bf16[512,768]{1,0:T(8,128)(2,1)}, bf16[512,768]{1,0:T(8,128)(2,1)S(1)}, u32[]{:S(2)}, u32[]{:S(2)}) collective-permute-start(bf16[512,768]{1,0:T(8,128)(2,1)} %pad_maximum_fusion.refs_4_), channel_id=1, source_target_pairs={{0,4},{1,5},{2,6},{3,7},{4,0},{5,1},{6,2},{7,3},{8,12},{9,13},{10,... | collective-permute-start | bytes 2359304 | tf_op jit(solution)/shard_map/ppermute | solution.py:39
  55.4 35.6 %collective-permute-start.20 = (bf16[512,768]{1,0:T(8,128)(2,1)}, bf16[512,768]{1,0:T(8,128)(2,1)S(1)}, u32[]{:S(2)}, u32[]{:S(2)}) collective-permute-start(bf16[512,768]{1,0:T(8,128)(2,1)} %pad_maximum_fusion.refs_4_), channel_id=1, source_target_pairs={{0,6},{1,7},{2,0},{3,1},{4,2},{5,3},{6,4},{7,5},{8,14},{9,15},{10,... | collective-permute-start | bytes 2359304 | tf_op jit(solution)/shard_map/ppermute | solution.py:39
  77.8 13.7 %collective-permute-start.15 = (bf16[128,768]{1,0:T(8,128)(2,1)S(1)}, bf16[128,768]{1,0:T(8,128)(2,1)S(1)}, u32[]{:S(2)}, u32[]{:S(2)}) collective-permute-start(bf16[128,768]{1,0:T(8,128)(2,1)S(1)} %pad_maximum_fusion.1.refs_0_), channel_id=1, source_target_pairs={{0,2},{1,3},{2,4},{3,5},{4,6},{5,7},{6,0},{7,1},{8,10},{9,11},{10,... | collective-permute-start | bytes 589832 | tf_op jit(solution)/shard_map/ppermute | solution.py:39
  78.6 16.6 %collective-permute-start.16 = (bf16[128,768]{1,0:T(8,128)(2,1)S(1)}, bf16[128,768]{1,0:T(8,128)(2,1)S(1)}, u32[]{:S(2)}, u32[]{:S(2)}) collective-permute-start(bf16[128,768]{1,0:T(8,128)(2,1)S(1)} %pad_maximum_fusion.1.refs_0_), channel_id=1, source_target_pairs={{0,4},{1,5},{2,6},{3,7},{4,0},{5,1},{6,2},{7,3},{8,12},{9,13},{10,... | collective-permute-start | bytes 589832 | tf_op jit(solution)/shard_map/ppermute | solution.py:39
  79.7 19.2 %collective-permute-start.17 = (bf16[128,768]{1,0:T(8,128)(2,1)S(1)}, bf16[128,768]{1,0:T(8,128)(2,1)S(1)}, u32[]{:S(2)}, u32[]{:S(2)}) collective-permute-start(bf16[128,768]{1,0:T(8,128)(2,1)S(1)} %pad_maximum_fusion.1.refs_0_), channel_id=1, source_target_pairs={{0,6},{1,7},{2,0},{3,1},{4,2},{5,3},{6,4},{7,5},{8,14},{9,15},{10,... | collective-permute-start | bytes 589832 | tf_op jit(solution)/shard_map/ppermute | solution.py:39
  172.5 6.4 %collective-permute-start.23 = (bf16[8,48,768]{2,1,0:T(8,128)(2,1)}, bf16[8,48,768]{2,1,0:T(8,128)(2,1)}, u32[]{:S(2)}, u32[]{:S(2)}) collective-permute-start(bf16[8,48,768]{2,1,0:T(8,128)(2,1)} %fusion.2), channel_id=1, source_target_pairs={{0,8},{8,0},{1,9},{9,1},{2,10},{10,2},{3,11},{11,3},{4,12},{12,4},... | collective-permute-start | bytes 1769480 | tf_op jit(solution)/shard_map/ppermute | solution.py:361
  174.8 36.8 %collective-permute-start.26 = (bf16[512,768]{1,0:T(8,128)(2,1)}, bf16[512,768]{1,0:T(8,128)(2,1)}, u32[]{:S(2)}, u32[]{:S(2)}) collective-permute-start(bf16[512,768]{1,0:T(8,128)(2,1)} %get-tuple-element.49), channel_id=1, source_target_pairs={{0,6},{1,7},{2,0},{3,1},{4,2},{5,3},{6,4},{7,5},{8,14},{9,15},{10,... | collective-permute-start | bytes 2359304 | tf_op jit(solution)/shard_map/ppermute | solution.py:39
  177.4 37.5 %collective-permute-start.25 = (bf16[512,768]{1,0:T(8,128)(2,1)}, bf16[512,768]{1,0:T(8,128)(2,1)}, u32[]{:S(2)}, u32[]{:S(2)}) collective-permute-start(bf16[512,768]{1,0:T(8,128)(2,1)} %get-tuple-element.48), channel_id=1, source_target_pairs={{0,2},{1,3},{2,4},{3,5},{4,6},{5,7},{6,0},{7,1},{8,10},{9,11},{10,... | collective-permute-start | bytes 2359304 | tf_op jit(solution)/shard_map/ppermute | solution.py:39
  177.4 37.5 %collective-permute-start.24 = (bf16[512,768]{1,0:T(8,128)(2,1)}, bf16[512,768]{1,0:T(8,128)(2,1)}, u32[]{:S(2)}, u32[]{:S(2)}) collective-permute-start(bf16[512,768]{1,0:T(8,128)(2,1)} %get-tuple-element.47), channel_id=1, source_target_pairs={{0,4},{1,5},{2,6},{3,7},{4,0},{5,1},{6,2},{7,3},{8,12},{9,13},{10,... | collective-permute-start | bytes 2359304 | tf_op jit(solution)/shard_map/ppermute | solution.py:39
  181.3 39.9 %all-to-all-start = ((bf16[8,48,768]{2,1,0:T(8,128)(2,1)}), bf16[8,48,768]{2,1,0:T(8,128)(2,1)}, u32[]{:S(2)}, u32[]{:S(2)}) async-start(bf16[8,48,768]{2,1,0:T(8,128)(2,1)} %fusion), calls=%async_computation | async-start | bytes 1179648 | tf_op jit(solution)/shard_map/all_to_all | solution.py:362
  219.2 11.7 %collective-permute-start.27 = (bf16[256,768]{1,0:T(8,128)(2,1)}, bf16[256,768]{1,0:T(8,128)(2,1)}, u32[]{:S(2)}, u32[]{:S(2)}) collective-permute-start(bf16[256,768]{1,0:T(8,128)(2,1)} %fusion.6), channel_id=1, source_target_pairs={{0,1},{1,0},{2,3},{3,2},{4,5},{5,4},{6,7},{7,6},{8,9},{9,8},{10,11... | collective-permute-start | bytes 1179656 | tf_op jit(solution)/shard_map/ppermute | solution.py:39
  (25 other events, 259.8 us)

commit v3 on v2

--- a/solution.py
+++ b/solution.py
@@ -11,6 +11,7 @@
 
 logit_cap = 20.0
 PARTS = 2
+HEADV = 20
 BIN = ("bz", "core")
 TRK = ("y", "zh")
 ALL = BIN + TRK
@@ -43,6 +44,27 @@
     return pl.BlockSpec(array.shape, lambda *_: (0,) * array.ndim, pipeline_mode=pl.Buffered(1))
 
 
+def join_kernel(*refs):
+    out = refs[-1]
+    rows = refs[0].shape[0]
+    for index, ref in enumerate(refs[:-1]):
+        out[index * rows : (index + 1) * rows, :] = ref[...]
+
+
+def join(*pieces):
+    rows, columns = pieces[0].shape
+    out = jax.ShapeDtypeStruct((len(pieces) * rows, columns), pieces[0].dtype)
+    return pl.pallas_call(
+        join_kernel,
+        in_specs=[pl.BlockSpec(memory_space=pltpu.VMEM)] * len(pieces),
+        out_specs=pl.BlockSpec(memory_space=pltpu.VMEM),
+        out_shape=out,
+        cost_estimate=pl.CostEstimate(flops=0, transcendentals=0, bytes_accessed=4 * out.size),
+        compiler_params=pltpu.CompilerParams(vmem_limit_bytes=4 << 20),
+        name="join",
+    )(*pieces)
+
+
 def attend_kernel(head_dim, first, *refs):
     q_ref, refs = refs[0], refs[1:]
     num_ref, den_ref = refs[-2:]
@@ -56,24 +78,18 @@
     outer = logit_cap * math.log2(math.e)
     num = jnp.zeros(num_ref.shape, f32) if first else refs[-4][...]
     den = jnp.zeros(den_ref.shape, f32) if first else refs[-3][...]
-    step = 512
+    step = 256
     for piece in pieces:
-
-        def block(index, pair, piece=piece):
-            num, den = pair
-            rows = pl.ds(pl.multiple_of(index * step, step), step)
+        for start in range(0, piece.shape[0], step):
+            keys = piece[start : start + step, :head_dim]
+            values = piece[start : start + step, head_dim:]
             scores = lax.dot_general(
-                queries, piece[rows, :head_dim], (((1,), (1,)), ((), ())), preferred_element_type=f32
+                queries, keys, (((1,), (1,)), ((), ())), preferred_element_type=f32
             )
             weights = jnp.exp2(outer * jnp.tanh(scores * inner))
-            num = num + jnp.dot(
-                weights.astype(bf16), piece[rows, head_dim:], preferred_element_type=f32
-            )
+            num = num + jnp.dot(weights.astype(bf16), values, preferred_element_type=f32)
             for lane in range(0, step, 128):
                 den = den + weights[:, lane : lane + 128]
-            return num, den
-
-        num, den = lax.fori_loop(0, piece.shape[0] // step, block, (num, den))
     num_ref[...] = num
     den_ref[...] = den
 
@@ -133,9 +149,9 @@
 
 def expand_kernel(at_ref, *refs):
     f32, bf16 = jnp.float32, jnp.bfloat16
-    ups, skips, wide = refs[:4], refs[4:8], refs[8]
+    ups, skips, (wide, first, last) = refs[:4], refs[4:6], refs[6:]
     bins, channels = ups[0].shape[0] // 2, ups[0].shape[1]
-    rows = skips[0].shape[0] // 2
+    rows = skips[0].shape[0] // 4
     factor = rows // bins
     row = lax.broadcasted_iota(jnp.int32, (rows, bins), 0)
     col = lax.broadcasted_iota(jnp.int32, (rows, bins), 1) * factor
@@ -150,28 +166,31 @@
             tall = jnp.dot(
                 spread, ups[step][half * bins : (half + 1) * bins, :], preferred_element_type=f32
             )
-            tall = tall + skips[step][half * rows : (half + 1) * rows, :].astype(f32)
+            tall = tall + skips[half][step * rows : (step + 1) * rows, :].astype(f32)
             start = pl.multiple_of(segment * rows + 8, 8)
             wide[pl.ds(start, rows), :] = tall.astype(bf16).astype(f32)
+    first[...] = wide[8:16, :].astype(bf16)
+    last[...] = wide[8 * rows : 8 * rows + 8, :].astype(bf16)
 
 
 def expand(at, ups, skips):
     operands = (*ups, *skips)
     channels = skips[0].shape[1]
-    out = jax.ShapeDtypeStruct((4 * skips[0].shape[0] + 16, channels), jnp.float32)
+    out = jax.ShapeDtypeStruct((2 * skips[0].shape[0] + 16, channels), jnp.float32)
+    edge = jax.ShapeDtypeStruct((8, channels), jnp.bfloat16)
     return pl.pallas_call(
         expand_kernel,
         grid_spec=pltpu.PrefetchScalarGridSpec(
             num_scalar_prefetch=1,
             grid=(1,),
-            in_specs=[whole(operand) for operand in operands],
-            out_specs=whole(out),
-        ),
-        out_shape=out,
+            in_specs=[pl.BlockSpec(memory_space=pltpu.VMEM)] * len(operands),
+            out_specs=[pl.BlockSpec(memory_space=pltpu.VMEM)] * 3,
+        ),
+        out_shape=[out, edge, edge],
         cost_estimate=pl.CostEstimate(
             flops=2 * out.size * 64, transcendentals=0, bytes_accessed=10 << 20
         ),
-        compiler_params=pltpu.CompilerParams(vmem_limit_bytes=24 << 20),
+        compiler_params=pltpu.CompilerParams(vmem_limit_bytes=8 << 20),
         name="expand",
     )(at, *operands)
 
@@ -181,12 +200,13 @@
     scale_ref, keep_ref, target_ref, *refs,
 ):
     f32, bf16 = jnp.float32, jnp.bfloat16
+    near = refs[-1]
     if first:
-        near, total = refs[-1], None
         pred_ref, partial_ref, total_ref = refs[:3]
+    elif last:
+        old_ref, pred_ref, partial_ref, mine_ref, theirs_ref, total_ref = refs[1:7]
     else:
-        near, old_ref = refs[-1], refs[1]
-        pred_ref, partial_ref, total_ref = refs[2:5]
+        old_ref, pred_ref, partial_ref, total_ref = refs[1:5]
     part = pl.program_id(0)
     segment = at_ref[0] * PARTS + part
     rows, channels = partial_ref.shape
@@ -196,12 +216,23 @@
 
     @pl.when(segment == 0)
     def _():
-        near[8 - rim : 8, :] = before_ref[...].astype(f32)
+        near[0:8, :] = before_ref[...].astype(f32)
 
     @pl.when(segment == 4 * PARTS - 1)
     def _():
-        near[rows + 8 : rows + 8 + rim, :] = after_ref[...].astype(f32)
-
+        near[rows + 8 : rows + 16, :] = after_ref[...].astype(f32)
+
+    bins = keep_ref.shape[2]
+    factor = PARTS * rows // bins
+    row = lax.broadcasted_iota(jnp.int32, (rows, bins), 0) + part * rows
+    col = lax.broadcasted_iota(jnp.int32, (rows, bins), 1) * factor
+    spread = jnp.where((row >= col) & (row < col + factor), 1.0, 0.0).astype(bf16)
+    keep = lax.dot_general(
+        spread,
+        jnp.broadcast_to(keep_ref[0].astype(bf16), (8, bins)),
+        (((1,), (1,)), ((), ())),
+        preferred_element_type=f32,
+    )[:, :1]
     conved = jnp.zeros((rows, channels), f32)
     for tap in range(taps):
         begin = 8 - rim + tap
@@ -216,14 +247,13 @@
     sigmoid = jnp.where(logits >= 0.0, 1.0, decay) / (1.0 + decay)
     pred_ref[...] = smooth.astype(bf16)
     misfit = smooth - target_ref[...].astype(f32)
-    slope = (keep_ref[...] * scale_ref[...] * misfit * sigmoid).astype(bf16)
+    slope = (keep * scale_ref[...] * misfit * sigmoid).astype(bf16)
     partial_ref[...] = lax.dot_general(
         slope, head_ref[...], (((1,), (1,)), ((), ())), preferred_element_type=f32
     ).astype(bf16)
     product = lax.dot_general(
         feature, slope, (((0,), (0,)), ((), ())), preferred_element_type=f32
     )
-    scale = 1.0 / positions if last else 1.0
 
     @pl.when(part == 0)
     def _():
@@ -231,7 +261,17 @@
 
     @pl.when(part > 0)
     def _():
-        total_ref[...] = (total_ref[...] + product) * scale
+        if not last:
+            total_ref[...] += product
+            return
+        total_ref[...] = (total_ref[...] + product) / positions
+        core, height = at_ref[1], channels // 16
+        for pair in range(8):
+            at = pl.multiple_of((2 * pair + core) * height, height)
+            other = pl.multiple_of((2 * pair + 1 - core) * height, height)
+            into = slice(pair * height, (pair + 1) * height)
+            mine_ref[into, :] = total_ref[pl.ds(at, height), :]
+            theirs_ref[into, :] = total_ref[pl.ds(other, height), :].astype(bf16)
 
 
 def head_pass(at, carried, wide, before, after, conv_w, head_w, bias, scale, keep, targets, last, positions):
@@ -243,31 +283,35 @@
     by_rows = pl.BlockSpec((rows, tracks), lambda i, at: (at[0] * PARTS + i, 0))
     operands = (wide, before, after, conv_w, head_w, bias, scale)
     totals = jax.ShapeDtypeStruct((channels, tracks), f32)
-    extra = [] if first else [pl.BlockSpec(memory_space=pl.ANY), whole(totals)]
+    extra = [] if first else [pl.BlockSpec(memory_space=pl.ANY), pl.BlockSpec(memory_space=pltpu.VMEM)]
     at_input = 1 + len(operands) + 2
+    half = (channels // 2, tracks)
+    sums = [jax.ShapeDtypeStruct(half, f32), jax.ShapeDtypeStruct(half, bf16)] if last else [totals]
     return pl.pallas_call(
         functools.partial(head_kernel, first, last, positions),
         grid_spec=pltpu.PrefetchScalarGridSpec(
             num_scalar_prefetch=1,
             grid=(PARTS,),
-            in_specs=[whole(operand) for operand in operands]
-            + [pl.BlockSpec((rows, 1), lambda i, at: (at[0] * PARTS + i, 0)), by_rows]
+            in_specs=[pl.BlockSpec(memory_space=pltpu.VMEM)] * len(operands)
+            + [pl.BlockSpec((1,) + keep.shape[1:], lambda i, at: (at[0], 0, 0)), by_rows]
             + extra,
-            out_specs=[by_rows, pl.BlockSpec((rows, channels), lambda i, at: (i, 0)), whole(totals)],
-            scratch_shapes=[pltpu.VMEM((rows + 16, channels), f32)],
+            out_specs=[by_rows, pl.BlockSpec((rows, channels), lambda i, at: (i, 0))]
+            + [pl.BlockSpec(memory_space=pltpu.VMEM)] * len(sums),
+            scratch_shapes=([pltpu.VMEM((channels, tracks), f32)] if last else [])
+            + [pltpu.VMEM((rows + 16, channels), f32)],
         ),
         out_shape=[
-            jax.ShapeDtypeStruct((count, tracks), bf16),
-            jax.ShapeDtypeStruct((PARTS * rows, channels), bf16),
-            totals,
+            pltpu.HBM((count, tracks), bf16),
+            pltpu.HBM((PARTS * rows, channels), bf16),
+            *sums,
         ],
-        input_output_aliases={} if first else {at_input: 0, at_input + 1: 2},
+        input_output_aliases={} if first else {at_input: 0},
         cost_estimate=pl.CostEstimate(
             flops=2 * PARTS * rows * (conv_w.size + 3 * head_w.size),
             transcendentals=4 * PARTS * rows * tracks,
             bytes_accessed=16 << 20,
         ),
-        compiler_params=pltpu.CompilerParams(vmem_limit_bytes=36 << 20),
+        compiler_params=pltpu.CompilerParams(vmem_limit_bytes=HEADV << 20),
         name="head_pass",
     )(at, *operands, keep, targets, *(carried or ()))
 
@@ -296,32 +340,33 @@
     meansq = jnp.mean(widened * widened, axis=1, keepdims=True)
     normed = (widened * lax.rsqrt(meansq + 1e-06) * norm_gain).astype(bf16)
     keyvals = jnp.dot(normed, w_kv, preferred_element_type=f32).astype(bf16)
-    skip_pair = jnp.concatenate([skip, moved(skip, 2, 2)], 0)
+    skip_parts = [moved(skip, 1, step) for step in (1, 2, 3)]
     for dim in (2, 1):
-        keyvals = jnp.concatenate([keyvals] + [moved(keyvals, dim, step) for step in (1, 3, 2)], 0)
-    skip_pair, keyvals = lax.optimization_barrier((skip_pair, keyvals))
+        keyvals = join(keyvals, *[moved(keyvals, dim, step) for step in (1, 3, 2)])
+    skip_parts, keyvals = lax.optimization_barrier((skip_parts, keyvals))
+    skip_run = join(skip, *skip_parts)
     queries = jnp.dot(normed, w_query, preferred_element_type=f32).astype(bf16)
     crossed = moved(keyvals, 3, 1)
     pieces = [moved(keyvals, 0, step) for step in (1, 3, 2)]
-    skips = [skip_pair] + [moved(skip_pair, 1, step) for step in (1, 2, 3)]
+    skips = [skip_run, moved(skip_run, 2, 2)]
     state = attend(None, queries, [keyvals], head_dim)
     for piece in pieces:
         state = attend(state, queries, [crossed, piece], head_dim)
         crossed = moved(piece, 3, 1)
     state = attend(state, queries, [crossed], head_dim)
+    state, skips = lax.optimization_barrier((state, skips))
     upward = project(state, trunk, w_out, w_up)
-    up_pair = jnp.concatenate([upward, moved(upward, 2, 2)], 0)
+    up_pair = join(upward, moved(upward, 2, 2))
     ups = [up_pair] + [moved(up_pair, 1, step) for step in (1, 2, 3)]
     y, zh, core = lax.axis_index("y"), lax.axis_index("zh"), lax.axis_index("core")
-    wide = expand(jnp.stack([y, zh]).astype(jnp.int32), ups, skips)
-    factor = skip.shape[0] // row_count
+    wide, edge_first, edge_last = expand(jnp.stack([y, zh]).astype(jnp.int32), ups, skips)
     tap_count, channels = conv_w.shape[:2]
     rim = tap_count // 2
     pos_count = targets.shape[0]
     n_bin = lax.axis_size(BIN)
     up_pairs = [(i, i + 1) for i in range(n_bin - 1)]
-    before = lax.ppermute(wide[pos_count + 8 - rim : pos_count + 8].astype(bf16), BIN, up_pairs)
-    after = lax.ppermute(wide[8 : 8 + rim].astype(bf16), BIN, [(j, i) for i, j in up_pairs])
+    before = lax.ppermute(edge_last, BIN, up_pairs)
+    after = lax.ppermute(edge_first, BIN, [(j, i) for i, j in up_pairs])
     tile_width = head_w.shape[1]
     groups = group_weight.shape[0]
     total_tracks = group_ids.shape[0]
@@ -330,10 +375,13 @@
     per_group = group_weight * total_tracks / (groups * counts.astype(f32))
     local_ids = lax.dynamic_slice_in_dim(group_ids, lax.axis_index(TRK) * tile_width, tile_width, 0)
     track_scale = jnp.sum(jnp.where(local_ids == labels[None, :], per_group[None, :], 0.0), axis=1)
-    keep_mask = 1.0 - jnp.repeat(missing.astype(f32), factor)[:, None]
+    keep_mask = 1.0 - missing.astype(f32).reshape(4, 1, missing.shape[0] // 4)
+    targets = pltpu.with_memory_space_constraint(targets, pltpu.HBM)
     carried, received = None, []
     for step in (2, 1, 3, 0):
-        prediction, partial, total = head_pass(
+        if step == 0:
+            before, received[0] = lax.optimization_barrier((before, received[0]))
+        prediction, partial, *total = head_pass(
             jnp.stack([lax.rem(y + step, 4), core]).astype(jnp.int32),
             carried,
             wide,
@@ -348,17 +396,17 @@
             step == 0,
             pos_count * n_bin,
         )
-        carried = (prediction, total)
+        carried = (prediction, *total)
         received.append(moved(partial, 1, step) if step else partial)
+    mine, theirs = total
+    theirs, received[1] = lax.optimization_barrier((theirs, received[1]))
     summed = sum(part.astype(f32) for part in received)
     halves = summed.reshape(2, summed.shape[0] // 2, channels)
     away = lax.dynamic_index_in_dim(halves, 1 - zh, 0, keepdims=False).astype(bf16)
     here = lax.dynamic_index_in_dim(halves, zh, 0, keepdims=False)
     feature_grad = (here + moved(away, 2, 2).astype(f32)).astype(bf16)
-    blocks = total.reshape(lax.axis_size("bz"), 2, channels // n_bin, tile_width)
-    mine = lax.dynamic_index_in_dim(blocks, core, 1, keepdims=False)
-    theirs = lax.dynamic_index_in_dim(blocks, 1 - core, 1, keepdims=False).astype(bf16)
     pair_sum = (mine + lax.ppermute(theirs, "core", [(0, 1), (1, 0)]).astype(f32)).astype(bf16)
+    pair_sum = pair_sum.reshape(lax.axis_size("bz"), channels // n_bin, tile_width)
     gathered = lax.all_to_all(pair_sum, "bz", 0, 0, tiled=True)
     head_grad = jnp.sum(gathered.astype(f32), axis=0)
     return (prediction, head_grad, feature_grad)

time: 236 us -> 185 us (0.78)
  local copies, waits for them, and re-layouts: 23.3 us -> 2.87 us
  waiting for transfers between devices: 79.3 us -> 64 us
  Pallas kernels: 69.9 us -> 61.2 us
  starting transfers between devices: 45.1 us -> 42.4 us
    ppermute x25, waiting for transfers between devices: 79.3 us -> 58.8 us  [moved(): return lax.ppermute(value, ALL, pairs)]
    unnamed x45 -> x36, local copies, waits for them, and re-layouts: 18 us -> 1.98 us
    pallas_call x4, Pallas kernels: 50 us -> 44 us  [head_pass(): pl.pallas_call(functools.partial(head_kernel, first, last, positions), gr...]
    pallas_call x5, Pallas kernels: 16.1 us -> 10.7 us  [attend(): pl.pallas_call(functools.partial(attend_kernel, head_dim, state is None),...]
    ppermute x2, waiting for transfers between devices: 0.01 us -> 2.82 us  [the longest x1 2.81 us: body(): after = lax.ppermute(edge_first, BIN, [(j, i) for i, j in up_pairs])]
  transfers between devices with their start and end apart: 29 -> 29, of which waited for: 15 -> 15; matrix products, arithmetic and copies ran while one was open for 7% -> 6% of each run, Pallas kernels for 7% -> 24%
where the time goes in v3:
time: 185 us; the launch traced here: 183 us
  waiting for transfers between devices  64 us (35%)
  Pallas kernels  61.2 us (33%)
  starting transfers between devices  42.4 us (23%)
  other arithmetic  9.65 us (5%)
  local copies, waits for them, and re-layouts  2.87 us (2%)
  matrix products  2.27 us (1%)
    ppermute x25, waiting for transfers between devices, moved(): return lax.ppermute(value, ALL, pairs)  58.8 us
    pallas_call x4, Pallas kernels, head_pass(): pl.pallas_call(functools.partial(head_kernel, first, last, positions), gr...  44 us
    ppermute x25, starting transfers between devices, moved(): return lax.ppermute(value, ALL, pairs)  33.5 us
    pallas_call x5, Pallas kernels, attend(): pl.pallas_call(functools.partial(attend_kernel, head_dim, state is None),...  10.7 us
    all_to_all x1, starting transfers between devices, body(): gathered = lax.all_to_all(pair_sum, 'bz', 0, 0, tiled=True)  4.56 us
  transfers between devices with their start and end apart: 29, of which 15 were waited for; matrix products, arithmetic and copies ran while one was open for 6% of the time, Pallas kernels for 24%

profile of v3, /device:TPU:0, one launch (start us, length us, event | category | flops | bytes accessed | tf_op | source)
XLA Modules:
  0.0 183.4 jit_solution(10488095282283540136)
XLA Ops:
  2.4 2.9 %collective-permute-start.1 = (bf16[256,768]{1,0:T(8,128)(2,1)}, bf16[256,768]{1,0:T(8,128)(2,1)S(1)}, u32[]{:S(2)}, u32[]{:S(2)}) collective-permute-start(bf16[256,768]{1,0:T(8,128)(2,1)} %refs_0_.1), channel_id=1, source_target_pairs={{0,4},{1,5},{2,6},{3,7},{4,0},{5,1},{6,2},{7,3},{8,12},{9,13},{10,... | collective-permute-start | bytes 1179656 | tf_op jit(solution)/shard_map/ppermute | solution.py:40
  17.1 3.6 %collective-permute-done.5.refs_3_ = bf16[64,256]{1,0:T(8,128)(2,1)S(1)} collective-permute-done((bf16[64,256]{1,0:T(8,128)(2,1)S(1)}, bf16[64,256]{1,0:T(8,128)(2,1)S(1)}, u32[]{:S(2)}, u32[]{:S(2)}) %collective-permute-start.5) | collective-permute-done | bytes 32800 | tf_op jit(solution)/shard_map/ppermute | solution.py:40
  21.5 2.6 %collective-permute-start.7 = (bf16[256,256]{1,0:T(8,128)(2,1)S(1)}, bf16[256,256]{1,0:T(8,128)(2,1)S(1)}, u32[]{:S(2)}, u32[]{:S(2)}) collective-permute-start(bf16[256,256]{1,0:T(8,128)(2,1)S(1)} %join.4.refs_0_), channel_id=1, source_target_pairs={{0,6},{1,7},{2,0},{3,1},{4,2},{5,3},{6,4},{7,5},{8,14},{9,15},{10,... | collective-permute-start | bytes 393224 | tf_op jit(solution)/shard_map/ppermute | solution.py:40
  24.0 2.9 %collective-permute-done.6.refs_1_ = bf16[256,256]{1,0:T(8,128)(2,1)S(1)} collective-permute-done((bf16[256,256]{1,0:T(8,128)(2,1)S(1)}, bf16[256,256]{1,0:T(8,128)(2,1)S(1)}, u32[]{:S(2)}, u32[]{:S(2)}) %collective-permute-start.6) | collective-permute-done | bytes 131104 | tf_op jit(solution)/shard_map/ppermute | solution.py:40
  27.9 5.5 %collective-permute-done.8.refs_3_ = bf16[256,256]{1,0:T(8,128)(2,1)S(1)} collective-permute-done((bf16[256,256]{1,0:T(8,128)(2,1)S(1)}, bf16[256,256]{1,0:T(8,128)(2,1)S(1)}, u32[]{:S(2)}, u32[]{:S(2)}) %collective-permute-start.8) | collective-permute-done | bytes 131104 | tf_op jit(solution)/shard_map/ppermute | solution.py:40
  35.6 2.5 %collective-permute-start.16 = (bf16[1024,768]{1,0:T(8,128)(2,1)}, bf16[1024,768]{1,0:T(8,128)(2,1)}, u32[]{:S(2)}, u32[]{:S(2)}) collective-permute-start(bf16[1024,768]{1,0:T(8,128)(2,1)} %join.6.refs_4_), channel_id=1, source_target_pairs={{0,1},{1,0},{2,3},{3,2},{4,5},{5,4},{6,7},{7,6},{8,9},{9,8},{10,11... | collective-permute-start | bytes 4718600 | tf_op jit(solution)/shard_map/ppermute | solution.py:40
  44.1 9.4 %collective-permute-done.13.refs_2_ = bf16[1024,256]{1,0:T(8,128)(2,1)} collective-permute-done((bf16[1024,256]{1,0:T(8,128)(2,1)}, bf16[1024,256]{1,0:T(8,128)(2,1)}, u32[]{:S(2)}, u32[]{:S(2)}) %collective-permute-start.13) | collective-permute-done | bytes 524320 | tf_op jit(solution)/shard_map/ppermute | solution.py:40
  53.4 8.1 %collective-permute-done.11.refs_2_ = bf16[1024,256]{1,0:T(8,128)(2,1)} collective-permute-done((bf16[1024,256]{1,0:T(8,128)(2,1)}, bf16[1024,256]{1,0:T(8,128)(2,1)}, u32[]{:S(2)}, u32[]{:S(2)}) %collective-permute-start.11) | collective-permute-done | bytes 524320 | tf_op jit(solution)/shard_map/ppermute | solution.py:40
  65.4 2.6 %attend.6 = (f32[512,128]{1,0:T(8,128)S(1)}, f32[512,128]{1,0:T(8,128)S(1)}) custom-call(bf16[64,1024]{1,0:T(8,128)(2,1)S(1)} %convolution_convert_fusion.refs_0_, bf16[1024,256]{1,0:T(8,128)(2,1)} %collective-permute-done.15.refs_1_, bf16[1024,256]{1,0:T(8,128)(2,1)} %collective-permute-done.13.refs_2_, f32[512,128]{1,0:T(8,128)S(1)} %get-tuple-element.42.refs_3_, ...), custom_call_target="tpu_custom_call" | custom-call | flops 1073741824 | bytes 1048576 | tf_op jit(solution)/shard_map/attend/pallas_call | solution.py:101
  68.0 2.6 %attend.7 = (f32[512,128]{1,0:T(8,128)S(1)}, f32[512,128]{1,0:T(8,128)S(1)}) custom-call(bf16[64,1024]{1,0:T(8,128)(2,1)S(1)} %convolution_convert_fusion.refs_0_, bf16[1024,256]{1,0:T(8,128)(2,1)} %collective-permute-done.14.refs_1_, bf16[1024,256]{1,0:T(8,128)(2,1)} %collective-permute-done.11.refs_2_, f32[512,128]{1,0:T(8,128)S(1)} %get-tuple-element.44.refs_3_, ...), custom_call_target="tpu_custom_call" | custom-call | flops 1073741824 | bytes 1048576 | tf_op jit(solution)/shard_map/attend/pallas_call | solution.py:101
  70.6 2.7 %attend.8 = (f32[512,128]{1,0:T(8,128)S(1)}, f32[512,128]{1,0:T(8,128)S(1)}) custom-call(bf16[64,1024]{1,0:T(8,128)(2,1)S(1)} %convolution_convert_fusion.refs_0_, bf16[1024,256]{1,0:T(8,128)(2,1)} %collective-permute-done.12.refs_1_, bf16[1024,256]{1,0:T(8,128)(2,1)} %collective-permute-done.9.refs_2_, f32[512,128]{1,0:T(8,128)S(1)} %get-tuple-element.46.refs_3_, ...), custom_call_target="tpu_custom_call" | custom-call | flops 1073741824 | bytes 1048576 | tf_op jit(solution)/shard_map/attend/pallas_call | solution.py:101
  75.7 6.4 %collective-permute-done.17.refs_1_ = bf16[64,768]{1,0:T(8,128)(2,1)S(1)} collective-permute-done((bf16[64,768]{1,0:T(8,128)(2,1)S(1)}, bf16[64,768]{1,0:T(8,128)(2,1)S(1)}, u32[]{:S(2)}, u32[]{:S(2)}) %collective-permute-start.17) | collective-permute-done | bytes 98336 | tf_op jit(solution)/shard_map/ppermute | solution.py:40
  84.2 2.5 %collective-permute-start.20 = (bf16[128,768]{1,0:T(8,128)(2,1)S(1)}, bf16[128,768]{1,0:T(8,128)(2,1)S(1)}, u32[]{:S(2)}, u32[]{:S(2)}) collective-permute-start(bf16[128,768]{1,0:T(8,128)(2,1)S(1)} %join.7.refs_0_), channel_id=1, source_target_pairs={{0,6},{1,7},{2,0},{3,1},{4,2},{5,3},{6,4},{7,5},{8,14},{9,15},{10,... | collective-permute-start | bytes 589832 | tf_op jit(solution)/shard_map/ppermute | solution.py:40
  86.8 7.3 %collective-permute-done.18.refs_1_ = bf16[128,768]{1,0:T(8,128)(2,1)S(1)} collective-permute-done((bf16[128,768]{1,0:T(8,128)(2,1)S(1)}, bf16[128,768]{1,0:T(8,128)(2,1)S(1)}, u32[]{:S(2)}, u32[]{:S(2)}) %collective-permute-start.18) | collective-permute-done | bytes 196640 | tf_op jit(solution)/shard_map/ppermute | solution.py:40
  94.7 3.5 %expand.1 = (f32[2064,768]{1,0:T(8,128)S(1)}, bf16[8,768]{1,0:T(8,128)(2,1)S(1)}, bf16[8,768]{1,0:T(8,128)(2,1)S(1)}) custom-call(s32[2]{0:T(128)S(1)} %pad_add_fusion.1.at_ref, bf16[128,768]{1,0:T(8,128)(2,1)S(1)} %join.7.refs_0_, bf16[128,768]{1,0:T(8,128)(2,1)S(1)} %collective-permute-done.18.refs_1_, ...), custom_call_target="tpu_custom_call" | custom-call | flops 202899456 | bytes 10485760 | tf_op jit(solution)/shard_map/expand/pallas_call | solution.py:181
  101.1 2.8 %collective-permute-done.22.after_ref = bf16[8,768]{1,0:T(8,128)(2,1)S(1)} collective-permute-done((bf16[8,768]{1,0:T(8,128)(2,1)S(1)}, bf16[8,768]{1,0:T(8,128)(2,1)S(1)}, u32[]{:S(2)}, u32[]{:S(2)}) %collective-permute-start.22) | collective-permute-done | bytes 12320 | tf_op jit(solution)/shard_map/ppermute | solution.py:369
  104.0 10.7 %head_pass.4 = (bf16[2048,768]{1,0:T(8,128)(2,1)}, bf16[512,768]{1,0:T(8,128)(2,1)}, f32[768,768]{1,0:T(8,128)S(1)}) custom-call(s32[2]{0:T(128)S(1)} %get-tuple-element.80.at_ref, f32[2064,768]{1,0:T(8,128)S(1)} %get-tuple-element.59.wide_ref, bf16[8,768]{1,0:T(8,128)(2,1)S(1)} %collective-permute-done.21.before_ref, ...), custom_call_target="tpu_custom_call" | custom-call | flops 4831838208 | bytes 16777216 | tf_op jit(solution)/shard_map/head_pass/pallas_call | solution.py:290
  116.7 10.9 %head_pass.5 = (bf16[2048,768]{1,0:T(8,128)(2,1)}, bf16[512,768]{1,0:T(8,128)(2,1)}, f32[768,768]{1,0:T(8,128)S(1)}) custom-call(s32[2]{0:T(128)S(1)} %get-tuple-element.82.at_ref, f32[2064,768]{1,0:T(8,128)S(1)} %get-tuple-element.59.wide_ref, bf16[8,768]{1,0:T(8,128)(2,1)S(1)} %collective-permute-done.21.before_ref, ...), custom_call_target="tpu_custom_call", output_to_operand_aliasing={{0}: (10, {})} | custom-call | flops 4831838208 | bytes 16777216 | tf_op jit(solution)/shard_map/head_pass/pallas_call | solution.py:290
  129.1 10.9 %head_pass.6 = (bf16[2048,768]{1,0:T(8,128)(2,1)}, bf16[512,768]{1,0:T(8,128)(2,1)}, f32[768,768]{1,0:T(8,128)S(1)}) custom-call(s32[2]{0:T(128)S(1)} %get-tuple-element.81.at_ref, f32[2064,768]{1,0:T(8,128)S(1)} %get-tuple-element.59.wide_ref, bf16[8,768]{1,0:T(8,128)(2,1)S(1)} %collective-permute-done.21.before_ref, ...), custom_call_target="tpu_custom_call", output_to_operand_aliasing={{0}: (10, {})} | custom-call | flops 4831838208 | bytes 16777216 | tf_op jit(solution)/shard_map/head_pass/pallas_call | solution.py:290
  141.8 11.3 %head_pass.7 = (bf16[2048,768]{1,0:T(8,128)(2,1)}, bf16[512,768]{1,0:T(8,128)(2,1)}, f32[384,768]{1,0:T(8,128)S(1)}, bf16[384,768]{1,0:T(8,128)(2,1)}) custom-call(s32[2]{0:T(128)S(1)} %get-tuple-element.79.at_ref, f32[2064,768]{1,0:T(8,128)S(1)} %get-tuple-element.59.wide_ref, ...), custom_call_target="tpu_custom_call", output_to_operand_aliasing={{0}: (10, {})} | custom-call | flops 4831838208 | bytes 16777216 | tf_op jit(solution)/shard_map/head_pass/pallas_call | solution.py:290
  156.7 3.2 %collective-permute-done.26 = bf16[512,768]{1,0:T(8,128)(2,1)} collective-permute-done((bf16[512,768]{1,0:T(8,128)(2,1)}, bf16[512,768]{1,0:T(8,128)(2,1)}, u32[]{:S(2)}, u32[]{:S(2)}) %collective-permute-start.26) | collective-permute-done | bytes 786464 | tf_op jit(solution)/shard_map/ppermute | solution.py:40
  165.4 4.6 %all-to-all-start = ((bf16[8,48,768]{2,1,0:T(8,128)(2,1)}), bf16[8,48,768]{2,1,0:T(8,128)(2,1)}, u32[]{:S(2)}, u32[]{:S(2)}) async-start(bf16[8,48,768]{2,1,0:T(8,128)(2,1)} %bitcast.27), calls=%async_computation | async-start | bytes 1179648 | tf_op jit(solution)/shard_map/all_to_all | solution.py:410
  170.0 7.4 %collective-permute-done.27 = bf16[256,768]{1,0:T(8,128)(2,1)S(1)} collective-permute-done((bf16[256,768]{1,0:T(8,128)(2,1)}, bf16[256,768]{1,0:T(8,128)(2,1)S(1)}, u32[]{:S(2)}, u32[]{:S(2)}) %collective-permute-start.27) | collective-permute-done | bytes 393248 | tf_op jit(solution)/shard_map/ppermute | solution.py:40
  179.3 2.3 %all-to-all-done = bf16[8,48,768]{2,1,0:T(8,128)(2,1)} async-done(((bf16[8,48,768]{2,1,0:T(8,128)(2,1)}), bf16[8,48,768]{2,1,0:T(8,128)(2,1)}, u32[]{:S(2)}, u32[]{:S(2)}) %all-to-all-start) | async-done | bytes 589856 | tf_op jit(solution)/shard_map/all_to_all | solution.py:410
  (105 shorter events, 53.2 us)
Async XLA Ops:
  0.7 33.6 %collective-permute-start = (bf16[256,768]{1,0:T(8,128)(2,1)}, bf16[256,768]{1,0:T(8,128)(2,1)S(1)}, u32[]{:S(2)}, u32[]{:S(2)}) collective-permute-start(bf16[256,768]{1,0:T(8,128)(2,1)} %refs_0_.1), channel_id=1, source_target_pairs={{0,2},{1,3},{2,4},{3,5},{4,6},{5,7},{6,0},{7,1},{8,10},{9,11},{10,... | collective-permute-start | bytes 1179656 | tf_op jit(solution)/shard_map/ppermute | solution.py:40
  2.4 31.9 %collective-permute-start.1 = (bf16[256,768]{1,0:T(8,128)(2,1)}, bf16[256,768]{1,0:T(8,128)(2,1)S(1)}, u32[]{:S(2)}, u32[]{:S(2)}) collective-permute-start(bf16[256,768]{1,0:T(8,128)(2,1)} %refs_0_.1), channel_id=1, source_target_pairs={{0,4},{1,5},{2,6},{3,7},{4,0},{5,1},{6,2},{7,3},{8,12},{9,13},{10,... | collective-permute-start | bytes 1179656 | tf_op jit(solution)/shard_map/ppermute | solution.py:40
  5.3 29.0 %collective-permute-start.2 = (bf16[256,768]{1,0:T(8,128)(2,1)}, bf16[256,768]{1,0:T(8,128)(2,1)S(1)}, u32[]{:S(2)}, u32[]{:S(2)}) collective-permute-start(bf16[256,768]{1,0:T(8,128)(2,1)} %refs_0_.1), channel_id=1, source_target_pairs={{0,6},{1,7},{2,0},{3,1},{4,2},{5,3},{6,4},{7,5},{8,14},{9,15},{10,... | collective-permute-start | bytes 1179656 | tf_op jit(solution)/shard_map/ppermute | solution.py:40
  20.7 6.2 %collective-permute-start.6 = (bf16[256,256]{1,0:T(8,128)(2,1)S(1)}, bf16[256,256]{1,0:T(8,128)(2,1)S(1)}, u32[]{:S(2)}, u32[]{:S(2)}) collective-permute-start(bf16[256,256]{1,0:T(8,128)(2,1)S(1)} %join.4.refs_0_), channel_id=1, source_target_pairs={{0,2},{1,3},{2,4},{3,5},{4,6},{5,7},{6,0},{7,1},{8,10},{9,11},{10,... | collective-permute-start | bytes 393224 | tf_op jit(solution)/shard_map/ppermute | solution.py:40
  21.5 6.5 %collective-permute-start.7 = (bf16[256,256]{1,0:T(8,128)(2,1)S(1)}, bf16[256,256]{1,0:T(8,128)(2,1)S(1)}, u32[]{:S(2)}, u32[]{:S(2)}) collective-permute-start(bf16[256,256]{1,0:T(8,128)(2,1)S(1)} %join.4.refs_0_), channel_id=1, source_target_pairs={{0,6},{1,7},{2,0},{3,1},{4,2},{5,3},{6,4},{7,5},{8,14},{9,15},{10,... | collective-permute-start | bytes 393224 | tf_op jit(solution)/shard_map/ppermute | solution.py:40
  27.0 6.5 %collective-permute-start.8 = (bf16[256,256]{1,0:T(8,128)(2,1)S(1)}, bf16[256,256]{1,0:T(8,128)(2,1)S(1)}, u32[]{:S(2)}, u32[]{:S(2)}) collective-permute-start(bf16[256,256]{1,0:T(8,128)(2,1)S(1)} %join.4.refs_0_), channel_id=1, source_target_pairs={{0,4},{1,5},{2,6},{3,7},{4,0},{5,1},{6,2},{7,3},{8,12},{9,13},{10,... | collective-permute-start | bytes 393224 | tf_op jit(solution)/shard_map/ppermute | solution.py:40
  35.6 38.7 %collective-permute-start.16 = (bf16[1024,768]{1,0:T(8,128)(2,1)}, bf16[1024,768]{1,0:T(8,128)(2,1)}, u32[]{:S(2)}, u32[]{:S(2)}) collective-permute-start(bf16[1024,768]{1,0:T(8,128)(2,1)} %join.6.refs_4_), channel_id=1, source_target_pairs={{0,1},{1,0},{2,3},{3,2},{4,5},{5,4},{6,7},{7,6},{8,9},{9,8},{10,11... | collective-permute-start | bytes 4718600 | tf_op jit(solution)/shard_map/ppermute | solution.py:40
  38.0 15.4 %collective-permute-start.13 = (bf16[1024,256]{1,0:T(8,128)(2,1)}, bf16[1024,256]{1,0:T(8,128)(2,1)}, u32[]{:S(2)}, u32[]{:S(2)}) collective-permute-start(bf16[1024,256]{1,0:T(8,128)(2,1)} %join.5.refs_1_), channel_id=1, source_target_pairs={{0,16},{1,17},{2,18},{3,19},{4,20},{5,21},{6,22},{7,23},{8,24},{9,... | collective-permute-start | bytes 1572872 | tf_op jit(solution)/shard_map/ppermute | solution.py:40
  39.5 22.0 %collective-permute-start.11 = (bf16[1024,256]{1,0:T(8,128)(2,1)}, bf16[1024,256]{1,0:T(8,128)(2,1)}, u32[]{:S(2)}, u32[]{:S(2)}) collective-permute-start(bf16[1024,256]{1,0:T(8,128)(2,1)} %join.5.refs_1_), channel_id=1, source_target_pairs={{0,48},{1,49},{2,50},{3,51},{4,52},{5,53},{6,54},{7,55},{8,56},{9,... | collective-permute-start | bytes 1572872 | tf_op jit(solution)/shard_map/ppermute | solution.py:40
  41.3 22.0 %collective-permute-start.9 = (bf16[1024,256]{1,0:T(8,128)(2,1)}, bf16[1024,256]{1,0:T(8,128)(2,1)}, u32[]{:S(2)}, u32[]{:S(2)}) collective-permute-start(bf16[1024,256]{1,0:T(8,128)(2,1)} %join.5.refs_1_), channel_id=1, source_target_pairs={{0,32},{1,33},{2,34},{3,35},{4,36},{5,37},{6,38},{7,39},{8,40},{9,... | collective-permute-start | bytes 1572872 | tf_op jit(solution)/shard_map/ppermute | solution.py:40
  43.8 21.6 %collective-permute-start.15 = (bf16[1024,256]{1,0:T(8,128)(2,1)}, bf16[1024,256]{1,0:T(8,128)(2,1)}, u32[]{:S(2)}, u32[]{:S(2)}) collective-permute-start(bf16[1024,256]{1,0:T(8,128)(2,1)} %join.5.refs_1_), channel_id=1, source_target_pairs={{0,8},{1,9},{2,10},{3,11},{4,12},{5,13},{6,14},{7,15},{8,0},{9,1},... | collective-permute-start | bytes 1572872 | tf_op jit(solution)/shard_map/ppermute | solution.py:40
  53.4 14.6 %collective-permute-start.14 = (bf16[1024,256]{1,0:T(8,128)(2,1)}, bf16[1024,256]{1,0:T(8,128)(2,1)}, u32[]{:S(2)}, u32[]{:S(2)}) collective-permute-start(bf16[1024,256]{1,0:T(8,128)(2,1)} %collective-permute-done.13.refs_2_), channel_id=1, source_target_pairs={{0,8},{1,9},{2,10},{3,11},{4,12},{5,13},{6,14},{7,15},{8,0},{9,1},... | collective-permute-start | bytes 1572872 | tf_op jit(solution)/shard_map/ppermute | solution.py:40
  61.6 9.0 %collective-permute-start.12 = (bf16[1024,256]{1,0:T(8,128)(2,1)}, bf16[1024,256]{1,0:T(8,128)(2,1)}, u32[]{:S(2)}, u32[]{:S(2)}) collective-permute-start(bf16[1024,256]{1,0:T(8,128)(2,1)} %collective-permute-done.11.refs_2_), channel_id=1, source_target_pairs={{0,8},{1,9},{2,10},{3,11},{4,12},{5,13},{6,14},{7,15},{8,0},{9,1},... | collective-permute-start | bytes 1572872 | tf_op jit(solution)/shard_map/ppermute | solution.py:40
  63.2 10.1 %collective-permute-start.10 = (bf16[1024,256]{1,0:T(8,128)(2,1)}, bf16[1024,256]{1,0:T(8,128)(2,1)S(1)}, u32[]{:S(2)}, u32[]{:S(2)}) collective-permute-start(bf16[1024,256]{1,0:T(8,128)(2,1)} %collective-permute-done.9.refs_2_), channel_id=1, source_target_pairs={{0,8},{1,9},{2,10},{3,11},{4,12},{5,13},{6,14},{7,15},{8,0},{9,1},... | collective-permute-start | bytes 1572872 | tf_op jit(solution)/shard_map/ppermute | solution.py:40
  75.3 6.8 %collective-permute-start.17 = (bf16[64,768]{1,0:T(8,128)(2,1)S(1)}, bf16[64,768]{1,0:T(8,128)(2,1)S(1)}, u32[]{:S(2)}, u32[]{:S(2)}) collective-permute-start(bf16[64,768]{1,0:T(8,128)(2,1)S(1)} %project.1.refs_0_), channel_id=1, source_target_pairs={{0,1},{1,0},{2,3},{3,2},{4,5},{5,4},{6,7},{7,6},{8,9},{9,8},{10,11... | collective-permute-start | bytes 294920 | tf_op jit(solution)/shard_map/ppermute | solution.py:40
  82.1 12.0 %collective-permute-start.18 = (bf16[128,768]{1,0:T(8,128)(2,1)S(1)}, bf16[128,768]{1,0:T(8,128)(2,1)S(1)}, u32[]{:S(2)}, u32[]{:S(2)}) collective-permute-start(bf16[128,768]{1,0:T(8,128)(2,1)S(1)} %join.7.refs_0_), channel_id=1, source_target_pairs={{0,2},{1,3},{2,4},{3,5},{4,6},{5,7},{6,0},{7,1},{8,10},{9,11},{10,... | collective-permute-start | bytes 589832 | tf_op jit(solution)/shard_map/ppermute | solution.py:40
  82.2 11.9 %collective-permute-start.19 = (bf16[128,768]{1,0:T(8,128)(2,1)S(1)}, bf16[128,768]{1,0:T(8,128)(2,1)S(1)}, u32[]{:S(2)}, u32[]{:S(2)}) collective-permute-start(bf16[128,768]{1,0:T(8,128)(2,1)S(1)} %join.7.refs_0_), channel_id=1, source_target_pairs={{0,4},{1,5},{2,6},{3,7},{4,0},{5,1},{6,2},{7,3},{8,12},{9,13},{10,... | collective-permute-start | bytes 589832 | tf_op jit(solution)/shard_map/ppermute | solution.py:40
  84.2 10.5 %collective-permute-start.20 = (bf16[128,768]{1,0:T(8,128)(2,1)S(1)}, bf16[128,768]{1,0:T(8,128)(2,1)S(1)}, u32[]{:S(2)}, u32[]{:S(2)}) collective-permute-start(bf16[128,768]{1,0:T(8,128)(2,1)S(1)} %join.7.refs_0_), channel_id=1, source_target_pairs={{0,6},{1,7},{2,0},{3,1},{4,2},{5,3},{6,4},{7,5},{8,14},{9,15},{10,... | collective-permute-start | bytes 589832 | tf_op jit(solution)/shard_map/ppermute | solution.py:40
  114.7 27.1 %collective-permute-start.23 = (bf16[512,768]{1,0:T(8,128)(2,1)}, bf16[512,768]{1,0:T(8,128)(2,1)S(1)}, u32[]{:S(2)}, u32[]{:S(2)}) collective-permute-start(bf16[512,768]{1,0:T(8,128)(2,1)} %get-tuple-element.62), channel_id=1, source_target_pairs={{0,4},{1,5},{2,6},{3,7},{4,0},{5,1},{6,2},{7,3},{8,12},{9,13},{10,... | collective-permute-start | bytes 2359304 | tf_op jit(solution)/shard_map/ppermute | solution.py:40
  127.6 26.5 %collective-permute-start.24 = (bf16[512,768]{1,0:T(8,128)(2,1)}, bf16[512,768]{1,0:T(8,128)(2,1)S(1)}, u32[]{:S(2)}, u32[]{:S(2)}) collective-permute-start(bf16[512,768]{1,0:T(8,128)(2,1)} %get-tuple-element.73), channel_id=1, source_target_pairs={{0,2},{1,3},{2,4},{3,5},{4,6},{5,7},{6,0},{7,1},{8,10},{9,11},{10,... | collective-permute-start | bytes 2359304 | tf_op jit(solution)/shard_map/ppermute | solution.py:40
  140.1 19.8 %collective-permute-start.26 = (bf16[512,768]{1,0:T(8,128)(2,1)}, bf16[512,768]{1,0:T(8,128)(2,1)}, u32[]{:S(2)}, u32[]{:S(2)}) collective-permute-start(bf16[512,768]{1,0:T(8,128)(2,1)} %get-tuple-element.77), channel_id=1, source_target_pairs={{0,6},{1,7},{2,0},{3,1},{4,2},{5,3},{6,4},{7,5},{8,14},{9,15},{10,... | collective-permute-start | bytes 2359304 | tf_op jit(solution)/shard_map/ppermute | solution.py:40
  155.1 8.3 %collective-permute-start.25 = (bf16[384,768]{1,0:T(8,128)(2,1)}, bf16[384,768]{1,0:T(8,128)(2,1)}, u32[]{:S(2)}, u32[]{:S(2)}) collective-permute-start(bf16[384,768]{1,0:T(8,128)(2,1)} %get-tuple-element.74), channel_id=1, source_target_pairs={{0,8},{8,0},{1,9},{9,1},{2,10},{10,2},{3,11},{11,3},{4,12},{12,4},... | collective-permute-start | bytes 1769480 | tf_op jit(solution)/shard_map/ppermute | solution.py:408
  163.1 14.3 %collective-permute-start.27 = (bf16[256,768]{1,0:T(8,128)(2,1)}, bf16[256,768]{1,0:T(8,128)(2,1)S(1)}, u32[]{:S(2)}, u32[]{:S(2)}) collective-permute-start(bf16[256,768]{1,0:T(8,128)(2,1)} %fusion.4), channel_id=1, source_target_pairs={{0,1},{1,0},{2,3},{3,2},{4,5},{5,4},{6,7},{7,6},{8,9},{9,8},{10,11... | collective-permute-start | bytes 1179656 | tf_op jit(solution)/shard_map/ppermute | solution.py:40
  165.4 16.2 %all-to-all-start = ((bf16[8,48,768]{2,1,0:T(8,128)(2,1)}), bf16[8,48,768]{2,1,0:T(8,128)(2,1)}, u32[]{:S(2)}, u32[]{:S(2)}) async-start(bf16[8,48,768]{2,1,0:T(8,128)(2,1)} %bitcast.27), calls=%async_computation | async-start | bytes 1179648 | tf_op jit(solution)/shard_map/all_to_all | solution.py:410
  (23 other events, 284.3 us)

commit v4 on v3

v4 whole, which is shorter than its diff:
```python
import functools
import math

import jax
import jax.numpy as jnp
import numpy as np
from jax import lax
from jax.experimental import pallas as pl
from jax.experimental.pallas import tpu as pltpu
from jax.sharding import Mesh, PartitionSpec as P

logit_cap = 20.0
BIN = ("bz", "core")
TRK = ("y", "zh")
ALL = BIN + TRK


def place(index):
    bz, rest = divmod(index, 16)
    core, rest = divmod(rest, 8)
    y, zh = divmod(rest, 2)
    zlo, x = divmod(bz, 4)
    return (x, y, zh * 2 + zlo, core)


def number(x, y, z, core):
    zh, zlo = divmod(z, 2)
    return ((zlo * 4 + x) * 2 + core) * 8 + y * 2 + zh


def moved(value, dim, step):
    sizes = (4, 4, 4, 2)
    pairs = []
    for index in range(128):
        target = list(place(index))
        target[dim] = (target[dim] + step) % sizes[dim]
        pairs.append((index, number(*target)))
    return lax.ppermute(value, ALL, pairs)


def whole(array):
    return pl.BlockSpec(array.shape, lambda *_: (0,) * array.ndim, pipeline_mode=pl.Buffered(1))


def join_kernel(*refs):
    out = refs[-1]
    rows = refs[0].shape[0]
    for index, ref in enumerate(refs[:-1]):
        out[index * rows : (index + 1) * rows, :] = ref[...]


def join(*pieces):
    rows, columns = pieces[0].shape
    out = jax.ShapeDtypeStruct((len(pieces) * rows, columns), pieces[0].dtype)
    return pl.pallas_call(
        join_kernel,
        in_specs=[pl.BlockSpec(memory_space=pltpu.VMEM)] * len(pieces),
        out_specs=pl.BlockSpec(memory_space=pltpu.VMEM),
        out_shape=out,
        cost_estimate=pl.CostEstimate(flops=0, transcendentals=0, bytes_accessed=4 * out.size),
        compiler_params=pltpu.CompilerParams(vmem_limit_bytes=4 << 20),
        name="join",
    )(*pieces)


def attend_kernel(head_dim, first, *refs):
    q_ref, refs = refs[0], refs[1:]
    num_ref, den_ref = refs[-2:]
    pieces = refs[:-2] if first else refs[:-4]
    f32, bf16 = jnp.float32, jnp.bfloat16
    heads = q_ref.shape[1] // head_dim
    queries = jnp.concatenate(
        [q_ref[:, h * head_dim : (h + 1) * head_dim] for h in range(heads)], 0
    )
    inner = 1.0 / (math.sqrt(head_dim) * logit_cap)
    outer = logit_cap * math.log2(math.e)
    num = jnp.zeros(num_ref.shape, f32) if first else refs[-4][...]
    den = jnp.zeros(den_ref.shape, f32) if first else refs[-3][...]
    step = 256
    for piece in pieces:
        for start in range(0, piece.shape[0], step):
            keys = piece[start : start + step, :head_dim]
            values = piece[start : start + step, head_dim:]
            scores = lax.dot_general(
                queries, keys, (((1,), (1,)), ((), ())), preferred_element_type=f32
            )
            weights = jnp.exp2(outer * jnp.tanh(scores * inner))
            num = num + jnp.dot(weights.astype(bf16), values, preferred_element_type=f32)
            for lane in range(0, step, 128):
                den = den + weights[:, lane : lane + 128]
    num_ref[...] = num
    den_ref[...] = den


def attend(state, queries, pieces, head_dim):
    rows = queries.shape[0] * queries.shape[1] // head_dim
    operands = [queries, *pieces, *(state or ())]
    keys = sum(piece.shape[0] for piece in pieces)
    return pl.pallas_call(
        functools.partial(attend_kernel, head_dim, state is None),
        grid=(1,),
        in_specs=[whole(operand) for operand in operands],
        out_specs=[pl.BlockSpec((rows, head_dim), lambda i: (0, 0))] * 2,
        out_shape=[jax.ShapeDtypeStruct((rows, head_dim), jnp.float32)] * 2,
        cost_estimate=pl.CostEstimate(
            flops=8 * rows * keys * head_dim,
            transcendentals=2 * rows * keys,
            bytes_accessed=1 << 20,
        ),
        compiler_params=pltpu.CompilerParams(vmem_limit_bytes=8 << 20),
        name="attend",
    )(*operands)


def project_kernel(num_ref, den_ref, trunk_ref, out_ref, up_ref, skip_ref, wide_ref, first_ref, last_ref):
    f32, bf16 = jnp.float32, jnp.bfloat16
    rows, positions = trunk_ref.shape[0], skip_ref.shape[0]
    total = jnp.sum(den_ref[...], axis=1, keepdims=True)
    ratio = (num_ref[...] / total).astype(bf16)
    heads = ratio.shape[0] // rows
    attended = jnp.concatenate([ratio[h * rows : (h + 1) * rows] for h in range(heads)], 1)
    hidden = (
        trunk_ref[...].astype(f32)
        + jnp.dot(attended, out_ref[...], preferred_element_type=f32)
    ).astype(bf16)
    upward = jnp.dot(hidden, up_ref[...], preferred_element_type=f32)
    factor = positions // rows
    for row in range(rows):
        part = slice(row * factor, (row + 1) * factor)
        wide_ref[part, :] = jnp.broadcast_to(upward[row : row + 1, :], (factor, upward.shape[1]))
    upsampled = (wide_ref[...] + skip_ref[...].astype(f32)).astype(bf16)
    wide_ref[...] = upsampled.astype(f32)
    first_ref[...] = wide_ref[0:8, :].astype(bf16)
    last_ref[...] = wide_ref[positions - 8 : positions, :].astype(bf16)


def project(state, trunk, w_out, w_up, skip):
    operands = (*state, trunk, w_out, w_up, skip)
    edge = jax.ShapeDtypeStruct((8, skip.shape[1]), jnp.bfloat16)
    return pl.pallas_call(
        project_kernel,
        in_specs=[pl.BlockSpec(memory_space=pltpu.VMEM)] * len(operands),
        out_specs=[pl.BlockSpec(memory_space=pltpu.VMEM)] * 3,
        out_shape=[jax.ShapeDtypeStruct(skip.shape, jnp.float32), edge, edge],
        cost_estimate=pl.CostEstimate(
            flops=2 * trunk.shape[0] * (w_out.size + w_up.size),
            transcendentals=0,
            bytes_accessed=2 * (w_out.size + w_up.size),
        ),
        compiler_params=pltpu.CompilerParams(vmem_limit_bytes=8 << 20),
        name="project",
    )(*operands)


def conv_kernel(wide_ref, before_ref, after_ref, conv_ref, feature_ref, near):
    f32, bf16 = jnp.float32, jnp.bfloat16
    rows, channels = wide_ref.shape
    taps = conv_ref.shape[0]
    rim = taps // 2
    near[0:8, :] = before_ref[...].astype(f32)
    near[8 : rows + 8, :] = wide_ref[...]
    near[rows + 8 : rows + 16, :] = after_ref[...].astype(f32)
    conved = jnp.zeros((rows, channels), f32)
    for tap in range(taps):
        begin = 8 - rim + tap
        conved = conved + jnp.dot(
            near[begin : begin + rows, :].astype(bf16), conv_ref[tap], preferred_element_type=f32
        )
    cubic = math.sqrt(2.0 / math.pi) * (conved + 0.044715 * (conved * conved * conved))
    feature_ref[...] = (wide_ref[...] + 0.5 * conved * (1.0 + jnp.tanh(cubic))).astype(bf16)


def convolve(wide, before, after, conv_w):
    operands = (wide, before, after, conv_w)
    return pl.pallas_call(
        conv_kernel,
        in_specs=[pl.BlockSpec(memory_space=pltpu.VMEM)] * len(operands),
        out_specs=pl.BlockSpec(memory_space=pltpu.VMEM),
        out_shape=jax.ShapeDtypeStruct(wide.shape, jnp.bfloat16),
        scratch_shapes=[pltpu.VMEM((wide.shape[0] + 16, wide.shape[1]), jnp.float32)],
        cost_estimate=pl.CostEstimate(
            flops=2 * wide.shape[0] * conv_w.size,
            transcendentals=wide.size,
            bytes_accessed=2 * conv_w.size,
        ),
        compiler_params=pltpu.CompilerParams(vmem_limit_bytes=10 << 20),
        name="convolve",
    )(*operands)


def head_kernel(
    first, last, positions, at_ref, near_ref, far_ref, head_ref, bias_ref, scale_ref, keep_ref, target_ref,
    *refs,
):
    f32, bf16 = jnp.float32, jnp.bfloat16
    if not first:
        old_ref, refs = refs[1], refs[2:]
    pred_ref, partial_ref, sums = refs[0], refs[1], refs[2:]
    total_ref = sums[-1]
    step = pl.program_id(0)
    rows, channels = partial_ref.shape
    bins = keep_ref.shape[2]
    factor = rows // bins
    row = lax.broadcasted_iota(jnp.int32, (rows, bins), 0)
    col = lax.broadcasted_iota(jnp.int32, (rows, bins), 1) * factor
    spread = jnp.where((row >= col) & (row < col + factor), 1.0, 0.0).astype(bf16)
    keep = lax.dot_general(
        spread,
        jnp.broadcast_to(keep_ref[0].astype(bf16), (8, bins)),
        (((1,), (1,)), ((), ())),
        preferred_element_type=f32,
    )[:, :1]
    feature = jnp.where(step == 0, near_ref[...], far_ref[...])
    logits = jnp.dot(feature, head_ref[...], preferred_element_type=f32) + bias_ref[...]
    decay = jnp.exp(-jnp.abs(logits))
    smooth = jnp.maximum(logits, 0.0) + jnp.log1p(decay)
    sigmoid = jnp.where(logits >= 0.0, 1.0, decay) / (1.0 + decay)
    pred_ref[...] = smooth.astype(bf16)
    misfit = smooth - target_ref[...].astype(f32)
    slope = (keep * scale_ref[...] * misfit * sigmoid).astype(bf16)
    partial_ref[...] = lax.dot_general(
        slope, head_ref[...], (((1,), (1,)), ((), ())), preferred_element_type=f32
    ).astype(bf16)
    product = lax.dot_general(
        feature, slope, (((0,), (0,)), ((), ())), preferred_element_type=f32
    )

    @pl.when(step == 0)
    def _():
        total_ref[...] = product if first else product + old_ref[...]

    @pl.when(step > 0)
    def _():
        total_ref[...] += product

    @pl.when(step == 1)
    def _():
        if not last:
            return
        mine_ref, theirs_ref = sums[:2]
        core, height = at_ref[0], channels // 16
        for pair in range(8):
            at = pl.multiple_of((2 * pair + core) * height, height)
            other = pl.multiple_of((2 * pair + 1 - core) * height, height)
            into = slice(pair * height, (pair + 1) * height)
            mine_ref[into, :] = total_ref[pl.ds(at, height), :] / positions
            theirs_ref[into, :] = (total_ref[pl.ds(other, height), :] / positions).astype(bf16)


def head_pass(at, carried, feature, head_w, bias, scale, keep, targets, last, positions):
    f32, bf16 = jnp.float32, jnp.bfloat16
    count, tracks = targets.shape
    channels = head_w.shape[0]
    rows = count // 8
    first = carried is None

    def segment(i, at):
        return at[1] * 2 + jnp.abs(at[2] - i)

    by_rows = pl.BlockSpec((rows, tracks), lambda i, at: (segment(i, at), 0))
    by_step = pl.BlockSpec((rows, channels), lambda i, at: (i, 0))
    vmem = pl.BlockSpec(memory_space=pltpu.VMEM)
    totals = jax.ShapeDtypeStruct((channels, tracks), f32)
    half = (channels // 2, tracks)
    sums = [jax.ShapeDtypeStruct(half, f32), jax.ShapeDtypeStruct(half, bf16)] if last else [totals]
    return pl.pallas_call(
        functools.partial(head_kernel, first, last, positions),
        grid_spec=pltpu.PrefetchScalarGridSpec(
            num_scalar_prefetch=1,
            grid=(2,),
            in_specs=[vmem] * 5
            + [pl.BlockSpec((1,) + keep.shape[1:], lambda i, at: (segment(i, at), 0, 0)), by_rows]
            + ([] if first else [pl.BlockSpec(memory_space=pl.ANY), vmem]),
            out_specs=[by_rows, by_step] + [vmem] * len(sums),
            scratch_shapes=[pltpu.VMEM((channels, tracks), f32)] if last else [],
        ),
        out_shape=[
            pltpu.HBM((count, tracks), bf16),
            jax.ShapeDtypeStruct((2 * rows, channels), bf16),
            *sums,
        ],
        input_output_aliases={} if first else {8: 0},
        cost_estimate=pl.CostEstimate(
            flops=12 * rows * head_w.size,
            transcendentals=8 * rows * tracks,
            bytes_accessed=6 << 20,
        ),
        compiler_params=pltpu.CompilerParams(vmem_limit_bytes=16 << 20),
        name="head_pass",
    )(at, *feature, head_w, bias, scale, keep, targets, *(carried or ()))


def body(
    trunk,
    norm_gain,
    w_query,
    w_kv,
    w_out,
    w_up,
    skip,
    conv_w,
    head_w,
    head_bias,
    targets,
    missing,
    group_ids,
    group_weight,
):
    f32, bf16 = jnp.float32, jnp.bfloat16
    row_count = trunk.shape[0]
    head_dim = w_kv.shape[1] // 2
    head_count = w_query.shape[1] // head_dim
    widened = trunk.astype(f32)
    meansq = jnp.mean(widened * widened, axis=1, keepdims=True)
    normed = (widened * lax.rsqrt(meansq + 1e-06) * norm_gain).astype(bf16)
    keyvals = jnp.dot(normed, w_kv, preferred_element_type=f32).astype(bf16)
    for dim in (2, 1):
        keyvals = join(keyvals, *[moved(keyvals, dim, step) for step in (1, 3, 2)])
    queries = jnp.dot(normed, w_query, preferred_element_type=f32).astype(bf16)
    crossed = moved(keyvals, 3, 1)
    pieces = [moved(keyvals, 0, step) for step in (1, 3, 2)]
    state = attend(None, queries, [keyvals], head_dim)
    for piece in pieces:
        state = attend(state, queries, [crossed, piece], head_dim)
        crossed = moved(piece, 3, 1)
    state = attend(state, queries, [crossed], head_dim)
    wide, edge_first, edge_last = project(state, trunk, w_out, w_up, skip)
    channels = conv_w.shape[1]
    pos_count = targets.shape[0]
    n_bin, n_all = lax.axis_size(BIN), lax.axis_size(ALL)
    ups = [(i, i + 1) for i in range(n_all - 1)]
    before = lax.ppermute(edge_last, ALL, ups)
    after = lax.ppermute(edge_first, ALL, [(j, i) for i, j in ups])
    feature = convolve(wide, before, after, conv_w)
    features = {0: (feature, moved(feature, 2, 2))}
    for step in (2, 1, 3):
        near = moved(feature, 1, step)
        features[step] = (near, moved(near, 2, 2))
    y, zh, core = lax.axis_index("y"), lax.axis_index("zh"), lax.axis_index("core")
    tile_width = head_w.shape[1]
    groups = group_weight.shape[0]
    total_tracks = group_ids.shape[0]
    labels = jnp.arange(groups, dtype=jnp.int32)
    counts = jnp.sum((group_ids == labels[None, :]).astype(jnp.int32), axis=0)
    per_group = group_weight * total_tracks / (groups * counts.astype(f32))
    local_ids = lax.dynamic_slice_in_dim(group_ids, lax.axis_index(TRK) * tile_width, tile_width, 0)
    track_scale = jnp.sum(jnp.where(local_ids == labels[None, :], per_group[None, :], 0.0), axis=1)
    keep_mask = 1.0 - missing.astype(f32).reshape(8, 1, missing.shape[0] // 8)
    targets = pltpu.with_memory_space_constraint(targets, pltpu.HBM)
    carried, received = None, []
    for step in (2, 1, 3, 0):
        if step == 0:
            features[0], received[0] = lax.optimization_barrier((features[0], received[0]))
        prediction, partial, *total = head_pass(
            jnp.stack([core, lax.rem(y + 4 - step, 4), zh]).astype(jnp.int32),
            carried,
            features[step],
            head_w,
            head_bias[None, :],
            track_scale[None, :],
            keep_mask,
            targets,
            step == 0,
            pos_count * n_bin,
        )
        carried = (prediction, *total)
        received.append(moved(partial, 1, 4 - step) if step else partial)
    mine, theirs = total
    theirs, received[1] = lax.optimization_barrier((theirs, received[1]))
    summed = sum(part.astype(f32) for part in received)
    half = summed.shape[0] // 2
    away = summed[half:].astype(bf16)
    feature_grad = (summed[:half] + moved(away, 2, 2).astype(f32)).astype(bf16)
    pair_sum = (mine + lax.ppermute(theirs, "core", [(0, 1), (1, 0)]).astype(f32)).astype(bf16)
    pair_sum = pair_sum.reshape(lax.axis_size("bz"), channels // n_bin, tile_width)
    gathered = lax.all_to_all(pair_sum, "bz", 0, 0, tiled=True)
    head_grad = jnp.sum(gathered.astype(f32), axis=0)
    return (prediction, head_grad, feature_grad)


def solution(mesh):
    inner = Mesh(np.asarray(mesh.devices).reshape(8, 2, 4, 2), ALL)
    in_specs = (
        P(ALL, None),
        P(),
        P(),
        P(),
        P(),
        P(),
        P(ALL, None),
        P(),
        P(None, TRK),
        P(TRK),
        P(BIN, TRK),
        P(BIN),
        P(),
        P(),
    )
    out_specs = (P(BIN, TRK), P(BIN, TRK), P(ALL, None))
    return jax.shard_map(body, mesh=inner, in_specs=in_specs, out_specs=out_specs, check_vma=False)
```

time: 185 us -> 167 us (0.903)
  Pallas kernels: 61.2 us -> 35.1 us
  starting transfers between devices: 42.4 us -> 47.9 us
  local copies, waits for them, and re-layouts: 2.87 us -> 6.9 us
    pallas_call x4, Pallas kernels: 44 us -> 26.1 us  [head_pass(): pl.pallas_call(functools.partial(head_kernel, first, last, positions), gr...]
    ppermute x25 -> x24, starting transfers between devices: 33.5 us -> 39.1 us  [moved(): return lax.ppermute(value, ALL, pairs)]
    pallas_call x5, Pallas kernels: 10.7 us -> 5.92 us  [attend(): pl.pallas_call(functools.partial(attend_kernel, head_dim, state is None),...]
    unnamed x36, local copies, waits for them, and re-layouts: 1.98 us -> 6.07 us
    ppermute x2, waiting for transfers between devices: 2.82 us -> 5.6 us  [the longest x1 5.6 us: body(): after = lax.ppermute(edge_first, ALL, [(j, i) for i, j in ups])]
    pallas_call x4 -> x2, Pallas kernels: 2.11 us -> 0.04 us  [join(): pl.pallas_call(join_kernel, in_specs=[pl.BlockSpec(memory_space=pltpu.VME...]
    ppermute x25 -> x24, waiting for transfers between devices: 58.8 us -> 57.7 us  [moved(): return lax.ppermute(value, ALL, pairs)]
  transfers between devices with their start and end apart: 29 -> 28, of which waited for: 15 -> 14; matrix products, arithmetic and copies ran while one was open for 6% -> 4% of each run, Pallas kernels for 24% -> 19%
where the time goes in v4:
time: 167 us; the launch traced here: 166 us
  waiting for transfers between devices  63.8 us (38%)
  starting transfers between devices  47.9 us (29%)
  Pallas kernels  35.1 us (21%)
  other arithmetic  8.6 us (5%)
  local copies, waits for them, and re-layouts  6.9 us (4%)
  matrix products  2.27 us (1%)
    ppermute x24, waiting for transfers between devices, moved(): return lax.ppermute(value, ALL, pairs)  57.7 us
    ppermute x24, starting transfers between devices, moved(): return lax.ppermute(value, ALL, pairs)  39.1 us
    pallas_call x4, Pallas kernels, head_pass(): pl.pallas_call(functools.partial(head_kernel, first, last, positions), gr...  26.1 us
    unnamed x36, local copies, waits for them, and re-layouts  6.07 us
    pallas_call x5, Pallas kernels, attend(): pl.pallas_call(functools.partial(attend_kernel, head_dim, state is None),...  5.92 us
    ppermute x1, waiting for transfers between devices, body(): after = lax.ppermute(edge_first, ALL, [(j, i) for i, j in ups])  5.6 us
    all_to_all x1, starting transfers between devices, body(): gathered = lax.all_to_all(pair_sum, 'bz', 0, 0, tiled=True)  4.19 us
  transfers between devices with their start and end apart: 28, of which 14 were waited for; matrix products, arithmetic and copies ran while one was open for 4% of the time, Pallas kernels for 19%

profile of v4, /device:TPU:0, one launch (start us, length us, event | category | flops | bytes accessed | tf_op | source)
XLA Modules:
  0.0 165.6 jit_solution(8065819920762979806)
XLA Ops:
  5.5 2.2 %collective-permute-start.1 = (bf16[64,256]{1,0:T(8,128)(2,1)S(1)}, bf16[64,256]{1,0:T(8,128)(2,1)S(1)}, u32[]{:S(2)}, u32[]{:S(2)}) collective-permute-start(bf16[64,256]{1,0:T(8,128)(2,1)S(1)} %convolution_convert_fusion.1.refs_0_), channel_id=1, source_target_pairs={{0,65},{1,64},{2,67},{3,66},{4,69},{5,68},{6,71},{7,70},{8,73},{9,... | collective-permute-start | bytes 98312 | tf_op jit(solution)/shard_map/ppermute | solution.py:38
  9.6 3.6 %collective-permute-done.2.refs_3_ = bf16[64,256]{1,0:T(8,128)(2,1)S(1)} collective-permute-done((bf16[64,256]{1,0:T(8,128)(2,1)S(1)}, bf16[64,256]{1,0:T(8,128)(2,1)S(1)}, u32[]{:S(2)}, u32[]{:S(2)}) %collective-permute-start.2) | collective-permute-done | bytes 32800 | tf_op jit(solution)/shard_map/ppermute | solution.py:38
  18.5 2.4 %collective-permute-done.3.refs_1_ = bf16[256,256]{1,0:T(8,128)(2,1)S(1)} collective-permute-done((bf16[256,256]{1,0:T(8,128)(2,1)S(1)}, bf16[256,256]{1,0:T(8,128)(2,1)S(1)}, u32[]{:S(2)}, u32[]{:S(2)}) %collective-permute-start.3) | collective-permute-done | bytes 131104 | tf_op jit(solution)/shard_map/ppermute | solution.py:38
  20.8 2.1 %collective-permute-done.5.refs_3_ = bf16[256,256]{1,0:T(8,128)(2,1)S(1)} collective-permute-done((bf16[256,256]{1,0:T(8,128)(2,1)S(1)}, bf16[256,256]{1,0:T(8,128)(2,1)S(1)}, u32[]{:S(2)}, u32[]{:S(2)}) %collective-permute-start.5) | collective-permute-done | bytes 131104 | tf_op jit(solution)/shard_map/ppermute | solution.py:38
  28.1 10.0 %collective-permute-done.10.refs_2_ = bf16[1024,256]{1,0:T(8,128)(2,1)S(1)} collective-permute-done((bf16[1024,256]{1,0:T(8,128)(2,1)S(1)}, bf16[1024,256]{1,0:T(8,128)(2,1)S(1)}, u32[]{:S(2)}, u32[]{:S(2)}) %collective-permute-start.10) | collective-permute-done | bytes 524320 | tf_op jit(solution)/shard_map/ppermute | solution.py:38
  38.1 8.1 %collective-permute-done.8.refs_2_ = bf16[1024,256]{1,0:T(8,128)(2,1)S(1)} collective-permute-done((bf16[1024,256]{1,0:T(8,128)(2,1)S(1)}, bf16[1024,256]{1,0:T(8,128)(2,1)S(1)}, u32[]{:S(2)}, u32[]{:S(2)}) %collective-permute-start.8) | collective-permute-done | bytes 524320 | tf_op jit(solution)/shard_map/ppermute | solution.py:38
  56.2 3.1 %collective-permute-start.13 = (bf16[8,768]{1,0:T(8,128)(2,1)S(1)}, bf16[8,768]{1,0:T(8,128)(2,1)S(1)}, u32[]{:S(2)}, u32[]{:S(2)}) collective-permute-start(bf16[8,768]{1,0:T(8,128)(2,1)S(1)} %get-tuple-element.45), channel_id=1, source_target_pairs={{0,1},{1,2},{2,3},{3,4},{4,5},{5,6},{6,7},{7,8},{8,9},{9,10},{10,1... | collective-permute-start | bytes 36872 | tf_op jit(solution)/shard_map/ppermute | solution.py:332
  60.8 5.6 %collective-permute-done.14.after_ref = bf16[8,768]{1,0:T(8,128)(2,1)S(1)} collective-permute-done((bf16[8,768]{1,0:T(8,128)(2,1)S(1)}, bf16[8,768]{1,0:T(8,128)(2,1)S(1)}, u32[]{:S(2)}, u32[]{:S(2)}) %collective-permute-start.14) | collective-permute-done | bytes 12320 | tf_op jit(solution)/shard_map/ppermute | solution.py:333
  68.4 2.7 %collective-permute-start.16 = (bf16[256,768]{1,0:T(8,128)(2,1)S(1)}, bf16[256,768]{1,0:T(8,128)(2,1)}, u32[]{:S(2)}, u32[]{:S(2)}) collective-permute-start(bf16[256,768]{1,0:T(8,128)(2,1)S(1)} %convolve.1.near_ref), channel_id=1, source_target_pairs={{0,4},{1,5},{2,6},{3,7},{4,0},{5,1},{6,2},{7,3},{8,12},{9,13},{10,... | collective-permute-start | bytes 1179656 | tf_op jit(solution)/shard_map/ppermute | solution.py:38
  72.2 3.3 %collective-permute-start.19 = (bf16[256,768]{1,0:T(8,128)(2,1)S(1)}, bf16[256,768]{1,0:T(8,128)(2,1)}, u32[]{:S(2)}, u32[]{:S(2)}) collective-permute-start(bf16[256,768]{1,0:T(8,128)(2,1)S(1)} %convolve.1.near_ref), channel_id=1, source_target_pairs={{0,6},{1,7},{2,0},{3,1},{4,2},{5,3},{6,4},{7,5},{8,14},{9,15},{10,... | collective-permute-start | bytes 1179656 | tf_op jit(solution)/shard_map/ppermute | solution.py:38
  75.5 6.6 %collective-permute-done.16.near_ref = bf16[256,768]{1,0:T(8,128)(2,1)} collective-permute-done((bf16[256,768]{1,0:T(8,128)(2,1)S(1)}, bf16[256,768]{1,0:T(8,128)(2,1)}, u32[]{:S(2)}, u32[]{:S(2)}) %collective-permute-start.16) | collective-permute-done | bytes 393248 | tf_op jit(solution)/shard_map/ppermute | solution.py:38
  82.1 2.7 %collective-permute-start.17 = (bf16[256,768]{1,0:T(8,128)(2,1)}, bf16[256,768]{1,0:T(8,128)(2,1)}, u32[]{:S(2)}, u32[]{:S(2)}) collective-permute-start(bf16[256,768]{1,0:T(8,128)(2,1)} %collective-permute-done.16.near_ref), channel_id=1, source_target_pairs={{0,1},{1,0},{2,3},{3,2},{4,5},{5,4},{6,7},{7,6},{8,9},{9,8},{10,11... | collective-permute-start | bytes 1179656 | tf_op jit(solution)/shard_map/ppermute | solution.py:38
  84.9 4.9 %collective-permute-done.21.near_ref = bf16[256,768]{1,0:T(8,128)(2,1)} collective-permute-done((bf16[256,768]{1,0:T(8,128)(2,1)S(1)}, bf16[256,768]{1,0:T(8,128)(2,1)}, u32[]{:S(2)}, u32[]{:S(2)}) %collective-permute-start.21) | collective-permute-done | bytes 393248 | tf_op jit(solution)/shard_map/ppermute | solution.py:38
  91.4 2.6 %collective-permute-start.20 = (bf16[256,768]{1,0:T(8,128)(2,1)}, bf16[256,768]{1,0:T(8,128)(2,1)S(1)}, u32[]{:S(2)}, u32[]{:S(2)}) collective-permute-start(bf16[256,768]{1,0:T(8,128)(2,1)} %collective-permute-done.19.near_ref), channel_id=1, source_target_pairs={{0,1},{1,0},{2,3},{3,2},{4,5},{5,4},{6,7},{7,6},{8,9},{9,8},{10,11... | collective-permute-start | bytes 1179656 | tf_op jit(solution)/shard_map/ppermute | solution.py:38
  95.3 6.6 %head_pass.4 = (bf16[2048,768]{1,0:T(8,128)(2,1)}, bf16[512,768]{1,0:T(8,128)(2,1)}, f32[768,768]{1,0:T(8,128)S(1)}) custom-call(s32[3]{0:T(128)S(1)} %add_add_fusion.1.at_ref, bf16[256,768]{1,0:T(8,128)(2,1)} %collective-permute-done.16.near_ref, bf16[256,768]{1,0:T(8,128)(2,1)} %collective-permute-done.17.far_ref, bf16[768,768]{1,0:T(8,128)(2,1)S(1)} %copy-done.1, ...), custom_call_target="tpu_custom_call" | custom-call | flops 1811939328 | bytes 6291456 | tf_op jit(solution)/shard_map/head_pass/pallas_call | solution.py:266
  103.5 6.5 %head_pass.5 = (bf16[2048,768]{1,0:T(8,128)(2,1)}, bf16[512,768]{1,0:T(8,128)(2,1)}, f32[768,768]{1,0:T(8,128)S(1)}) custom-call(s32[3]{0:T(128)S(1)} %add_add_fusion.3.at_ref, bf16[256,768]{1,0:T(8,128)(2,1)} %collective-permute-done.21.near_ref, bf16[256,768]{1,0:T(8,128)(2,1)S(1)} %collective-permute-done.22.far_ref, ...), custom_call_target="tpu_custom_call", output_to_operand_aliasing={{0}: (8, {})} | custom-call | flops 1811939328 | bytes 6291456 | tf_op jit(solution)/shard_map/head_pass/pallas_call | solution.py:266
  110.0 3.9 %collective-permute-start.23 = (bf16[512,768]{1,0:T(8,128)(2,1)}, bf16[512,768]{1,0:T(8,128)(2,1)}, u32[]{:S(2)}, u32[]{:S(2)}) collective-permute-start(bf16[512,768]{1,0:T(8,128)(2,1)} %get-tuple-element.59), channel_id=1, source_target_pairs={{0,6},{1,7},{2,0},{3,1},{4,2},{5,3},{6,4},{7,5},{8,14},{9,15},{10,... | collective-permute-start | bytes 2359304 | tf_op jit(solution)/shard_map/ppermute | solution.py:38
  114.0 3.6 %collective-permute-start.15 = (bf16[256,768]{1,0:T(8,128)(2,1)S(1)}, bf16[256,768]{1,0:T(8,128)(2,1)}, u32[]{:S(2)}, u32[]{:S(2)}) collective-permute-start(bf16[256,768]{1,0:T(8,128)(2,1)S(1)} %convolve.1.near_ref), channel_id=1, source_target_pairs={{0,1},{1,0},{2,3},{3,2},{4,5},{5,4},{6,7},{7,6},{8,9},{9,8},{10,11... | collective-permute-start | bytes 1179656 | tf_op jit(solution)/shard_map/ppermute | solution.py:38
  117.6 6.5 %head_pass.6 = (bf16[2048,768]{1,0:T(8,128)(2,1)}, bf16[512,768]{1,0:T(8,128)(2,1)}, f32[768,768]{1,0:T(8,128)S(1)}) custom-call(s32[3]{0:T(128)S(1)} %add_add_fusion.2.at_ref, bf16[256,768]{1,0:T(8,128)(2,1)} %collective-permute-done.19.near_ref, bf16[256,768]{1,0:T(8,128)(2,1)S(1)} %collective-permute-done.20.far_ref, ...), custom_call_target="tpu_custom_call", output_to_operand_aliasing={{0}: (8, {})} | custom-call | flops 1811939328 | bytes 6291456 | tf_op jit(solution)/shard_map/head_pass/pallas_call | solution.py:266
  128.9 6.4 %head_pass.7 = (bf16[2048,768]{1,0:T(8,128)(2,1)}, bf16[512,768]{1,0:T(8,128)(2,1)S(1)}, f32[384,768]{1,0:T(8,128)S(1)}, bf16[384,768]{1,0:T(8,128)(2,1)S(1)}) custom-call(s32[3]{0:T(128)S(1)} %add_add_fusion.at_ref, bf16[256,768]{1,0:T(8,128)(2,1)S(1)} %convolve.1.near_ref, ...), custom_call_target="tpu_custom_call", output_to_operand_aliasing={{0}: (8, {})} | custom-call | flops 1811939328 | bytes 6291456 | tf_op jit(solution)/shard_map/head_pass/pallas_call | solution.py:266
  135.4 6.6 %collective-permute-done.23 = bf16[512,768]{1,0:T(8,128)(2,1)} collective-permute-done((bf16[512,768]{1,0:T(8,128)(2,1)}, bf16[512,768]{1,0:T(8,128)(2,1)}, u32[]{:S(2)}, u32[]{:S(2)}) %collective-permute-start.23) | collective-permute-done | bytes 786464 | tf_op jit(solution)/shard_map/ppermute | solution.py:38
  142.0 3.0 %collective-permute-done.25 = bf16[512,768]{1,0:T(8,128)(2,1)} collective-permute-done((bf16[512,768]{1,0:T(8,128)(2,1)}, bf16[512,768]{1,0:T(8,128)(2,1)}, u32[]{:S(2)}, u32[]{:S(2)}) %collective-permute-start.25) | collective-permute-done | bytes 786464 | tf_op jit(solution)/shard_map/ppermute | solution.py:38
  148.7 4.2 %all-to-all-start = ((bf16[8,48,768]{2,1,0:T(8,128)(2,1)}), bf16[8,48,768]{2,1,0:T(8,128)(2,1)}, u32[]{:S(2)}, u32[]{:S(2)}) async-start(bf16[8,48,768]{2,1,0:T(8,128)(2,1)} %bitcast.12), calls=%async_computation | async-start | bytes 1179648 | tf_op jit(solution)/shard_map/all_to_all | solution.py:376
  152.9 8.4 %collective-permute-done.26 = bf16[256,768]{1,0:T(8,128)(2,1)} collective-permute-done((bf16[256,768]{1,0:T(8,128)(2,1)S(1)}, bf16[256,768]{1,0:T(8,128)(2,1)}, u32[]{:S(2)}, u32[]{:S(2)}) %collective-permute-start.26) | collective-permute-done | bytes 393248 | tf_op jit(solution)/shard_map/ppermute | solution.py:38
  (103 shorter events, 48.9 us)
Async XLA Ops:
  3.5 6.1 %collective-permute-start = (bf16[64,256]{1,0:T(8,128)(2,1)S(1)}, bf16[64,256]{1,0:T(8,128)(2,1)S(1)}, u32[]{:S(2)}, u32[]{:S(2)}) collective-permute-start(bf16[64,256]{1,0:T(8,128)(2,1)S(1)} %convolution_convert_fusion.1.refs_0_), channel_id=1, source_target_pairs={{0,64},{1,65},{2,66},{3,67},{4,68},{5,69},{6,70},{7,71},{8,72},{9,... | collective-permute-start | bytes 98312 | tf_op jit(solution)/shard_map/ppermute | solution.py:38
  13.2 7.7 %collective-permute-start.3 = (bf16[256,256]{1,0:T(8,128)(2,1)S(1)}, bf16[256,256]{1,0:T(8,128)(2,1)S(1)}, u32[]{:S(2)}, u32[]{:S(2)}) collective-permute-start(bf16[256,256]{1,0:T(8,128)(2,1)S(1)} %join.2.refs_0_), channel_id=1, source_target_pairs={{0,2},{1,3},{2,4},{3,5},{4,6},{5,7},{6,0},{7,1},{8,10},{9,11},{10,... | collective-permute-start | bytes 393224 | tf_op jit(solution)/shard_map/ppermute | solution.py:38
  14.8 6.0 %collective-permute-start.4 = (bf16[256,256]{1,0:T(8,128)(2,1)S(1)}, bf16[256,256]{1,0:T(8,128)(2,1)S(1)}, u32[]{:S(2)}, u32[]{:S(2)}) collective-permute-start(bf16[256,256]{1,0:T(8,128)(2,1)S(1)} %join.2.refs_0_), channel_id=1, source_target_pairs={{0,6},{1,7},{2,0},{3,1},{4,2},{5,3},{6,4},{7,5},{8,14},{9,15},{10,... | collective-permute-start | bytes 393224 | tf_op jit(solution)/shard_map/ppermute | solution.py:38
  16.5 6.5 %collective-permute-start.5 = (bf16[256,256]{1,0:T(8,128)(2,1)S(1)}, bf16[256,256]{1,0:T(8,128)(2,1)S(1)}, u32[]{:S(2)}, u32[]{:S(2)}) collective-permute-start(bf16[256,256]{1,0:T(8,128)(2,1)S(1)} %join.2.refs_0_), channel_id=1, source_target_pairs={{0,4},{1,5},{2,6},{3,7},{4,0},{5,1},{6,2},{7,3},{8,12},{9,13},{10,... | collective-permute-start | bytes 393224 | tf_op jit(solution)/shard_map/ppermute | solution.py:38
  23.0 15.2 %collective-permute-start.10 = (bf16[1024,256]{1,0:T(8,128)(2,1)S(1)}, bf16[1024,256]{1,0:T(8,128)(2,1)S(1)}, u32[]{:S(2)}, u32[]{:S(2)}) collective-permute-start(bf16[1024,256]{1,0:T(8,128)(2,1)S(1)} %join.3.refs_1_), channel_id=1, source_target_pairs={{0,16},{1,17},{2,18},{3,19},{4,20},{5,21},{6,22},{7,23},{8,24},{9,... | collective-permute-start | bytes 1572872 | tf_op jit(solution)/shard_map/ppermute | solution.py:38
  24.5 21.7 %collective-permute-start.8 = (bf16[1024,256]{1,0:T(8,128)(2,1)S(1)}, bf16[1024,256]{1,0:T(8,128)(2,1)S(1)}, u32[]{:S(2)}, u32[]{:S(2)}) collective-permute-start(bf16[1024,256]{1,0:T(8,128)(2,1)S(1)} %join.3.refs_1_), channel_id=1, source_target_pairs={{0,48},{1,49},{2,50},{3,51},{4,52},{5,53},{6,54},{7,55},{8,56},{9,... | collective-permute-start | bytes 1572872 | tf_op jit(solution)/shard_map/ppermute | solution.py:38
  26.3 21.6 %collective-permute-start.6 = (bf16[1024,256]{1,0:T(8,128)(2,1)S(1)}, bf16[1024,256]{1,0:T(8,128)(2,1)S(1)}, u32[]{:S(2)}, u32[]{:S(2)}) collective-permute-start(bf16[1024,256]{1,0:T(8,128)(2,1)S(1)} %join.3.refs_1_), channel_id=1, source_target_pairs={{0,32},{1,33},{2,34},{3,35},{4,36},{5,37},{6,38},{7,39},{8,40},{9,... | collective-permute-start | bytes 1572872 | tf_op jit(solution)/shard_map/ppermute | solution.py:38
  28.1 21.5 %collective-permute-start.12 = (bf16[1024,256]{1,0:T(8,128)(2,1)S(1)}, bf16[1024,256]{1,0:T(8,128)(2,1)S(1)}, u32[]{:S(2)}, u32[]{:S(2)}) collective-permute-start(bf16[1024,256]{1,0:T(8,128)(2,1)S(1)} %join.3.refs_1_), channel_id=1, source_target_pairs={{0,8},{1,9},{2,10},{3,11},{4,12},{5,13},{6,14},{7,15},{8,0},{9,1},... | collective-permute-start | bytes 1572872 | tf_op jit(solution)/shard_map/ppermute | solution.py:38
  38.1 12.9 %collective-permute-start.11 = (bf16[1024,256]{1,0:T(8,128)(2,1)S(1)}, bf16[1024,256]{1,0:T(8,128)(2,1)S(1)}, u32[]{:S(2)}, u32[]{:S(2)}) collective-permute-start(bf16[1024,256]{1,0:T(8,128)(2,1)S(1)} %collective-permute-done.10.refs_2_), channel_id=1, source_target_pairs={{0,8},{1,9},{2,10},{3,11},{4,12},{5,13},{6,14},{7,15},{8,0},{9,1},... | collective-permute-start | bytes 1572872 | tf_op jit(solution)/shard_map/ppermute | solution.py:38
  46.2 6.2 %collective-permute-start.9 = (bf16[1024,256]{1,0:T(8,128)(2,1)S(1)}, bf16[1024,256]{1,0:T(8,128)(2,1)S(1)}, u32[]{:S(2)}, u32[]{:S(2)}) collective-permute-start(bf16[1024,256]{1,0:T(8,128)(2,1)S(1)} %collective-permute-done.8.refs_2_), channel_id=1, source_target_pairs={{0,8},{1,9},{2,10},{3,11},{4,12},{5,13},{6,14},{7,15},{8,0},{9,1},... | collective-permute-start | bytes 1572872 | tf_op jit(solution)/shard_map/ppermute | solution.py:38
  47.9 5.9 %collective-permute-start.7 = (bf16[1024,256]{1,0:T(8,128)(2,1)S(1)}, bf16[1024,256]{1,0:T(8,128)(2,1)S(1)}, u32[]{:S(2)}, u32[]{:S(2)}) collective-permute-start(bf16[1024,256]{1,0:T(8,128)(2,1)S(1)} %collective-permute-done.6.refs_2_), channel_id=1, source_target_pairs={{0,8},{1,9},{2,10},{3,11},{4,12},{5,13},{6,14},{7,15},{8,0},{9,1},... | collective-permute-start | bytes 1572872 | tf_op jit(solution)/shard_map/ppermute | solution.py:38
  59.3 7.1 %collective-permute-start.14 = (bf16[8,768]{1,0:T(8,128)(2,1)S(1)}, bf16[8,768]{1,0:T(8,128)(2,1)S(1)}, u32[]{:S(2)}, u32[]{:S(2)}) collective-permute-start(bf16[8,768]{1,0:T(8,128)(2,1)S(1)} %get-tuple-element.46), channel_id=1, source_target_pairs={{1,0},{2,1},{3,2},{4,3},{5,4},{6,5},{7,6},{8,7},{9,8},{10,9},{11,1... | collective-permute-start | bytes 36872 | tf_op jit(solution)/shard_map/ppermute | solution.py:333
  68.4 13.7 %collective-permute-start.16 = (bf16[256,768]{1,0:T(8,128)(2,1)S(1)}, bf16[256,768]{1,0:T(8,128)(2,1)}, u32[]{:S(2)}, u32[]{:S(2)}) collective-permute-start(bf16[256,768]{1,0:T(8,128)(2,1)S(1)} %convolve.1.near_ref), channel_id=1, source_target_pairs={{0,4},{1,5},{2,6},{3,7},{4,0},{5,1},{6,2},{7,3},{8,12},{9,13},{10,... | collective-permute-start | bytes 1179656 | tf_op jit(solution)/shard_map/ppermute | solution.py:38
  71.3 18.5 %collective-permute-start.21 = (bf16[256,768]{1,0:T(8,128)(2,1)S(1)}, bf16[256,768]{1,0:T(8,128)(2,1)}, u32[]{:S(2)}, u32[]{:S(2)}) collective-permute-start(bf16[256,768]{1,0:T(8,128)(2,1)S(1)} %convolve.1.near_ref), channel_id=1, source_target_pairs={{0,2},{1,3},{2,4},{3,5},{4,6},{5,7},{6,0},{7,1},{8,10},{9,11},{10,... | collective-permute-start | bytes 1179656 | tf_op jit(solution)/shard_map/ppermute | solution.py:38
  72.2 19.2 %collective-permute-start.19 = (bf16[256,768]{1,0:T(8,128)(2,1)S(1)}, bf16[256,768]{1,0:T(8,128)(2,1)}, u32[]{:S(2)}, u32[]{:S(2)}) collective-permute-start(bf16[256,768]{1,0:T(8,128)(2,1)S(1)} %convolve.1.near_ref), channel_id=1, source_target_pairs={{0,6},{1,7},{2,0},{3,1},{4,2},{5,3},{6,4},{7,5},{8,14},{9,15},{10,... | collective-permute-start | bytes 1179656 | tf_op jit(solution)/shard_map/ppermute | solution.py:38
  82.1 12.0 %collective-permute-start.17 = (bf16[256,768]{1,0:T(8,128)(2,1)}, bf16[256,768]{1,0:T(8,128)(2,1)}, u32[]{:S(2)}, u32[]{:S(2)}) collective-permute-start(bf16[256,768]{1,0:T(8,128)(2,1)} %collective-permute-done.16.near_ref), channel_id=1, source_target_pairs={{0,1},{1,0},{2,3},{3,2},{4,5},{5,4},{6,7},{7,6},{8,9},{9,8},{10,11... | collective-permute-start | bytes 1179656 | tf_op jit(solution)/shard_map/ppermute | solution.py:38
  89.8 13.7 %collective-permute-start.22 = (bf16[256,768]{1,0:T(8,128)(2,1)}, bf16[256,768]{1,0:T(8,128)(2,1)S(1)}, u32[]{:S(2)}, u32[]{:S(2)}) collective-permute-start(bf16[256,768]{1,0:T(8,128)(2,1)} %collective-permute-done.21.near_ref), channel_id=1, source_target_pairs={{0,1},{1,0},{2,3},{3,2},{4,5},{5,4},{6,7},{7,6},{8,9},{9,8},{10,11... | collective-permute-start | bytes 1179656 | tf_op jit(solution)/shard_map/ppermute | solution.py:38
  91.4 26.2 %collective-permute-start.20 = (bf16[256,768]{1,0:T(8,128)(2,1)}, bf16[256,768]{1,0:T(8,128)(2,1)S(1)}, u32[]{:S(2)}, u32[]{:S(2)}) collective-permute-start(bf16[256,768]{1,0:T(8,128)(2,1)} %collective-permute-done.19.near_ref), channel_id=1, source_target_pairs={{0,1},{1,0},{2,3},{3,2},{4,5},{5,4},{6,7},{7,6},{8,9},{9,8},{10,11... | collective-permute-start | bytes 1179656 | tf_op jit(solution)/shard_map/ppermute | solution.py:38
  101.9 24.1 %collective-permute-start.18 = (bf16[512,768]{1,0:T(8,128)(2,1)}, bf16[512,768]{1,0:T(8,128)(2,1)}, u32[]{:S(2)}, u32[]{:S(2)}) collective-permute-start(bf16[512,768]{1,0:T(8,128)(2,1)} %get-tuple-element.47), channel_id=1, source_target_pairs={{0,4},{1,5},{2,6},{3,7},{4,0},{5,1},{6,2},{7,3},{8,12},{9,13},{10,... | collective-permute-start | bytes 2359304 | tf_op jit(solution)/shard_map/ppermute | solution.py:38
  110.0 32.0 %collective-permute-start.23 = (bf16[512,768]{1,0:T(8,128)(2,1)}, bf16[512,768]{1,0:T(8,128)(2,1)}, u32[]{:S(2)}, u32[]{:S(2)}) collective-permute-start(bf16[512,768]{1,0:T(8,128)(2,1)} %get-tuple-element.59), channel_id=1, source_target_pairs={{0,6},{1,7},{2,0},{3,1},{4,2},{5,3},{6,4},{7,5},{8,14},{9,15},{10,... | collective-permute-start | bytes 2359304 | tf_op jit(solution)/shard_map/ppermute | solution.py:38
  114.0 12.0 %collective-permute-start.15 = (bf16[256,768]{1,0:T(8,128)(2,1)S(1)}, bf16[256,768]{1,0:T(8,128)(2,1)}, u32[]{:S(2)}, u32[]{:S(2)}) collective-permute-start(bf16[256,768]{1,0:T(8,128)(2,1)S(1)} %convolve.1.near_ref), channel_id=1, source_target_pairs={{0,1},{1,0},{2,3},{3,2},{4,5},{5,4},{6,7},{7,6},{8,9},{9,8},{10,11... | collective-permute-start | bytes 1179656 | tf_op jit(solution)/shard_map/ppermute | solution.py:38
  125.6 19.4 %collective-permute-start.25 = (bf16[512,768]{1,0:T(8,128)(2,1)}, bf16[512,768]{1,0:T(8,128)(2,1)}, u32[]{:S(2)}, u32[]{:S(2)}) collective-permute-start(bf16[512,768]{1,0:T(8,128)(2,1)} %get-tuple-element.63), channel_id=1, source_target_pairs={{0,2},{1,3},{2,4},{3,5},{4,6},{5,7},{6,0},{7,1},{8,10},{9,11},{10,... | collective-permute-start | bytes 2359304 | tf_op jit(solution)/shard_map/ppermute | solution.py:38
  147.1 14.2 %collective-permute-start.26 = (bf16[256,768]{1,0:T(8,128)(2,1)S(1)}, bf16[256,768]{1,0:T(8,128)(2,1)}, u32[]{:S(2)}, u32[]{:S(2)}) collective-permute-start(bf16[256,768]{1,0:T(8,128)(2,1)S(1)} %slice.15), channel_id=1, source_target_pairs={{0,1},{1,0},{2,3},{3,2},{4,5},{5,4},{6,7},{7,6},{8,9},{9,8},{10,11... | collective-permute-start | bytes 1179656 | tf_op jit(solution)/shard_map/ppermute | solution.py:38
  148.7 15.1 %all-to-all-start = ((bf16[8,48,768]{2,1,0:T(8,128)(2,1)}), bf16[8,48,768]{2,1,0:T(8,128)(2,1)}, u32[]{:S(2)}, u32[]{:S(2)}) async-start(bf16[8,48,768]{2,1,0:T(8,128)(2,1)} %bitcast.12), calls=%async_computation | async-start | bytes 1179648 | tf_op jit(solution)/shard_map/all_to_all | solution.py:376
  (22 other events, 261.5 us)

commit v5 on v4

v5 whole, which is shorter than its diff:
```python
import functools
import math

import jax
import jax.numpy as jnp
import numpy as np
from jax import lax
from jax.experimental import pallas as pl
from jax.experimental.pallas import tpu as pltpu
from jax.sharding import Mesh, PartitionSpec as P

logit_cap = 20.0
ORDER = ((2,), (1,), (3,), (0,))
BIN = ("bz", "core")
TRK = ("y", "zh")
ALL = BIN + TRK


def place(index):
    bz, rest = divmod(index, 16)
    core, rest = divmod(rest, 8)
    y, zh = divmod(rest, 2)
    zlo, x = divmod(bz, 4)
    return (x, y, zh * 2 + zlo, core)


def number(x, y, z, core):
    zh, zlo = divmod(z, 2)
    return ((zlo * 4 + x) * 2 + core) * 8 + y * 2 + zh


def moved(value, dim, step):
    sizes = (4, 4, 4, 2)
    pairs = []
    for index in range(128):
        target = list(place(index))
        target[dim] = (target[dim] + step) % sizes[dim]
        pairs.append((index, number(*target)))
    return lax.ppermute(value, ALL, pairs)


def whole(array):
    return pl.BlockSpec(array.shape, lambda *_: (0,) * array.ndim, pipeline_mode=pl.Buffered(1))


def join_kernel(*refs):
    out = refs[-1]
    rows = refs[0].shape[0]
    for index, ref in enumerate(refs[:-1]):
        out[index * rows : (index + 1) * rows, :] = ref[...]


def join(*pieces):
    rows, columns = pieces[0].shape
    out = jax.ShapeDtypeStruct((len(pieces) * rows, columns), pieces[0].dtype)
    return pl.pallas_call(
        join_kernel,
        in_specs=[pl.BlockSpec(memory_space=pltpu.VMEM)] * len(pieces),
        out_specs=pl.BlockSpec(memory_space=pltpu.VMEM),
        out_shape=out,
        cost_estimate=pl.CostEstimate(flops=0, transcendentals=0, bytes_accessed=4 * out.size),
        compiler_params=pltpu.CompilerParams(vmem_limit_bytes=4 << 20),
        name="join",
    )(*pieces)


def normalized(value, gain):
    widened = value.astype(jnp.float32)
    meansq = jnp.mean(widened * widened, axis=1, keepdims=True)
    return (widened * lax.rsqrt(meansq + 1e-06) * gain).astype(jnp.bfloat16)


def start_kernel(trunk_ref, gain_ref, kv_ref, skip_ref, keyvals_ref, next_ref, prev_ref, tall):
    f32, bf16 = jnp.float32, jnp.bfloat16
    normed = normalized(trunk_ref[...], gain_ref[...])
    keyvals_ref[...] = jnp.dot(normed, kv_ref[...], preferred_element_type=f32).astype(bf16)
    rows, width = trunk_ref.shape
    positions, channels = skip_ref.shape
    count = width // channels
    widened = trunk_ref[...].astype(f32)
    for out, row, near in ((next_ref, rows - 1, positions - 8), (prev_ref, 0, 0)):
        tall[...] = skip_ref[near : near + 8, :].astype(f32)
        rim = tall[6:8, :] if row else tall[0:2, :]
        tall[count : count + 2, :] = rim
        for piece in range(count):
            tall[piece : piece + 1, :] = widened[
                row : row + 1, piece * channels : (piece + 1) * channels
            ]
        out[...] = tall[...].astype(bf16)


def start(trunk, gain, w_kv, skip):
    vmem = pl.BlockSpec(memory_space=pltpu.VMEM)
    edge = jax.ShapeDtypeStruct((8, skip.shape[1]), jnp.bfloat16)
    return pl.pallas_call(
        start_kernel,
        grid=(1,),
        in_specs=[whole(operand) for operand in (trunk, gain, w_kv, skip)],
        out_specs=[vmem] * 3,
        out_shape=[jax.ShapeDtypeStruct((trunk.shape[0], w_kv.shape[1]), jnp.bfloat16), edge, edge],
        scratch_shapes=[pltpu.VMEM(edge.shape, jnp.float32)],
        cost_estimate=pl.CostEstimate(
            flops=2 * trunk.shape[0] * w_kv.size, transcendentals=64, bytes_accessed=2 * w_kv.size
        ),
        compiler_params=pltpu.CompilerParams(vmem_limit_bytes=6 << 20),
        name="start",
    )(trunk, gain, w_kv, skip)


def query_kernel(trunk_ref, gain_ref, before_ref, after_ref, w_ref, queries_ref, rims_ref, tall):
    f32, bf16 = jnp.float32, jnp.bfloat16
    rows, width = trunk_ref.shape
    channels, head_dim = before_ref.shape[1], rims_ref.shape[1]
    sides = [
        jnp.concatenate(
            [ref[piece : piece + 1, :].astype(f32) for piece in range(width // channels)], 1
        )
        for ref in (before_ref, after_ref)
    ]
    every = jnp.concatenate(
        [trunk_ref[...].astype(f32)] + sides + [jnp.zeros((14, width), f32)], 0
    )
    normed = normalized(every, gain_ref[...])
    projected = jnp.dot(normed, w_ref[...], preferred_element_type=f32)
    queries_ref[...] = projected[:rows].astype(bf16)
    for head in range(projected.shape[1] // head_dim):
        tall[2 * head : 2 * head + 2, :] = projected[
            rows : rows + 2, head * head_dim : (head + 1) * head_dim
        ]
    rims_ref[...] = tall[...].astype(bf16)


def query(trunk, gain, before, after, w_query, head_dim):
    vmem = pl.BlockSpec(memory_space=pltpu.VMEM)
    rims = (2 * w_query.shape[1] // head_dim, head_dim)
    return pl.pallas_call(
        query_kernel,
        in_specs=[vmem] * 5,
        out_specs=[vmem] * 2,
        out_shape=[
            jax.ShapeDtypeStruct((trunk.shape[0], w_query.shape[1]), jnp.bfloat16),
            jax.ShapeDtypeStruct(rims, jnp.bfloat16),
        ],
        scratch_shapes=[pltpu.VMEM(rims, jnp.float32)],
        cost_estimate=pl.CostEstimate(
            flops=2 * trunk.shape[0] * w_query.size,
            transcendentals=64,
            bytes_accessed=2 * w_query.size,
        ),
        compiler_params=pltpu.CompilerParams(vmem_limit_bytes=8 << 20),
        name="query",
    )(trunk, gain, before, after, w_query)


def attend_kernel(head_dim, first, *refs):
    q_ref, rim_ref, refs = refs[0], refs[1], refs[2:]
    num_ref, den_ref = refs[-2:]
    pieces = refs[:-2] if first else refs[:-4]
    f32, bf16 = jnp.float32, jnp.bfloat16
    heads = q_ref.shape[1] // head_dim
    queries = jnp.concatenate(
        [q_ref[:, h * head_dim : (h + 1) * head_dim] for h in range(heads)] + [rim_ref[...]], 0
    )
    inner = 1.0 / (math.sqrt(head_dim) * logit_cap)
    outer = logit_cap * math.log2(math.e)
    num = jnp.zeros(num_ref.shape, f32) if first else refs[-4][...]
    den = jnp.zeros(den_ref.shape, f32) if first else refs[-3][...]
    step = 256
    for piece in pieces:
        for start in range(0, piece.shape[0], step):
            keys = piece[start : start + step, :head_dim]
            values = piece[start : start + step, head_dim:]
            scores = lax.dot_general(
                queries, keys, (((1,), (1,)), ((), ())), preferred_element_type=f32
            )
            weights = jnp.exp2(outer * jnp.tanh(scores * inner))
            num = num + jnp.dot(weights.astype(bf16), values, preferred_element_type=f32)
            for lane in range(0, step, 128):
                den = den + weights[:, lane : lane + 128]
    num_ref[...] = num
    den_ref[...] = den


def attend(state, queries, pieces, head_dim):
    rows = queries[0].size // head_dim + queries[1].shape[0]
    operands = [*queries, *pieces, *(state or ())]
    keys = sum(piece.shape[0] for piece in pieces)
    return pl.pallas_call(
        functools.partial(attend_kernel, head_dim, state is None),
        grid=(1,),
        in_specs=[whole(operand) for operand in operands],
        out_specs=[pl.BlockSpec((rows, head_dim), lambda i: (0, 0))] * 2,
        out_shape=[jax.ShapeDtypeStruct((rows, head_dim), jnp.float32)] * 2,
        cost_estimate=pl.CostEstimate(
            flops=8 * rows * keys * head_dim,
            transcendentals=2 * rows * keys,
            bytes_accessed=1 << 20,
        ),
        compiler_params=pltpu.CompilerParams(vmem_limit_bytes=8 << 20),
        name="attend",
    )(*operands)


def finish_kernel(
    at_ref, num_ref, den_ref, trunk_ref, before_ref, after_ref, out_ref, up_ref, skip_ref, conv_ref,
    feature_ref, ratio, near,
):
    f32, bf16 = jnp.float32, jnp.bfloat16
    rows, positions = trunk_ref.shape[0], skip_ref.shape[0]
    width, channels = trunk_ref.shape[1], skip_ref.shape[1]
    taps = conv_ref.shape[0]
    rim = taps // 2
    ratio[...] = num_ref[...] / jnp.sum(den_ref[...], axis=1, keepdims=True)
    heads = (ratio.shape[0] - 16) // rows
    attended = jnp.concatenate([ratio[h * rows : (h + 1) * rows, :] for h in range(heads)], 1)
    edge = jnp.concatenate(
        [ratio[heads * rows + 2 * h : heads * rows + 2 * h + 2, :] for h in range(heads)], 1
    )
    edge = jnp.concatenate([edge, jnp.zeros((14, edge.shape[1]), f32)], 0)
    attended = jnp.concatenate([attended.astype(bf16), edge.astype(bf16)], 0)
    sides = [
        jnp.concatenate(
            [ref[piece : piece + 1, :] for piece in range(width // channels)], 1
        ).astype(f32)
        for ref in (before_ref, after_ref)
    ]
    residual = jnp.concatenate(
        [trunk_ref[...].astype(f32)] + sides + [jnp.zeros((14, width), f32)], 0
    )
    hidden = (residual + jnp.dot(attended, out_ref[...], preferred_element_type=f32)).astype(bf16)
    upward = jnp.dot(hidden, up_ref[...], preferred_element_type=f32)
    factor = positions // rows
    for row in range(rows):
        begin = 8 + row * factor
        near[begin : begin + factor, :] = jnp.broadcast_to(
            upward[row : row + 1, :], (factor, channels)
        )
    inside = near[8 : 8 + positions, :] + skip_ref[...].astype(f32)
    near[8 : 8 + positions, :] = inside.astype(bf16).astype(f32)
    for index, (ref, begin) in enumerate(((before_ref, 8 - rim), (after_ref, 8 + positions))):
        tall = upward[rows + index : rows + index + 1, :] + ref[rim : 2 * rim, :].astype(f32)
        tall = tall.astype(bf16).astype(f32)
        near[begin : begin + rim, :] = jnp.where(at_ref[index] > 0, tall, 0.0)
    conved = jnp.zeros((positions, channels), f32)
    for tap in range(taps):
        begin = 8 - rim + tap
        conved = conved + jnp.dot(
            near[begin : begin + positions, :].astype(bf16),
            conv_ref[tap],
            preferred_element_type=f32,
        )
    cubic = math.sqrt(2.0 / math.pi) * (conved + 0.044715 * (conved * conved * conved))
    center = near[8 : 8 + positions, :]
    feature_ref[...] = (center + 0.5 * conved * (1.0 + jnp.tanh(cubic))).astype(bf16)


def finish(at, state, trunk, before, after, w_out, w_up, skip, conv_w):
    operands = (*state, trunk, before, after, w_out, w_up, skip, conv_w)
    vmem = pl.BlockSpec(memory_space=pltpu.VMEM)
    return pl.pallas_call(
        finish_kernel,
        in_specs=[pl.BlockSpec(memory_space=pltpu.SMEM)] + [vmem] * len(operands),
        out_specs=vmem,
        out_shape=jax.ShapeDtypeStruct(skip.shape, jnp.bfloat16),
        scratch_shapes=[
            pltpu.VMEM(state[0].shape, jnp.float32),
            pltpu.VMEM((skip.shape[0] + 16, skip.shape[1]), jnp.float32),
        ],
        cost_estimate=pl.CostEstimate(
            flops=2 * trunk.shape[0] * (w_out.size + w_up.size) + 2 * skip.shape[0] * conv_w.size,
            transcendentals=skip.size,
            bytes_accessed=2 * (w_out.size + w_up.size + conv_w.size),
        ),
        compiler_params=pltpu.CompilerParams(vmem_limit_bytes=14 << 20),
        name="finish",
    )(at, *operands)


def head_kernel(
    groups, first, last, positions, at_ref, *refs,
):
    f32, bf16 = jnp.float32, jnp.bfloat16
    halves, refs = refs[: 2 * groups], refs[2 * groups :]
    head_ref, bias_ref, scale_ref, keep_ref, target_ref = refs[:5]
    refs = refs[5:]
    if not first:
        old_ref, refs = refs[1], refs[2:]
    pred_ref, partials, sums = refs[0], refs[1 : 1 + groups], refs[1 + groups :]
    total_ref = sums[-1]
    step = pl.program_id(0)
    rows, channels = partials[0].shape
    bins = keep_ref.shape[2]
    factor = rows // bins
    row = lax.broadcasted_iota(jnp.int32, (rows, bins), 0)
    col = lax.broadcasted_iota(jnp.int32, (rows, bins), 1) * factor
    spread = jnp.where((row >= col) & (row < col + factor), 1.0, 0.0).astype(bf16)
    keep = lax.dot_general(
        spread,
        jnp.broadcast_to(keep_ref[0].astype(bf16), (8, bins)),
        (((1,), (1,)), ((), ())),
        preferred_element_type=f32,
    )[:, :1]
    feature = halves[-1][...]
    for index in range(len(halves) - 1):
        feature = jnp.where(step == index, halves[index][...], feature)
    logits = jnp.dot(feature, head_ref[...], preferred_element_type=f32) + bias_ref[...]
    decay = jnp.exp(-jnp.abs(logits))
    smooth = jnp.maximum(logits, 0.0) + jnp.log1p(decay)
    sigmoid = jnp.where(logits >= 0.0, 1.0, decay) / (1.0 + decay)
    pred_ref[...] = smooth.astype(bf16)
    misfit = smooth - target_ref[...].astype(f32)
    slope = (keep * scale_ref[...] * misfit * sigmoid).astype(bf16)
    partial = lax.dot_general(
        slope, head_ref[...], (((1,), (1,)), ((), ())), preferred_element_type=f32
    ).astype(bf16)
    for group in range(groups):

        @pl.when(lax.div(step, 2) == group)
        def _(group=group):
            partials[group][...] = partial

    product = lax.dot_general(
        feature, slope, (((0,), (0,)), ((), ())), preferred_element_type=f32
    )

    @pl.when(step == 0)
    def _():
        total_ref[...] = product if first else product + old_ref[...]

    @pl.when(step > 0)
    def _():
        total_ref[...] += product

    @pl.when(step == 2 * groups - 1)
    def _():
        if not last:
            return
        mine_ref, theirs_ref = sums[:2]
        core, height = at_ref[0], channels // 16
        for pair in range(8):
            at = pl.multiple_of((2 * pair + core) * height, height)
            other = pl.multiple_of((2 * pair + 1 - core) * height, height)
            into = slice(pair * height, (pair + 1) * height)
            mine_ref[into, :] = total_ref[pl.ds(at, height), :] / positions
            theirs_ref[into, :] = (total_ref[pl.ds(other, height), :] / positions).astype(bf16)


def head_pass(groups, at, carried, feature, head_w, bias, scale, keep, targets, last, positions):
    f32, bf16 = jnp.float32, jnp.bfloat16
    count, tracks = targets.shape
    channels = head_w.shape[0]
    rows = count // 8
    first = carried is None

    def segment(i, at):
        return at[2 + i // 2] * 2 + jnp.abs(at[1] - i % 2)

    by_rows = pl.BlockSpec((rows, tracks), lambda i, at: (segment(i, at), 0))
    by_group = [
        pl.BlockSpec((rows, channels), lambda i, at, g=g: (jnp.clip(i - 2 * g, 0, 1), 0))
        for g in range(groups)
    ]
    vmem = pl.BlockSpec(memory_space=pltpu.VMEM)
    totals = jax.ShapeDtypeStruct((channels, tracks), f32)
    half = (channels // 2, tracks)
    sums = [jax.ShapeDtypeStruct(half, f32), jax.ShapeDtypeStruct(half, bf16)] if last else [totals]
    return pl.pallas_call(
        functools.partial(head_kernel, groups, first, last, positions),
        grid_spec=pltpu.PrefetchScalarGridSpec(
            num_scalar_prefetch=1,
            grid=(2 * groups,),
            in_specs=[vmem] * (2 * groups + 3)
            + [pl.BlockSpec((1,) + keep.shape[1:], lambda i, at: (segment(i, at), 0, 0)), by_rows]
            + ([] if first else [pl.BlockSpec(memory_space=pl.ANY), vmem]),
            out_specs=[by_rows] + by_group + [vmem] * len(sums),
            scratch_shapes=[pltpu.VMEM((channels, tracks), f32)] if last else [],
        ),
        out_shape=[
            pltpu.HBM((count, tracks), bf16),
            *[jax.ShapeDtypeStruct((2 * rows, channels), bf16)] * groups,
            *sums,
        ],
        input_output_aliases={} if first else {6 + 2 * groups: 0},
        cost_estimate=pl.CostEstimate(
            flops=12 * groups * rows * head_w.size,
            transcendentals=8 * groups * rows * tracks,
            bytes_accessed=6 << 20,
        ),
        compiler_params=pltpu.CompilerParams(vmem_limit_bytes=16 << 20),
        name="head_pass",
    )(at, *feature, head_w, bias, scale, keep, targets, *(carried or ()))


def body(
    trunk,
    norm_gain,
    w_query,
    w_kv,
    w_out,
    w_up,
    skip,
    conv_w,
    head_w,
    head_bias,
    targets,
    missing,
    group_ids,
    group_weight,
):
    f32, bf16 = jnp.float32, jnp.bfloat16
    row_count = trunk.shape[0]
    head_dim = w_kv.shape[1] // 2
    head_count = w_query.shape[1] // head_dim
    n_all, index = lax.axis_size(ALL), lax.axis_index(ALL)
    channels = conv_w.shape[1]
    gain = norm_gain[None, :]
    keyvals, to_next, to_prev = start(
        *[pltpu.with_memory_space_constraint(value, pltpu.HBM) for value in (trunk, gain, w_kv, skip)]
    )
    nexts = [(i, i + 1) for i in range(n_all - 1)]
    keyvals = join(keyvals, *[moved(keyvals, 2, step) for step in (1, 3, 2)])
    before = lax.ppermute(to_next, ALL, nexts)
    after = lax.ppermute(to_prev, ALL, [(j, i) for i, j in nexts])
    keyvals = join(keyvals, *[moved(keyvals, 1, step) for step in (1, 3, 2)])
    crossed = moved(keyvals, 3, 1)
    pieces = [moved(keyvals, 0, step) for step in (1, 3, 2)]
    pieces[0], before, after = lax.optimization_barrier((pieces[0], before, after))
    queries = query(trunk, gain, before, after, w_query, head_dim)
    pieces[1], queries = lax.optimization_barrier((pieces[1], queries))
    state = attend(None, queries, [keyvals], head_dim)
    for piece in pieces:
        state = attend(state, queries, [crossed, piece], head_dim)
        crossed = moved(piece, 3, 1)
    state = attend(state, queries, [crossed], head_dim)
    at = jnp.stack([index, n_all - 1 - index]).astype(jnp.int32)
    feature = finish(at, state, trunk, before, after, w_out, w_up, skip, conv_w)
    pos_count = targets.shape[0]
    n_bin = lax.axis_size(BIN)
    features = {0: (feature, moved(feature, 2, 2))}
    for step in (2, 1, 3):
        near = moved(feature, 1, step)
        features[step] = (near, moved(near, 2, 2))
    y, zh, core = lax.axis_index("y"), lax.axis_index("zh"), lax.axis_index("core")
    tile_width = head_w.shape[1]
    groups = group_weight.shape[0]
    total_tracks = group_ids.shape[0]
    labels = jnp.arange(groups, dtype=jnp.int32)
    counts = jnp.sum((group_ids == labels[None, :]).astype(jnp.int32), axis=0)
    per_group = group_weight * total_tracks / (groups * counts.astype(f32))
    local_ids = lax.dynamic_slice_in_dim(group_ids, lax.axis_index(TRK) * tile_width, tile_width, 0)
    track_scale = jnp.sum(jnp.where(local_ids == labels[None, :], per_group[None, :], 0.0), axis=1)
    keep_mask = 1.0 - missing.astype(f32).reshape(8, 1, missing.shape[0] // 8)
    targets = pltpu.with_memory_space_constraint(targets, pltpu.HBM)
    bias = head_bias[None, :]
    bias, far = lax.optimization_barrier((bias, features[0][1]))
    features[0] = (features[0][0], far)
    carried, received = None, {}
    for steps in ORDER:
        if 0 in steps:
            bias, received[2] = lax.optimization_barrier((bias, received[2]))
        prediction, *results = head_pass(
            len(steps),
            jnp.stack([core, zh] + [lax.rem(y + 4 - step, 4) for step in steps]).astype(jnp.int32),
            carried,
            [half for step in steps for half in features[step]],
            head_w,
            bias,
            track_scale[None, :],
            keep_mask,
            targets,
            0 in steps,
            pos_count * n_bin,
        )
        total = results[len(steps) :]
        carried = (prediction, *total)
        for step, partial in zip(steps, results):
            received[step] = moved(partial, 1, 4 - step) if step else partial
    mine, theirs = total
    theirs, received[1] = lax.optimization_barrier((theirs, received[1]))
    summed = sum(part.astype(f32) for part in received.values())
    half = summed.shape[0] // 2
    away = summed[half:].astype(bf16)
    feature_grad = (summed[:half] + moved(away, 2, 2).astype(f32)).astype(bf16)
    pair_sum = (mine + lax.ppermute(theirs, "core", [(0, 1), (1, 0)]).astype(f32)).astype(bf16)
    pair_sum = pair_sum.reshape(lax.axis_size("bz"), channels // n_bin, tile_width)
    gathered = lax.all_to_all(pair_sum, "bz", 0, 0, tiled=True)
    head_grad = jnp.sum(gathered.astype(f32), axis=0)
    return (prediction, head_grad, feature_grad)


def solution(mesh):
    inner = Mesh(np.asarray(mesh.devices).reshape(8, 2, 4, 2), ALL)
    in_specs = (
        P(ALL, None),
        P(),
        P(),
        P(),
        P(),
        P(),
        P(ALL, None),
        P(),
        P(None, TRK),
        P(TRK),
        P(BIN, TRK),
        P(BIN),
        P(),
        P(),
    )
    out_specs = (P(BIN, TRK), P(BIN, TRK), P(ALL, None))
    return jax.shard_map(body, mesh=inner, in_specs=in_specs, out_specs=out_specs, check_vma=False)
```

time: 167 us -> 157 us (0.940)
  waiting for transfers between devices: 63.8 us -> 49.2 us
  starting transfers between devices: 47.9 us -> 55 us
  Pallas kernels: 35.1 us -> 42.1 us
  other arithmetic: 8.6 us -> 3.33 us
  local copies, waits for them, and re-layouts: 6.9 us -> 3.45 us
  matrix products: 2.27 us -> 0 us
    ppermute x24, waiting for transfers between devices: 57.7 us -> 36.4 us  [moved(): return lax.ppermute(value, ALL, pairs)]
    ppermute x24, starting transfers between devices: 39.1 us -> 44.1 us  [moved(): return lax.ppermute(value, ALL, pairs)]
    all_to_all x1, waiting for transfers between devices: 0.46 us -> 5.33 us  [body(): gathered = lax.all_to_all(pair_sum, 'bz', 0, 0, tiled=True)]
    unnamed x36 -> x26, local copies, waits for them, and re-layouts: 6.07 us -> 1.97 us
    pallas_call x5, Pallas kernels: 5.92 us -> 9.5 us  [attend(): pl.pallas_call(functools.partial(attend_kernel, head_dim, state is None),...]
    pallas_call x6 -> x7, Pallas kernels: 29.1 us -> 32.5 us  [the longest x4 26.4 us: head_pass(): pl.pallas_call(functools.partial(head_kernel, groups, first, last, positi...]
    dot_general x2 -> x0, matrix products: 2.27 us -> none  [the longest x1 1.56 us: body(): keyvals = jnp.dot(normed, w_kv, preferred_element_type=f32).astype(bf16)]
    ppermute x2, waiting for transfers between devices: 5.6 us -> 7.46 us  [the longest x1 6.07 us: body(): after = lax.ppermute(to_prev, ALL, [(j, i) for i, j in nexts])]
  transfers between devices with their start and end apart: 28 -> 28, of which waited for: 14 -> 15; matrix products, arithmetic and copies ran while one was open for 4% -> 2% of each run, Pallas kernels for 19% -> 23%
where the time goes in v5:
time: 157 us; the launch traced here: 154 us
  starting transfers between devices  55 us (35%)
  waiting for transfers between devices  49.2 us (31%)
  Pallas kernels  42.1 us (27%)
  local copies, waits for them, and re-layouts  3.45 us (2%)
  other arithmetic  3.33 us (2%)
    ppermute x24, starting transfers between devices, moved(): return lax.ppermute(value, ALL, pairs)  44.1 us
    ppermute x24, waiting for transfers between devices, moved(): return lax.ppermute(value, ALL, pairs)  36.4 us
    pallas_call x4, Pallas kernels, head_pass(): pl.pallas_call(functools.partial(head_kernel, groups, first, last, positi...  26.4 us
    pallas_call x5, Pallas kernels, attend(): pl.pallas_call(functools.partial(attend_kernel, head_dim, state is None),...  9.5 us
    ppermute x1, waiting for transfers between devices, body(): after = lax.ppermute(to_prev, ALL, [(j, i) for i, j in nexts])  6.07 us
    all_to_all x1, starting transfers between devices, body(): gathered = lax.all_to_all(pair_sum, 'bz', 0, 0, tiled=True)  5.98 us
    all_to_all x1, waiting for transfers between devices, body(): gathered = lax.all_to_all(pair_sum, 'bz', 0, 0, tiled=True)  5.33 us
    pallas_call x1, Pallas kernels, finish(): pl.pallas_call(finish_kernel, in_specs=[pl.BlockSpec(memory_space=pltpu.S...  3.69 us
  transfers between devices with their start and end apart: 28, of which 15 were waited for; matrix products, arithmetic and copies ran while one was open for 2% of the time, Pallas kernels for 23%

profile of v5, /device:TPU:0, one launch (start us, length us, event | category | flops | bytes accessed | tf_op | source)
XLA Modules:
  0.0 154.0 jit_solution(6102733224155174627)
XLA Ops:
  5.7 2.2 %collective-permute-start.1 = (bf16[64,256]{1,0:T(8,128)(2,1)S(1)}, bf16[64,256]{1,0:T(8,128)(2,1)S(1)}, u32[]{:S(2)}, u32[]{:S(2)}) collective-permute-start(bf16[64,256]{1,0:T(8,128)(2,1)S(1)} %get-tuple-element.43.refs_0_), channel_id=1, source_target_pairs={{0,65},{1,64},{2,67},{3,66},{4,69},{5,68},{6,71},{7,70},{8,73},{9,... | collective-permute-start | bytes 98312 | tf_op jit(solution)/shard_map/ppermute | solution.py:39
  9.8 3.6 %collective-permute-done.2.refs_3_ = bf16[64,256]{1,0:T(8,128)(2,1)S(1)} collective-permute-done((bf16[64,256]{1,0:T(8,128)(2,1)S(1)}, bf16[64,256]{1,0:T(8,128)(2,1)S(1)}, u32[]{:S(2)}, u32[]{:S(2)}) %collective-permute-start.2) | collective-permute-done | bytes 32800 | tf_op jit(solution)/shard_map/ppermute | solution.py:39
  18.7 2.4 %collective-permute-done.3.refs_1_ = bf16[256,256]{1,0:T(8,128)(2,1)S(1)} collective-permute-done((bf16[256,256]{1,0:T(8,128)(2,1)S(1)}, bf16[256,256]{1,0:T(8,128)(2,1)S(1)}, u32[]{:S(2)}, u32[]{:S(2)}) %collective-permute-start.3) | collective-permute-done | bytes 131104 | tf_op jit(solution)/shard_map/ppermute | solution.py:39
  21.0 2.1 %collective-permute-done.5.refs_3_ = bf16[256,256]{1,0:T(8,128)(2,1)S(1)} collective-permute-done((bf16[256,256]{1,0:T(8,128)(2,1)S(1)}, bf16[256,256]{1,0:T(8,128)(2,1)S(1)}, u32[]{:S(2)}, u32[]{:S(2)}) %collective-permute-start.5) | collective-permute-done | bytes 131104 | tf_op jit(solution)/shard_map/ppermute | solution.py:39
  28.3 3.7 %collective-permute-start.8 = (bf16[8,768]{1,0:T(8,128)(2,1)S(1)}, bf16[8,768]{1,0:T(8,128)(2,1)S(1)}, u32[]{:S(2)}, u32[]{:S(2)}) collective-permute-start(bf16[8,768]{1,0:T(8,128)(2,1)S(1)} %get-tuple-element.44), channel_id=1, source_target_pairs={{0,1},{1,2},{2,3},{3,4},{4,5},{5,6},{6,7},{7,8},{8,9},{9,10},{10,1... | collective-permute-start | bytes 36872 | tf_op jit(solution)/shard_map/ppermute | solution.py:422
  34.7 6.1 %collective-permute-done.9.after_ref = bf16[8,768]{1,0:T(8,128)(2,1)S(1)} collective-permute-done((bf16[8,768]{1,0:T(8,128)(2,1)S(1)}, bf16[8,768]{1,0:T(8,128)(2,1)S(1)}, u32[]{:S(2)}, u32[]{:S(2)}) %collective-permute-start.9) | collective-permute-done | bytes 12320 | tf_op jit(solution)/shard_map/ppermute | solution.py:423
  40.8 3.0 %collective-permute-start.13 = (bf16[1024,256]{1,0:T(8,128)(2,1)S(1)}, bf16[1024,256]{1,0:T(8,128)(2,1)}, u32[]{:S(2)}, u32[]{:S(2)}) collective-permute-start(bf16[1024,256]{1,0:T(8,128)(2,1)S(1)} %collective-permute-done.7.refs_3_), channel_id=1, source_target_pairs={{0,8},{1,9},{2,10},{3,11},{4,12},{5,13},{6,14},{7,15},{8,0},{9,1},... | collective-permute-start | bytes 1572872 | tf_op jit(solution)/shard_map/ppermute | solution.py:39
  50.6 2.6 %attend.7 = (f32[528,128]{1,0:T(8,128)S(1)}, f32[528,128]{1,0:T(8,128)S(1)}) custom-call(bf16[64,1024]{1,0:T(8,128)(2,1)S(1)} %get-tuple-element.50.refs_0_, bf16[16,128]{1,0:T(8,128)(2,1)S(1)} %get-tuple-element.51.refs_1_, bf16[1024,256]{1,0:T(8,128)(2,1)} %collective-permute-done.13.refs_2_, bf16[1024,256]{1,0:T(8,128)(2,1)S(1)} %collective-permute-done.6.refs_3_, ...), custom_call_target="tpu_custom_call" | custom-call | flops 1107296256 | bytes 1048576 | tf_op jit(solution)/shard_map/attend/pallas_call | solution.py:188
  53.3 2.6 %attend.8 = (f32[528,128]{1,0:T(8,128)S(1)}, f32[528,128]{1,0:T(8,128)S(1)}) custom-call(bf16[64,1024]{1,0:T(8,128)(2,1)S(1)} %get-tuple-element.50.refs_0_, bf16[16,128]{1,0:T(8,128)(2,1)S(1)} %get-tuple-element.51.refs_1_, bf16[1024,256]{1,0:T(8,128)(2,1)} %collective-permute-done.12.refs_2_, bf16[1024,256]{1,0:T(8,128)(2,1)S(1)} %collective-permute-done.10.refs_3_, ...), custom_call_target="tpu_custom_call" | custom-call | flops 1107296256 | bytes 1048576 | tf_op jit(solution)/shard_map/attend/pallas_call | solution.py:188
  57.9 3.7 %finish.1.refs_0_ = bf16[256,768]{1,0:T(8,128)(2,1)S(1)} custom-call(s32[2]{0:T(128)S(1)} %pad_add_fusion.2.at_ref, f32[528,128]{1,0:T(8,128)S(1)} %get-tuple-element.62.num_ref, f32[528,128]{1,0:T(8,128)S(1)} %get-tuple-element.63.den_ref, bf16[64,1536]{1,0:T(8,128)(2,1)S(1)} %copy-done.4, bf16[8,768]{1,0:T(8,128)(2,1)S(1)} %collective-permute-done.8.before_ref, ...), custom_call_target="tpu_custom_call" | custom-call | flops 1862270976 | bytes 11403264 | tf_op jit(solution)/shard_map/finish/pallas_call | solution.py:260
  64.7 7.3 %collective-permute-start.15 = (bf16[256,768]{1,0:T(8,128)(2,1)S(1)}, bf16[256,768]{1,0:T(8,128)(2,1)S(1)}, u32[]{:S(2)}, u32[]{:S(2)}) collective-permute-start(bf16[256,768]{1,0:T(8,128)(2,1)S(1)} %finish.1.refs_0_), channel_id=1, source_target_pairs={{0,1},{1,0},{2,3},{3,2},{4,5},{5,4},{6,7},{7,6},{8,9},{9,8},{10,11... | collective-permute-start | bytes 1179656 | tf_op jit(solution)/shard_map/ppermute | solution.py:39
  72.0 3.2 %collective-permute-done.16.refs_0_ = bf16[256,768]{1,0:T(8,128)(2,1)S(1)} collective-permute-done((bf16[256,768]{1,0:T(8,128)(2,1)S(1)}, bf16[256,768]{1,0:T(8,128)(2,1)S(1)}, u32[]{:S(2)}, u32[]{:S(2)}) %collective-permute-start.16) | collective-permute-done | bytes 393248 | tf_op jit(solution)/shard_map/ppermute | solution.py:39
  76.7 6.5 %collective-permute-done.21.refs_0_ = bf16[256,768]{1,0:T(8,128)(2,1)S(1)} collective-permute-done((bf16[256,768]{1,0:T(8,128)(2,1)S(1)}, bf16[256,768]{1,0:T(8,128)(2,1)S(1)}, u32[]{:S(2)}, u32[]{:S(2)}) %collective-permute-start.21) | collective-permute-done | bytes 393248 | tf_op jit(solution)/shard_map/ppermute | solution.py:39
  84.5 4.9 %collective-permute-start.20 = (bf16[256,768]{1,0:T(8,128)(2,1)S(1)}, bf16[256,768]{1,0:T(8,128)(2,1)S(1)}, u32[]{:S(2)}, u32[]{:S(2)}) collective-permute-start(bf16[256,768]{1,0:T(8,128)(2,1)S(1)} %collective-permute-done.19.refs_0_), channel_id=1, source_target_pairs={{0,1},{1,0},{2,3},{3,2},{4,5},{5,4},{6,7},{7,6},{8,9},{9,8},{10,11... | collective-permute-start | bytes 1179656 | tf_op jit(solution)/shard_map/ppermute | solution.py:39
  90.5 6.5 %head_pass.4 = (bf16[2048,768]{1,0:T(8,128)(2,1)}, bf16[512,768]{1,0:T(8,128)(2,1)S(1)}, f32[768,768]{1,0:T(8,128)S(1)}) custom-call(s32[3]{0:T(128)S(1)} %get-tuple-element.86.at_ref, bf16[256,768]{1,0:T(8,128)(2,1)S(1)} %collective-permute-done.16.refs_0_, bf16[256,768]{1,0:T(8,128)(2,1)} %collective-permute-done.17.refs_1_, bf16[768,768]{1,0:T(8,128)(2,1)S(1)} %copy-done, ...), custom_call_target="tpu_custom_call" | custom-call | flops 1811939328 | bytes 6291456 | tf_op jit(solution)/shard_map/head_pass/pallas_call | solution.py:367
  98.8 6.6 %head_pass.5 = (bf16[2048,768]{1,0:T(8,128)(2,1)}, bf16[512,768]{1,0:T(8,128)(2,1)S(1)}, f32[768,768]{1,0:T(8,128)S(1)}) custom-call(s32[3]{0:T(128)S(1)} %get-tuple-element.83.at_ref, bf16[256,768]{1,0:T(8,128)(2,1)S(1)} %collective-permute-done.21.refs_0_, bf16[256,768]{1,0:T(8,128)(2,1)S(1)} %collective-permute-done.22.refs_1_, ...), custom_call_target="tpu_custom_call", output_to_operand_aliasing={{0}: (8, {})} | custom-call | flops 1811939328 | bytes 6291456 | tf_op jit(solution)/shard_map/head_pass/pallas_call | solution.py:367
  105.4 3.9 %collective-permute-start.23 = (bf16[512,768]{1,0:T(8,128)(2,1)S(1)}, bf16[512,768]{1,0:T(8,128)(2,1)S(1)}, u32[]{:S(2)}, u32[]{:S(2)}) collective-permute-start(bf16[512,768]{1,0:T(8,128)(2,1)S(1)} %get-tuple-element.77), channel_id=1, source_target_pairs={{0,6},{1,7},{2,0},{3,1},{4,2},{5,3},{6,4},{7,5},{8,14},{9,15},{10,... | collective-permute-start | bytes 2359304 | tf_op jit(solution)/shard_map/ppermute | solution.py:39
  109.3 6.6 %head_pass.6 = (bf16[2048,768]{1,0:T(8,128)(2,1)}, bf16[512,768]{1,0:T(8,128)(2,1)S(1)}, f32[768,768]{1,0:T(8,128)S(1)}) custom-call(s32[3]{0:T(128)S(1)} %get-tuple-element.85.at_ref, bf16[256,768]{1,0:T(8,128)(2,1)S(1)} %collective-permute-done.19.refs_0_, bf16[256,768]{1,0:T(8,128)(2,1)S(1)} %collective-permute-done.20.refs_1_, ...), custom_call_target="tpu_custom_call", output_to_operand_aliasing={{0}: (8, {})} | custom-call | flops 1811939328 | bytes 6291456 | tf_op jit(solution)/shard_map/head_pass/pallas_call | solution.py:367
  116.3 6.7 %head_pass.7 = (bf16[2048,768]{1,0:T(8,128)(2,1)}, bf16[512,768]{1,0:T(8,128)(2,1)S(1)}, f32[384,768]{1,0:T(8,128)S(1)}, bf16[384,768]{1,0:T(8,128)(2,1)S(1)}) custom-call(s32[3]{0:T(128)S(1)} %get-tuple-element.87.at_ref, bf16[256,768]{1,0:T(8,128)(2,1)S(1)} %finish.1.refs_0_, ...), custom_call_target="tpu_custom_call", output_to_operand_aliasing={{0}: (8, {})} | custom-call | flops 1811939328 | bytes 6291456 | tf_op jit(solution)/shard_map/head_pass/pallas_call | solution.py:367
  123.0 10.5 %collective-permute-done.23 = bf16[512,768]{1,0:T(8,128)(2,1)S(1)} collective-permute-done((bf16[512,768]{1,0:T(8,128)(2,1)S(1)}, bf16[512,768]{1,0:T(8,128)(2,1)S(1)}, u32[]{:S(2)}, u32[]{:S(2)}) %collective-permute-start.23) | collective-permute-done | bytes 786464 | tf_op jit(solution)/shard_map/ppermute | solution.py:39
  133.9 2.5 %collective-permute-start.26 = (bf16[256,768]{1,0:T(8,128)(2,1)S(1)}, bf16[256,768]{1,0:T(8,128)(2,1)S(1)}, u32[]{:S(2)}, u32[]{:S(2)}) collective-permute-start(bf16[256,768]{1,0:T(8,128)(2,1)S(1)} %slice.15), channel_id=1, source_target_pairs={{0,1},{1,0},{2,3},{3,2},{4,5},{5,4},{6,7},{7,6},{8,9},{9,8},{10,11... | collective-permute-start | bytes 1179656 | tf_op jit(solution)/shard_map/ppermute | solution.py:39
  137.4 6.0 %all-to-all-start = ((bf16[8,48,768]{2,1,0:T(8,128)(2,1)}), bf16[8,48,768]{2,1,0:T(8,128)(2,1)S(1)}, u32[]{:S(2)}, u32[]{:S(2)}) async-start(bf16[8,48,768]{2,1,0:T(8,128)(2,1)} %bitcast.9), calls=%async_computation | async-start | bytes 1179648 | tf_op jit(solution)/shard_map/all_to_all | solution.py:486
  143.4 3.7 %collective-permute-done.26 = bf16[256,768]{1,0:T(8,128)(2,1)S(1)} collective-permute-done((bf16[256,768]{1,0:T(8,128)(2,1)S(1)}, bf16[256,768]{1,0:T(8,128)(2,1)S(1)}, u32[]{:S(2)}, u32[]{:S(2)}) %collective-permute-start.26) | collective-permute-done | bytes 393248 | tf_op jit(solution)/shard_map/ppermute | solution.py:39
  147.9 5.3 %all-to-all-done = bf16[8,48,768]{2,1,0:T(8,128)(2,1)S(1)} async-done(((bf16[8,48,768]{2,1,0:T(8,128)(2,1)}), bf16[8,48,768]{2,1,0:T(8,128)(2,1)S(1)}, u32[]{:S(2)}, u32[]{:S(2)}) %all-to-all-start) | async-done | bytes 589856 | tf_op jit(solution)/shard_map/all_to_all | solution.py:486
  (90 shorter events, 40.9 us)
Async XLA Ops:
  3.7 6.1 %collective-permute-start = (bf16[64,256]{1,0:T(8,128)(2,1)S(1)}, bf16[64,256]{1,0:T(8,128)(2,1)S(1)}, u32[]{:S(2)}, u32[]{:S(2)}) collective-permute-start(bf16[64,256]{1,0:T(8,128)(2,1)S(1)} %get-tuple-element.43.refs_0_), channel_id=1, source_target_pairs={{0,64},{1,65},{2,66},{3,67},{4,68},{5,69},{6,70},{7,71},{8,72},{9,... | collective-permute-start | bytes 98312 | tf_op jit(solution)/shard_map/ppermute | solution.py:39
  13.4 7.7 %collective-permute-start.3 = (bf16[256,256]{1,0:T(8,128)(2,1)S(1)}, bf16[256,256]{1,0:T(8,128)(2,1)S(1)}, u32[]{:S(2)}, u32[]{:S(2)}) collective-permute-start(bf16[256,256]{1,0:T(8,128)(2,1)S(1)} %join.2.refs_0_), channel_id=1, source_target_pairs={{0,2},{1,3},{2,4},{3,5},{4,6},{5,7},{6,0},{7,1},{8,10},{9,11},{10,... | collective-permute-start | bytes 393224 | tf_op jit(solution)/shard_map/ppermute | solution.py:39
  15.0 6.0 %collective-permute-start.4 = (bf16[256,256]{1,0:T(8,128)(2,1)S(1)}, bf16[256,256]{1,0:T(8,128)(2,1)S(1)}, u32[]{:S(2)}, u32[]{:S(2)}) collective-permute-start(bf16[256,256]{1,0:T(8,128)(2,1)S(1)} %join.2.refs_0_), channel_id=1, source_target_pairs={{0,6},{1,7},{2,0},{3,1},{4,2},{5,3},{6,4},{7,5},{8,14},{9,15},{10,... | collective-permute-start | bytes 393224 | tf_op jit(solution)/shard_map/ppermute | solution.py:39
  16.7 6.5 %collective-permute-start.5 = (bf16[256,256]{1,0:T(8,128)(2,1)S(1)}, bf16[256,256]{1,0:T(8,128)(2,1)S(1)}, u32[]{:S(2)}, u32[]{:S(2)}) collective-permute-start(bf16[256,256]{1,0:T(8,128)(2,1)S(1)} %join.2.refs_0_), channel_id=1, source_target_pairs={{0,4},{1,5},{2,6},{3,7},{4,0},{5,1},{6,2},{7,3},{8,12},{9,13},{10,... | collective-permute-start | bytes 393224 | tf_op jit(solution)/shard_map/ppermute | solution.py:39
  23.2 17.6 %collective-permute-start.7 = (bf16[1024,256]{1,0:T(8,128)(2,1)S(1)}, bf16[1024,256]{1,0:T(8,128)(2,1)S(1)}, u32[]{:S(2)}, u32[]{:S(2)}) collective-permute-start(bf16[1024,256]{1,0:T(8,128)(2,1)S(1)} %join.3.refs_2_), channel_id=1, source_target_pairs={{0,16},{1,17},{2,18},{3,19},{4,20},{5,21},{6,22},{7,23},{8,24},{9,... | collective-permute-start | bytes 1572872 | tf_op jit(solution)/shard_map/ppermute | solution.py:39
  24.8 21.7 %collective-permute-start.6 = (bf16[1024,256]{1,0:T(8,128)(2,1)S(1)}, bf16[1024,256]{1,0:T(8,128)(2,1)S(1)}, u32[]{:S(2)}, u32[]{:S(2)}) collective-permute-start(bf16[1024,256]{1,0:T(8,128)(2,1)S(1)} %join.3.refs_2_), channel_id=1, source_target_pairs={{0,48},{1,49},{2,50},{3,51},{4,52},{5,53},{6,54},{7,55},{8,56},{9,... | collective-permute-start | bytes 1572872 | tf_op jit(solution)/shard_map/ppermute | solution.py:39
  26.5 21.6 %collective-permute-start.10 = (bf16[1024,256]{1,0:T(8,128)(2,1)S(1)}, bf16[1024,256]{1,0:T(8,128)(2,1)S(1)}, u32[]{:S(2)}, u32[]{:S(2)}) collective-permute-start(bf16[1024,256]{1,0:T(8,128)(2,1)S(1)} %join.3.refs_2_), channel_id=1, source_target_pairs={{0,32},{1,33},{2,34},{3,35},{4,36},{5,37},{6,38},{7,39},{8,40},{9,... | collective-permute-start | bytes 1572872 | tf_op jit(solution)/shard_map/ppermute | solution.py:39
  28.3 20.9 %collective-permute-start.14 = (bf16[1024,256]{1,0:T(8,128)(2,1)S(1)}, bf16[1024,256]{1,0:T(8,128)(2,1)S(1)}, u32[]{:S(2)}, u32[]{:S(2)}) collective-permute-start(bf16[1024,256]{1,0:T(8,128)(2,1)S(1)} %join.3.refs_2_), channel_id=1, source_target_pairs={{0,8},{1,9},{2,10},{3,11},{4,12},{5,13},{6,14},{7,15},{8,0},{9,1},... | collective-permute-start | bytes 1572872 | tf_op jit(solution)/shard_map/ppermute | solution.py:39
  33.4 7.4 %collective-permute-start.9 = (bf16[8,768]{1,0:T(8,128)(2,1)S(1)}, bf16[8,768]{1,0:T(8,128)(2,1)S(1)}, u32[]{:S(2)}, u32[]{:S(2)}) collective-permute-start(bf16[8,768]{1,0:T(8,128)(2,1)S(1)} %get-tuple-element.45), channel_id=1, source_target_pairs={{1,0},{2,1},{3,2},{4,3},{5,4},{6,5},{7,6},{8,7},{9,8},{10,9},{11,1... | collective-permute-start | bytes 36872 | tf_op jit(solution)/shard_map/ppermute | solution.py:423
  40.8 9.9 %collective-permute-start.13 = (bf16[1024,256]{1,0:T(8,128)(2,1)S(1)}, bf16[1024,256]{1,0:T(8,128)(2,1)}, u32[]{:S(2)}, u32[]{:S(2)}) collective-permute-start(bf16[1024,256]{1,0:T(8,128)(2,1)S(1)} %collective-permute-done.7.refs_3_), channel_id=1, source_target_pairs={{0,8},{1,9},{2,10},{3,11},{4,12},{5,13},{6,14},{7,15},{8,0},{9,1},... | collective-permute-start | bytes 1572872 | tf_op jit(solution)/shard_map/ppermute | solution.py:39
  46.4 6.8 %collective-permute-start.12 = (bf16[1024,256]{1,0:T(8,128)(2,1)S(1)}, bf16[1024,256]{1,0:T(8,128)(2,1)}, u32[]{:S(2)}, u32[]{:S(2)}) collective-permute-start(bf16[1024,256]{1,0:T(8,128)(2,1)S(1)} %collective-permute-done.6.refs_3_), channel_id=1, source_target_pairs={{0,8},{1,9},{2,10},{3,11},{4,12},{5,13},{6,14},{7,15},{8,0},{9,1},... | collective-permute-start | bytes 1572872 | tf_op jit(solution)/shard_map/ppermute | solution.py:39
  48.1 7.8 %collective-permute-start.11 = (bf16[1024,256]{1,0:T(8,128)(2,1)S(1)}, bf16[1024,256]{1,0:T(8,128)(2,1)}, u32[]{:S(2)}, u32[]{:S(2)}) collective-permute-start(bf16[1024,256]{1,0:T(8,128)(2,1)S(1)} %collective-permute-done.10.refs_3_), channel_id=1, source_target_pairs={{0,8},{1,9},{2,10},{3,11},{4,12},{5,13},{6,14},{7,15},{8,0},{9,1},... | collective-permute-start | bytes 1572872 | tf_op jit(solution)/shard_map/ppermute | solution.py:39
  61.6 13.5 %collective-permute-start.16 = (bf16[256,768]{1,0:T(8,128)(2,1)S(1)}, bf16[256,768]{1,0:T(8,128)(2,1)S(1)}, u32[]{:S(2)}, u32[]{:S(2)}) collective-permute-start(bf16[256,768]{1,0:T(8,128)(2,1)S(1)} %finish.1.refs_0_), channel_id=1, source_target_pairs={{0,4},{1,5},{2,6},{3,7},{4,0},{5,1},{6,2},{7,3},{8,12},{9,13},{10,... | collective-permute-start | bytes 1179656 | tf_op jit(solution)/shard_map/ppermute | solution.py:39
  63.9 19.2 %collective-permute-start.21 = (bf16[256,768]{1,0:T(8,128)(2,1)S(1)}, bf16[256,768]{1,0:T(8,128)(2,1)S(1)}, u32[]{:S(2)}, u32[]{:S(2)}) collective-permute-start(bf16[256,768]{1,0:T(8,128)(2,1)S(1)} %finish.1.refs_0_), channel_id=1, source_target_pairs={{0,2},{1,3},{2,4},{3,5},{4,6},{5,7},{6,0},{7,1},{8,10},{9,11},{10,... | collective-permute-start | bytes 1179656 | tf_op jit(solution)/shard_map/ppermute | solution.py:39
  64.7 19.8 %collective-permute-start.15 = (bf16[256,768]{1,0:T(8,128)(2,1)S(1)}, bf16[256,768]{1,0:T(8,128)(2,1)S(1)}, u32[]{:S(2)}, u32[]{:S(2)}) collective-permute-start(bf16[256,768]{1,0:T(8,128)(2,1)S(1)} %finish.1.refs_0_), channel_id=1, source_target_pairs={{0,1},{1,0},{2,3},{3,2},{4,5},{5,4},{6,7},{7,6},{8,9},{9,8},{10,11... | collective-permute-start | bytes 1179656 | tf_op jit(solution)/shard_map/ppermute | solution.py:39
  72.0 12.5 %collective-permute-start.19 = (bf16[256,768]{1,0:T(8,128)(2,1)S(1)}, bf16[256,768]{1,0:T(8,128)(2,1)S(1)}, u32[]{:S(2)}, u32[]{:S(2)}) collective-permute-start(bf16[256,768]{1,0:T(8,128)(2,1)S(1)} %finish.1.refs_0_), channel_id=1, source_target_pairs={{0,6},{1,7},{2,0},{3,1},{4,2},{5,3},{6,4},{7,5},{8,14},{9,15},{10,... | collective-permute-start | bytes 1179656 | tf_op jit(solution)/shard_map/ppermute | solution.py:39
  75.2 15.3 %collective-permute-start.17 = (bf16[256,768]{1,0:T(8,128)(2,1)S(1)}, bf16[256,768]{1,0:T(8,128)(2,1)}, u32[]{:S(2)}, u32[]{:S(2)}) collective-permute-start(bf16[256,768]{1,0:T(8,128)(2,1)S(1)} %collective-permute-done.16.refs_0_), channel_id=1, source_target_pairs={{0,1},{1,0},{2,3},{3,2},{4,5},{5,4},{6,7},{7,6},{8,9},{9,8},{10,11... | collective-permute-start | bytes 1179656 | tf_op jit(solution)/shard_map/ppermute | solution.py:39
  83.2 15.7 %collective-permute-start.22 = (bf16[256,768]{1,0:T(8,128)(2,1)S(1)}, bf16[256,768]{1,0:T(8,128)(2,1)S(1)}, u32[]{:S(2)}, u32[]{:S(2)}) collective-permute-start(bf16[256,768]{1,0:T(8,128)(2,1)S(1)} %collective-permute-done.21.refs_0_), channel_id=1, source_target_pairs={{0,1},{1,0},{2,3},{3,2},{4,5},{5,4},{6,7},{7,6},{8,9},{9,8},{10,11... | collective-permute-start | bytes 1179656 | tf_op jit(solution)/shard_map/ppermute | solution.py:39
  84.5 24.8 %collective-permute-start.20 = (bf16[256,768]{1,0:T(8,128)(2,1)S(1)}, bf16[256,768]{1,0:T(8,128)(2,1)S(1)}, u32[]{:S(2)}, u32[]{:S(2)}) collective-permute-start(bf16[256,768]{1,0:T(8,128)(2,1)S(1)} %collective-permute-done.19.refs_0_), channel_id=1, source_target_pairs={{0,1},{1,0},{2,3},{3,2},{4,5},{5,4},{6,7},{7,6},{8,9},{9,8},{10,11... | collective-permute-start | bytes 1179656 | tf_op jit(solution)/shard_map/ppermute | solution.py:39
  97.0 19.2 %collective-permute-start.18 = (bf16[512,768]{1,0:T(8,128)(2,1)S(1)}, bf16[512,768]{1,0:T(8,128)(2,1)S(1)}, u32[]{:S(2)}, u32[]{:S(2)}) collective-permute-start(bf16[512,768]{1,0:T(8,128)(2,1)S(1)} %get-tuple-element.66), channel_id=1, source_target_pairs={{0,4},{1,5},{2,6},{3,7},{4,0},{5,1},{6,2},{7,3},{8,12},{9,13},{10,... | collective-permute-start | bytes 2359304 | tf_op jit(solution)/shard_map/ppermute | solution.py:39
  105.4 28.1 %collective-permute-start.23 = (bf16[512,768]{1,0:T(8,128)(2,1)S(1)}, bf16[512,768]{1,0:T(8,128)(2,1)S(1)}, u32[]{:S(2)}, u32[]{:S(2)}) collective-permute-start(bf16[512,768]{1,0:T(8,128)(2,1)S(1)} %get-tuple-element.77), channel_id=1, source_target_pairs={{0,6},{1,7},{2,0},{3,1},{4,2},{5,3},{6,4},{7,5},{8,14},{9,15},{10,... | collective-permute-start | bytes 2359304 | tf_op jit(solution)/shard_map/ppermute | solution.py:39
  115.9 17.6 %collective-permute-start.25 = (bf16[512,768]{1,0:T(8,128)(2,1)S(1)}, bf16[512,768]{1,0:T(8,128)(2,1)S(1)}, u32[]{:S(2)}, u32[]{:S(2)}) collective-permute-start(bf16[512,768]{1,0:T(8,128)(2,1)S(1)} %get-tuple-element.81), channel_id=1, source_target_pairs={{0,2},{1,3},{2,4},{3,5},{4,6},{5,7},{6,0},{7,1},{8,10},{9,11},{10,... | collective-permute-start | bytes 2359304 | tf_op jit(solution)/shard_map/ppermute | solution.py:39
  133.9 13.2 %collective-permute-start.26 = (bf16[256,768]{1,0:T(8,128)(2,1)S(1)}, bf16[256,768]{1,0:T(8,128)(2,1)S(1)}, u32[]{:S(2)}, u32[]{:S(2)}) collective-permute-start(bf16[256,768]{1,0:T(8,128)(2,1)S(1)} %slice.15), channel_id=1, source_target_pairs={{0,1},{1,0},{2,3},{3,2},{4,5},{5,4},{6,7},{7,6},{8,9},{9,8},{10,11... | collective-permute-start | bytes 1179656 | tf_op jit(solution)/shard_map/ppermute | solution.py:39
  137.4 15.9 %all-to-all-start = ((bf16[8,48,768]{2,1,0:T(8,128)(2,1)}), bf16[8,48,768]{2,1,0:T(8,128)(2,1)S(1)}, u32[]{:S(2)}, u32[]{:S(2)}) async-start(bf16[8,48,768]{2,1,0:T(8,128)(2,1)} %bitcast.9), calls=%async_computation | async-start | bytes 1179648 | tf_op jit(solution)/shard_map/all_to_all | solution.py:486
  (17 other events, 200.9 us)

commit v6 on v5

--- a/solution.py
+++ b/solution.py
@@ -413,7 +413,7 @@
     head_count = w_query.shape[1] // head_dim
     n_all, index = lax.axis_size(ALL), lax.axis_index(ALL)
     channels = conv_w.shape[1]
-    gain = norm_gain[None, :]
+    gain = norm_gain
     keyvals, to_next, to_prev = start(
         *[pltpu.with_memory_space_constraint(value, pltpu.HBM) for value in (trunk, gain, w_kv, skip)]
     )

time: 157 us -> 156 us (level)
  no operation moved by 1% of the time
where the time goes in v6:
time: 156 us; the launch traced here: 153 us
  starting transfers between devices  55 us (35%)
  waiting for transfers between devices  49.2 us (32%)
  Pallas kernels  42.1 us (27%)
  other arithmetic  3.33 us (2%)
  local copies, waits for them, and re-layouts  2.12 us (1%)
    ppermute x24, starting transfers between devices, moved(): return lax.ppermute(value, ALL, pairs)  44.1 us
    ppermute x24, waiting for transfers between devices, moved(): return lax.ppermute(value, ALL, pairs)  36.4 us
    pallas_call x4, Pallas kernels, head_pass(): pl.pallas_call(functools.partial(head_kernel, groups, first, last, positi...  26.4 us
    pallas_call x5, Pallas kernels, attend(): pl.pallas_call(functools.partial(attend_kernel, head_dim, state is None),...  9.5 us
    ppermute x1, waiting for transfers between devices, body(): after = lax.ppermute(to_prev, ALL, [(j, i) for i, j in nexts])  6.07 us
    all_to_all x1, starting transfers between devices, body(): gathered = lax.all_to_all(pair_sum, 'bz', 0, 0, tiled=True)  5.99 us
    all_to_all x1, waiting for transfers between devices, body(): gathered = lax.all_to_all(pair_sum, 'bz', 0, 0, tiled=True)  5.34 us
    pallas_call x1, Pallas kernels, finish(): pl.pallas_call(finish_kernel, in_specs=[pl.BlockSpec(memory_space=pltpu.S...  3.69 us
  transfers between devices with their start and end apart: 28, of which 15 were waited for; matrix products, arithmetic and copies ran while one was open for 2% of the time, Pallas kernels for 23%

profile of v6, /device:TPU:0, one launch (start us, length us, event | category | flops | bytes accessed | tf_op | source)
XLA Modules:
  0.0 152.7 jit_solution(17977018717298871138)
XLA Ops:
  4.4 2.2 %collective-permute-start.1 = (bf16[64,256]{1,0:T(8,128)(2,1)S(1)}, bf16[64,256]{1,0:T(8,128)(2,1)S(1)}, u32[]{:S(2)}, u32[]{:S(2)}) collective-permute-start(bf16[64,256]{1,0:T(8,128)(2,1)S(1)} %get-tuple-element.43.refs_0_), channel_id=1, source_target_pairs={{0,65},{1,64},{2,67},{3,66},{4,69},{5,68},{6,71},{7,70},{8,73},{9,... | collective-permute-start | bytes 98312 | tf_op jit(solution)/shard_map/ppermute | solution.py:39
  8.5 3.6 %collective-permute-done.2.refs_3_ = bf16[64,256]{1,0:T(8,128)(2,1)S(1)} collective-permute-done((bf16[64,256]{1,0:T(8,128)(2,1)S(1)}, bf16[64,256]{1,0:T(8,128)(2,1)S(1)}, u32[]{:S(2)}, u32[]{:S(2)}) %collective-permute-start.2) | collective-permute-done | bytes 32800 | tf_op jit(solution)/shard_map/ppermute | solution.py:39
  17.4 2.4 %collective-permute-done.3.refs_1_ = bf16[256,256]{1,0:T(8,128)(2,1)S(1)} collective-permute-done((bf16[256,256]{1,0:T(8,128)(2,1)S(1)}, bf16[256,256]{1,0:T(8,128)(2,1)S(1)}, u32[]{:S(2)}, u32[]{:S(2)}) %collective-permute-start.3) | collective-permute-done | bytes 131104 | tf_op jit(solution)/shard_map/ppermute | solution.py:39
  19.7 2.1 %collective-permute-done.5.refs_3_ = bf16[256,256]{1,0:T(8,128)(2,1)S(1)} collective-permute-done((bf16[256,256]{1,0:T(8,128)(2,1)S(1)}, bf16[256,256]{1,0:T(8,128)(2,1)S(1)}, u32[]{:S(2)}, u32[]{:S(2)}) %collective-permute-start.5) | collective-permute-done | bytes 131104 | tf_op jit(solution)/shard_map/ppermute | solution.py:39
  27.0 3.7 %collective-permute-start.8 = (bf16[8,768]{1,0:T(8,128)(2,1)S(1)}, bf16[8,768]{1,0:T(8,128)(2,1)S(1)}, u32[]{:S(2)}, u32[]{:S(2)}) collective-permute-start(bf16[8,768]{1,0:T(8,128)(2,1)S(1)} %get-tuple-element.44), channel_id=1, source_target_pairs={{0,1},{1,2},{2,3},{3,4},{4,5},{5,6},{6,7},{7,8},{8,9},{9,10},{10,1... | collective-permute-start | bytes 36872 | tf_op jit(solution)/shard_map/ppermute | solution.py:422
  33.4 6.1 %collective-permute-done.9.after_ref = bf16[8,768]{1,0:T(8,128)(2,1)S(1)} collective-permute-done((bf16[8,768]{1,0:T(8,128)(2,1)S(1)}, bf16[8,768]{1,0:T(8,128)(2,1)S(1)}, u32[]{:S(2)}, u32[]{:S(2)}) %collective-permute-start.9) | collective-permute-done | bytes 12320 | tf_op jit(solution)/shard_map/ppermute | solution.py:423
  39.4 3.0 %collective-permute-start.13 = (bf16[1024,256]{1,0:T(8,128)(2,1)S(1)}, bf16[1024,256]{1,0:T(8,128)(2,1)}, u32[]{:S(2)}, u32[]{:S(2)}) collective-permute-start(bf16[1024,256]{1,0:T(8,128)(2,1)S(1)} %collective-permute-done.7.refs_3_), channel_id=1, source_target_pairs={{0,8},{1,9},{2,10},{3,11},{4,12},{5,13},{6,14},{7,15},{8,0},{9,1},... | collective-permute-start | bytes 1572872 | tf_op jit(solution)/shard_map/ppermute | solution.py:39
  49.3 2.6 %attend.7 = (f32[528,128]{1,0:T(8,128)S(1)}, f32[528,128]{1,0:T(8,128)S(1)}) custom-call(bf16[64,1024]{1,0:T(8,128)(2,1)S(1)} %get-tuple-element.50.refs_0_, bf16[16,128]{1,0:T(8,128)(2,1)S(1)} %get-tuple-element.51.refs_1_, bf16[1024,256]{1,0:T(8,128)(2,1)} %collective-permute-done.13.refs_2_, bf16[1024,256]{1,0:T(8,128)(2,1)S(1)} %collective-permute-done.6.refs_3_, ...), custom_call_target="tpu_custom_call" | custom-call | flops 1107296256 | bytes 1048576 | tf_op jit(solution)/shard_map/attend/pallas_call | solution.py:188
  52.0 2.6 %attend.8 = (f32[528,128]{1,0:T(8,128)S(1)}, f32[528,128]{1,0:T(8,128)S(1)}) custom-call(bf16[64,1024]{1,0:T(8,128)(2,1)S(1)} %get-tuple-element.50.refs_0_, bf16[16,128]{1,0:T(8,128)(2,1)S(1)} %get-tuple-element.51.refs_1_, bf16[1024,256]{1,0:T(8,128)(2,1)} %collective-permute-done.12.refs_2_, bf16[1024,256]{1,0:T(8,128)(2,1)S(1)} %collective-permute-done.10.refs_3_, ...), custom_call_target="tpu_custom_call" | custom-call | flops 1107296256 | bytes 1048576 | tf_op jit(solution)/shard_map/attend/pallas_call | solution.py:188
  56.6 3.7 %finish.1.refs_0_ = bf16[256,768]{1,0:T(8,128)(2,1)S(1)} custom-call(s32[2]{0:T(128)S(1)} %pad_add_fusion.2.at_ref, f32[528,128]{1,0:T(8,128)S(1)} %get-tuple-element.62.num_ref, f32[528,128]{1,0:T(8,128)S(1)} %get-tuple-element.63.den_ref, bf16[64,1536]{1,0:T(8,128)(2,1)S(1)} %copy-done.4, bf16[8,768]{1,0:T(8,128)(2,1)S(1)} %collective-permute-done.8.before_ref, ...), custom_call_target="tpu_custom_call" | custom-call | flops 1862270976 | bytes 11403264 | tf_op jit(solution)/shard_map/finish/pallas_call | solution.py:260
  63.3 7.4 %collective-permute-start.15 = (bf16[256,768]{1,0:T(8,128)(2,1)S(1)}, bf16[256,768]{1,0:T(8,128)(2,1)S(1)}, u32[]{:S(2)}, u32[]{:S(2)}) collective-permute-start(bf16[256,768]{1,0:T(8,128)(2,1)S(1)} %finish.1.refs_0_), channel_id=1, source_target_pairs={{0,1},{1,0},{2,3},{3,2},{4,5},{5,4},{6,7},{7,6},{8,9},{9,8},{10,11... | collective-permute-start | bytes 1179656 | tf_op jit(solution)/shard_map/ppermute | solution.py:39
  70.7 3.2 %collective-permute-done.16.refs_0_ = bf16[256,768]{1,0:T(8,128)(2,1)S(1)} collective-permute-done((bf16[256,768]{1,0:T(8,128)(2,1)S(1)}, bf16[256,768]{1,0:T(8,128)(2,1)S(1)}, u32[]{:S(2)}, u32[]{:S(2)}) %collective-permute-start.16) | collective-permute-done | bytes 393248 | tf_op jit(solution)/shard_map/ppermute | solution.py:39
  75.4 6.5 %collective-permute-done.21.refs_0_ = bf16[256,768]{1,0:T(8,128)(2,1)S(1)} collective-permute-done((bf16[256,768]{1,0:T(8,128)(2,1)S(1)}, bf16[256,768]{1,0:T(8,128)(2,1)S(1)}, u32[]{:S(2)}, u32[]{:S(2)}) %collective-permute-start.21) | collective-permute-done | bytes 393248 | tf_op jit(solution)/shard_map/ppermute | solution.py:39
  83.2 4.9 %collective-permute-start.20 = (bf16[256,768]{1,0:T(8,128)(2,1)S(1)}, bf16[256,768]{1,0:T(8,128)(2,1)S(1)}, u32[]{:S(2)}, u32[]{:S(2)}) collective-permute-start(bf16[256,768]{1,0:T(8,128)(2,1)S(1)} %collective-permute-done.19.refs_0_), channel_id=1, source_target_pairs={{0,1},{1,0},{2,3},{3,2},{4,5},{5,4},{6,7},{7,6},{8,9},{9,8},{10,11... | collective-permute-start | bytes 1179656 | tf_op jit(solution)/shard_map/ppermute | solution.py:39
  89.2 6.5 %head_pass.4 = (bf16[2048,768]{1,0:T(8,128)(2,1)}, bf16[512,768]{1,0:T(8,128)(2,1)S(1)}, f32[768,768]{1,0:T(8,128)S(1)}) custom-call(s32[3]{0:T(128)S(1)} %get-tuple-element.86.at_ref, bf16[256,768]{1,0:T(8,128)(2,1)S(1)} %collective-permute-done.16.refs_0_, bf16[256,768]{1,0:T(8,128)(2,1)} %collective-permute-done.17.refs_1_, bf16[768,768]{1,0:T(8,128)(2,1)S(1)} %copy-done, ...), custom_call_target="tpu_custom_call" | custom-call | flops 1811939328 | bytes 6291456 | tf_op jit(solution)/shard_map/head_pass/pallas_call | solution.py:367
  97.5 6.6 %head_pass.5 = (bf16[2048,768]{1,0:T(8,128)(2,1)}, bf16[512,768]{1,0:T(8,128)(2,1)S(1)}, f32[768,768]{1,0:T(8,128)S(1)}) custom-call(s32[3]{0:T(128)S(1)} %get-tuple-element.83.at_ref, bf16[256,768]{1,0:T(8,128)(2,1)S(1)} %collective-permute-done.21.refs_0_, bf16[256,768]{1,0:T(8,128)(2,1)S(1)} %collective-permute-done.22.refs_1_, ...), custom_call_target="tpu_custom_call", output_to_operand_aliasing={{0}: (8, {})} | custom-call | flops 1811939328 | bytes 6291456 | tf_op jit(solution)/shard_map/head_pass/pallas_call | solution.py:367
  104.1 3.9 %collective-permute-start.23 = (bf16[512,768]{1,0:T(8,128)(2,1)S(1)}, bf16[512,768]{1,0:T(8,128)(2,1)S(1)}, u32[]{:S(2)}, u32[]{:S(2)}) collective-permute-start(bf16[512,768]{1,0:T(8,128)(2,1)S(1)} %get-tuple-element.77), channel_id=1, source_target_pairs={{0,6},{1,7},{2,0},{3,1},{4,2},{5,3},{6,4},{7,5},{8,14},{9,15},{10,... | collective-permute-start | bytes 2359304 | tf_op jit(solution)/shard_map/ppermute | solution.py:39
  108.0 6.6 %head_pass.6 = (bf16[2048,768]{1,0:T(8,128)(2,1)}, bf16[512,768]{1,0:T(8,128)(2,1)S(1)}, f32[768,768]{1,0:T(8,128)S(1)}) custom-call(s32[3]{0:T(128)S(1)} %get-tuple-element.85.at_ref, bf16[256,768]{1,0:T(8,128)(2,1)S(1)} %collective-permute-done.19.refs_0_, bf16[256,768]{1,0:T(8,128)(2,1)S(1)} %collective-permute-done.20.refs_1_, ...), custom_call_target="tpu_custom_call", output_to_operand_aliasing={{0}: (8, {})} | custom-call | flops 1811939328 | bytes 6291456 | tf_op jit(solution)/shard_map/head_pass/pallas_call | solution.py:367
  115.0 6.7 %head_pass.7 = (bf16[2048,768]{1,0:T(8,128)(2,1)}, bf16[512,768]{1,0:T(8,128)(2,1)S(1)}, f32[384,768]{1,0:T(8,128)S(1)}, bf16[384,768]{1,0:T(8,128)(2,1)S(1)}) custom-call(s32[3]{0:T(128)S(1)} %get-tuple-element.87.at_ref, bf16[256,768]{1,0:T(8,128)(2,1)S(1)} %finish.1.refs_0_, ...), custom_call_target="tpu_custom_call", output_to_operand_aliasing={{0}: (8, {})} | custom-call | flops 1811939328 | bytes 6291456 | tf_op jit(solution)/shard_map/head_pass/pallas_call | solution.py:367
  121.7 10.5 %collective-permute-done.23 = bf16[512,768]{1,0:T(8,128)(2,1)S(1)} collective-permute-done((bf16[512,768]{1,0:T(8,128)(2,1)S(1)}, bf16[512,768]{1,0:T(8,128)(2,1)S(1)}, u32[]{:S(2)}, u32[]{:S(2)}) %collective-permute-start.23) | collective-permute-done | bytes 786464 | tf_op jit(solution)/shard_map/ppermute | solution.py:39
  132.6 2.5 %collective-permute-start.26 = (bf16[256,768]{1,0:T(8,128)(2,1)S(1)}, bf16[256,768]{1,0:T(8,128)(2,1)S(1)}, u32[]{:S(2)}, u32[]{:S(2)}) collective-permute-start(bf16[256,768]{1,0:T(8,128)(2,1)S(1)} %slice.15), channel_id=1, source_target_pairs={{0,1},{1,0},{2,3},{3,2},{4,5},{5,4},{6,7},{7,6},{8,9},{9,8},{10,11... | collective-permute-start | bytes 1179656 | tf_op jit(solution)/shard_map/ppermute | solution.py:39
  136.1 6.0 %all-to-all-start = ((bf16[8,48,768]{2,1,0:T(8,128)(2,1)}), bf16[8,48,768]{2,1,0:T(8,128)(2,1)S(1)}, u32[]{:S(2)}, u32[]{:S(2)}) async-start(bf16[8,48,768]{2,1,0:T(8,128)(2,1)} %bitcast.9), calls=%async_computation | async-start | bytes 1179648 | tf_op jit(solution)/shard_map/all_to_all | solution.py:486
  142.1 3.7 %collective-permute-done.26 = bf16[256,768]{1,0:T(8,128)(2,1)S(1)} collective-permute-done((bf16[256,768]{1,0:T(8,128)(2,1)S(1)}, bf16[256,768]{1,0:T(8,128)(2,1)S(1)}, u32[]{:S(2)}, u32[]{:S(2)}) %collective-permute-start.26) | collective-permute-done | bytes 393248 | tf_op jit(solution)/shard_map/ppermute | solution.py:39
  146.6 5.3 %all-to-all-done = bf16[8,48,768]{2,1,0:T(8,128)(2,1)S(1)} async-done(((bf16[8,48,768]{2,1,0:T(8,128)(2,1)}), bf16[8,48,768]{2,1,0:T(8,128)(2,1)S(1)}, u32[]{:S(2)}, u32[]{:S(2)}) %all-to-all-start) | async-done | bytes 589856 | tf_op jit(solution)/shard_map/all_to_all | solution.py:486
  (89 shorter events, 39.5 us)
Async XLA Ops:
  2.4 6.1 %collective-permute-start = (bf16[64,256]{1,0:T(8,128)(2,1)S(1)}, bf16[64,256]{1,0:T(8,128)(2,1)S(1)}, u32[]{:S(2)}, u32[]{:S(2)}) collective-permute-start(bf16[64,256]{1,0:T(8,128)(2,1)S(1)} %get-tuple-element.43.refs_0_), channel_id=1, source_target_pairs={{0,64},{1,65},{2,66},{3,67},{4,68},{5,69},{6,70},{7,71},{8,72},{9,... | collective-permute-start | bytes 98312 | tf_op jit(solution)/shard_map/ppermute | solution.py:39
  12.1 7.7 %collective-permute-start.3 = (bf16[256,256]{1,0:T(8,128)(2,1)S(1)}, bf16[256,256]{1,0:T(8,128)(2,1)S(1)}, u32[]{:S(2)}, u32[]{:S(2)}) collective-permute-start(bf16[256,256]{1,0:T(8,128)(2,1)S(1)} %join.2.refs_0_), channel_id=1, source_target_pairs={{0,2},{1,3},{2,4},{3,5},{4,6},{5,7},{6,0},{7,1},{8,10},{9,11},{10,... | collective-permute-start | bytes 393224 | tf_op jit(solution)/shard_map/ppermute | solution.py:39
  13.7 6.0 %collective-permute-start.4 = (bf16[256,256]{1,0:T(8,128)(2,1)S(1)}, bf16[256,256]{1,0:T(8,128)(2,1)S(1)}, u32[]{:S(2)}, u32[]{:S(2)}) collective-permute-start(bf16[256,256]{1,0:T(8,128)(2,1)S(1)} %join.2.refs_0_), channel_id=1, source_target_pairs={{0,6},{1,7},{2,0},{3,1},{4,2},{5,3},{6,4},{7,5},{8,14},{9,15},{10,... | collective-permute-start | bytes 393224 | tf_op jit(solution)/shard_map/ppermute | solution.py:39
  15.4 6.5 %collective-permute-start.5 = (bf16[256,256]{1,0:T(8,128)(2,1)S(1)}, bf16[256,256]{1,0:T(8,128)(2,1)S(1)}, u32[]{:S(2)}, u32[]{:S(2)}) collective-permute-start(bf16[256,256]{1,0:T(8,128)(2,1)S(1)} %join.2.refs_0_), channel_id=1, source_target_pairs={{0,4},{1,5},{2,6},{3,7},{4,0},{5,1},{6,2},{7,3},{8,12},{9,13},{10,... | collective-permute-start | bytes 393224 | tf_op jit(solution)/shard_map/ppermute | solution.py:39
  21.9 17.6 %collective-permute-start.7 = (bf16[1024,256]{1,0:T(8,128)(2,1)S(1)}, bf16[1024,256]{1,0:T(8,128)(2,1)S(1)}, u32[]{:S(2)}, u32[]{:S(2)}) collective-permute-start(bf16[1024,256]{1,0:T(8,128)(2,1)S(1)} %join.3.refs_2_), channel_id=1, source_target_pairs={{0,16},{1,17},{2,18},{3,19},{4,20},{5,21},{6,22},{7,23},{8,24},{9,... | collective-permute-start | bytes 1572872 | tf_op jit(solution)/shard_map/ppermute | solution.py:39
  23.4 21.7 %collective-permute-start.6 = (bf16[1024,256]{1,0:T(8,128)(2,1)S(1)}, bf16[1024,256]{1,0:T(8,128)(2,1)S(1)}, u32[]{:S(2)}, u32[]{:S(2)}) collective-permute-start(bf16[1024,256]{1,0:T(8,128)(2,1)S(1)} %join.3.refs_2_), channel_id=1, source_target_pairs={{0,48},{1,49},{2,50},{3,51},{4,52},{5,53},{6,54},{7,55},{8,56},{9,... | collective-permute-start | bytes 1572872 | tf_op jit(solution)/shard_map/ppermute | solution.py:39
  25.2 21.6 %collective-permute-start.10 = (bf16[1024,256]{1,0:T(8,128)(2,1)S(1)}, bf16[1024,256]{1,0:T(8,128)(2,1)S(1)}, u32[]{:S(2)}, u32[]{:S(2)}) collective-permute-start(bf16[1024,256]{1,0:T(8,128)(2,1)S(1)} %join.3.refs_2_), channel_id=1, source_target_pairs={{0,32},{1,33},{2,34},{3,35},{4,36},{5,37},{6,38},{7,39},{8,40},{9,... | collective-permute-start | bytes 1572872 | tf_op jit(solution)/shard_map/ppermute | solution.py:39
  27.0 20.9 %collective-permute-start.14 = (bf16[1024,256]{1,0:T(8,128)(2,1)S(1)}, bf16[1024,256]{1,0:T(8,128)(2,1)S(1)}, u32[]{:S(2)}, u32[]{:S(2)}) collective-permute-start(bf16[1024,256]{1,0:T(8,128)(2,1)S(1)} %join.3.refs_2_), channel_id=1, source_target_pairs={{0,8},{1,9},{2,10},{3,11},{4,12},{5,13},{6,14},{7,15},{8,0},{9,1},... | collective-permute-start | bytes 1572872 | tf_op jit(solution)/shard_map/ppermute | solution.py:39
  32.1 7.4 %collective-permute-start.9 = (bf16[8,768]{1,0:T(8,128)(2,1)S(1)}, bf16[8,768]{1,0:T(8,128)(2,1)S(1)}, u32[]{:S(2)}, u32[]{:S(2)}) collective-permute-start(bf16[8,768]{1,0:T(8,128)(2,1)S(1)} %get-tuple-element.45), channel_id=1, source_target_pairs={{1,0},{2,1},{3,2},{4,3},{5,4},{6,5},{7,6},{8,7},{9,8},{10,9},{11,1... | collective-permute-start | bytes 36872 | tf_op jit(solution)/shard_map/ppermute | solution.py:423
  39.4 9.9 %collective-permute-start.13 = (bf16[1024,256]{1,0:T(8,128)(2,1)S(1)}, bf16[1024,256]{1,0:T(8,128)(2,1)}, u32[]{:S(2)}, u32[]{:S(2)}) collective-permute-start(bf16[1024,256]{1,0:T(8,128)(2,1)S(1)} %collective-permute-done.7.refs_3_), channel_id=1, source_target_pairs={{0,8},{1,9},{2,10},{3,11},{4,12},{5,13},{6,14},{7,15},{8,0},{9,1},... | collective-permute-start | bytes 1572872 | tf_op jit(solution)/shard_map/ppermute | solution.py:39
  45.1 6.8 %collective-permute-start.12 = (bf16[1024,256]{1,0:T(8,128)(2,1)S(1)}, bf16[1024,256]{1,0:T(8,128)(2,1)}, u32[]{:S(2)}, u32[]{:S(2)}) collective-permute-start(bf16[1024,256]{1,0:T(8,128)(2,1)S(1)} %collective-permute-done.6.refs_3_), channel_id=1, source_target_pairs={{0,8},{1,9},{2,10},{3,11},{4,12},{5,13},{6,14},{7,15},{8,0},{9,1},... | collective-permute-start | bytes 1572872 | tf_op jit(solution)/shard_map/ppermute | solution.py:39
  46.8 7.8 %collective-permute-start.11 = (bf16[1024,256]{1,0:T(8,128)(2,1)S(1)}, bf16[1024,256]{1,0:T(8,128)(2,1)}, u32[]{:S(2)}, u32[]{:S(2)}) collective-permute-start(bf16[1024,256]{1,0:T(8,128)(2,1)S(1)} %collective-permute-done.10.refs_3_), channel_id=1, source_target_pairs={{0,8},{1,9},{2,10},{3,11},{4,12},{5,13},{6,14},{7,15},{8,0},{9,1},... | collective-permute-start | bytes 1572872 | tf_op jit(solution)/shard_map/ppermute | solution.py:39
  60.3 13.5 %collective-permute-start.16 = (bf16[256,768]{1,0:T(8,128)(2,1)S(1)}, bf16[256,768]{1,0:T(8,128)(2,1)S(1)}, u32[]{:S(2)}, u32[]{:S(2)}) collective-permute-start(bf16[256,768]{1,0:T(8,128)(2,1)S(1)} %finish.1.refs_0_), channel_id=1, source_target_pairs={{0,4},{1,5},{2,6},{3,7},{4,0},{5,1},{6,2},{7,3},{8,12},{9,13},{10,... | collective-permute-start | bytes 1179656 | tf_op jit(solution)/shard_map/ppermute | solution.py:39
  62.6 19.2 %collective-permute-start.21 = (bf16[256,768]{1,0:T(8,128)(2,1)S(1)}, bf16[256,768]{1,0:T(8,128)(2,1)S(1)}, u32[]{:S(2)}, u32[]{:S(2)}) collective-permute-start(bf16[256,768]{1,0:T(8,128)(2,1)S(1)} %finish.1.refs_0_), channel_id=1, source_target_pairs={{0,2},{1,3},{2,4},{3,5},{4,6},{5,7},{6,0},{7,1},{8,10},{9,11},{10,... | collective-permute-start | bytes 1179656 | tf_op jit(solution)/shard_map/ppermute | solution.py:39
  63.3 19.8 %collective-permute-start.15 = (bf16[256,768]{1,0:T(8,128)(2,1)S(1)}, bf16[256,768]{1,0:T(8,128)(2,1)S(1)}, u32[]{:S(2)}, u32[]{:S(2)}) collective-permute-start(bf16[256,768]{1,0:T(8,128)(2,1)S(1)} %finish.1.refs_0_), channel_id=1, source_target_pairs={{0,1},{1,0},{2,3},{3,2},{4,5},{5,4},{6,7},{7,6},{8,9},{9,8},{10,11... | collective-permute-start | bytes 1179656 | tf_op jit(solution)/shard_map/ppermute | solution.py:39
  70.7 12.5 %collective-permute-start.19 = (bf16[256,768]{1,0:T(8,128)(2,1)S(1)}, bf16[256,768]{1,0:T(8,128)(2,1)S(1)}, u32[]{:S(2)}, u32[]{:S(2)}) collective-permute-start(bf16[256,768]{1,0:T(8,128)(2,1)S(1)} %finish.1.refs_0_), channel_id=1, source_target_pairs={{0,6},{1,7},{2,0},{3,1},{4,2},{5,3},{6,4},{7,5},{8,14},{9,15},{10,... | collective-permute-start | bytes 1179656 | tf_op jit(solution)/shard_map/ppermute | solution.py:39
  73.9 15.3 %collective-permute-start.17 = (bf16[256,768]{1,0:T(8,128)(2,1)S(1)}, bf16[256,768]{1,0:T(8,128)(2,1)}, u32[]{:S(2)}, u32[]{:S(2)}) collective-permute-start(bf16[256,768]{1,0:T(8,128)(2,1)S(1)} %collective-permute-done.16.refs_0_), channel_id=1, source_target_pairs={{0,1},{1,0},{2,3},{3,2},{4,5},{5,4},{6,7},{7,6},{8,9},{9,8},{10,11... | collective-permute-start | bytes 1179656 | tf_op jit(solution)/shard_map/ppermute | solution.py:39
  81.9 15.7 %collective-permute-start.22 = (bf16[256,768]{1,0:T(8,128)(2,1)S(1)}, bf16[256,768]{1,0:T(8,128)(2,1)S(1)}, u32[]{:S(2)}, u32[]{:S(2)}) collective-permute-start(bf16[256,768]{1,0:T(8,128)(2,1)S(1)} %collective-permute-done.21.refs_0_), channel_id=1, source_target_pairs={{0,1},{1,0},{2,3},{3,2},{4,5},{5,4},{6,7},{7,6},{8,9},{9,8},{10,11... | collective-permute-start | bytes 1179656 | tf_op jit(solution)/shard_map/ppermute | solution.py:39
  83.2 24.8 %collective-permute-start.20 = (bf16[256,768]{1,0:T(8,128)(2,1)S(1)}, bf16[256,768]{1,0:T(8,128)(2,1)S(1)}, u32[]{:S(2)}, u32[]{:S(2)}) collective-permute-start(bf16[256,768]{1,0:T(8,128)(2,1)S(1)} %collective-permute-done.19.refs_0_), channel_id=1, source_target_pairs={{0,1},{1,0},{2,3},{3,2},{4,5},{5,4},{6,7},{7,6},{8,9},{9,8},{10,11... | collective-permute-start | bytes 1179656 | tf_op jit(solution)/shard_map/ppermute | solution.py:39
  95.7 19.2 %collective-permute-start.18 = (bf16[512,768]{1,0:T(8,128)(2,1)S(1)}, bf16[512,768]{1,0:T(8,128)(2,1)S(1)}, u32[]{:S(2)}, u32[]{:S(2)}) collective-permute-start(bf16[512,768]{1,0:T(8,128)(2,1)S(1)} %get-tuple-element.66), channel_id=1, source_target_pairs={{0,4},{1,5},{2,6},{3,7},{4,0},{5,1},{6,2},{7,3},{8,12},{9,13},{10,... | collective-permute-start | bytes 2359304 | tf_op jit(solution)/shard_map/ppermute | solution.py:39
  104.1 28.1 %collective-permute-start.23 = (bf16[512,768]{1,0:T(8,128)(2,1)S(1)}, bf16[512,768]{1,0:T(8,128)(2,1)S(1)}, u32[]{:S(2)}, u32[]{:S(2)}) collective-permute-start(bf16[512,768]{1,0:T(8,128)(2,1)S(1)} %get-tuple-element.77), channel_id=1, source_target_pairs={{0,6},{1,7},{2,0},{3,1},{4,2},{5,3},{6,4},{7,5},{8,14},{9,15},{10,... | collective-permute-start | bytes 2359304 | tf_op jit(solution)/shard_map/ppermute | solution.py:39
  114.6 17.6 %collective-permute-start.25 = (bf16[512,768]{1,0:T(8,128)(2,1)S(1)}, bf16[512,768]{1,0:T(8,128)(2,1)S(1)}, u32[]{:S(2)}, u32[]{:S(2)}) collective-permute-start(bf16[512,768]{1,0:T(8,128)(2,1)S(1)} %get-tuple-element.81), channel_id=1, source_target_pairs={{0,2},{1,3},{2,4},{3,5},{4,6},{5,7},{6,0},{7,1},{8,10},{9,11},{10,... | collective-permute-start | bytes 2359304 | tf_op jit(solution)/shard_map/ppermute | solution.py:39
  132.6 13.2 %collective-permute-start.26 = (bf16[256,768]{1,0:T(8,128)(2,1)S(1)}, bf16[256,768]{1,0:T(8,128)(2,1)S(1)}, u32[]{:S(2)}, u32[]{:S(2)}) collective-permute-start(bf16[256,768]{1,0:T(8,128)(2,1)S(1)} %slice.15), channel_id=1, source_target_pairs={{0,1},{1,0},{2,3},{3,2},{4,5},{5,4},{6,7},{7,6},{8,9},{9,8},{10,11... | collective-permute-start | bytes 1179656 | tf_op jit(solution)/shard_map/ppermute | solution.py:39
  136.1 15.9 %all-to-all-start = ((bf16[8,48,768]{2,1,0:T(8,128)(2,1)}), bf16[8,48,768]{2,1,0:T(8,128)(2,1)S(1)}, u32[]{:S(2)}, u32[]{:S(2)}) async-start(bf16[8,48,768]{2,1,0:T(8,128)(2,1)} %bitcast.9), calls=%async_computation | async-start | bytes 1179648 | tf_op jit(solution)/shard_map/all_to_all | solution.py:486
  (17 other events, 199.6 us)

commit v7 on v6

--- a/solution.py
+++ b/solution.py
@@ -452,8 +452,6 @@
     keep_mask = 1.0 - missing.astype(f32).reshape(8, 1, missing.shape[0] // 8)
     targets = pltpu.with_memory_space_constraint(targets, pltpu.HBM)
     bias = head_bias[None, :]
-    bias, far = lax.optimization_barrier((bias, features[0][1]))
-    features[0] = (features[0][0], far)
     carried, received = None, {}
     for steps in ORDER:
         if 0 in steps:
@@ -476,7 +474,6 @@
         for step, partial in zip(steps, results):
             received[step] = moved(partial, 1, 4 - step) if step else partial
     mine, theirs = total
-    theirs, received[1] = lax.optimization_barrier((theirs, received[1]))
     summed = sum(part.astype(f32) for part in received.values())
     half = summed.shape[0] // 2
     away = summed[half:].astype(bf16)

time: 156 us -> 154 us (0.987)
    all_to_all x1, waiting for transfers between devices: 5.34 us -> 8.23 us  [body(): gathered = lax.all_to_all(pair_sum, 'bz', 0, 0, tiled=True)]
    ppermute x24, waiting for transfers between devices: 36.4 us -> 33.6 us  [moved(): return lax.ppermute(value, ALL, pairs)]
    ppermute x24, starting transfers between devices: 44.1 us -> 42.3 us  [moved(): return lax.ppermute(value, ALL, pairs)]
  transfers between devices with their start and end apart: 28 -> 28, of which waited for: 15 -> 13; matrix products, arithmetic and copies ran while one was open for 2% -> 2% of each run, Pallas kernels for 23% -> 23%
where the time goes in v7:
time: 154 us; the launch traced here: 152 us
  starting transfers between devices  53.8 us (35%)
  waiting for transfers between devices  49.2 us (32%)
  Pallas kernels  42.1 us (27%)
  other arithmetic  3.33 us (2%)
  local copies, waits for them, and re-layouts  2.11 us (1%)
    ppermute x24, starting transfers between devices, moved(): return lax.ppermute(value, ALL, pairs)  42.3 us
    ppermute x24, waiting for transfers between devices, moved(): return lax.ppermute(value, ALL, pairs)  33.6 us
    pallas_call x4, Pallas kernels, head_pass(): pl.pallas_call(functools.partial(head_kernel, groups, first, last, positi...  26.4 us
    pallas_call x5, Pallas kernels, attend(): pl.pallas_call(functools.partial(attend_kernel, head_dim, state is None),...  9.5 us
    all_to_all x1, waiting for transfers between devices, body(): gathered = lax.all_to_all(pair_sum, 'bz', 0, 0, tiled=True)  8.23 us
    all_to_all x1, starting transfers between devices, body(): gathered = lax.all_to_all(pair_sum, 'bz', 0, 0, tiled=True)  6.54 us
    ppermute x1, waiting for transfers between devices, body(): after = lax.ppermute(to_prev, ALL, [(j, i) for i, j in nexts])  6.07 us
    pallas_call x1, Pallas kernels, finish(): pl.pallas_call(finish_kernel, in_specs=[pl.BlockSpec(memory_space=pltpu.S...  3.69 us
  transfers between devices with their start and end apart: 28, of which 13 were waited for; matrix products, arithmetic and copies ran while one was open for 2% of the time, Pallas kernels for 23%

profile of v7, /device:TPU:0, one launch (start us, length us, event | category | flops | bytes accessed | tf_op | source)
XLA Modules:
  0.0 151.6 jit_solution(11331183529699867631)
XLA Ops:
  2.4 2.1 %collective-permute-start = (bf16[64,256]{1,0:T(8,128)(2,1)S(1)}, bf16[64,256]{1,0:T(8,128)(2,1)S(1)}, u32[]{:S(2)}, u32[]{:S(2)}) collective-permute-start(bf16[64,256]{1,0:T(8,128)(2,1)S(1)} %get-tuple-element.39.refs_0_), channel_id=1, source_target_pairs={{0,64},{1,65},{2,66},{3,67},{4,68},{5,69},{6,70},{7,71},{8,72},{9,... | collective-permute-start | bytes 98312 | tf_op jit(solution)/shard_map/ppermute | solution.py:39
  4.4 2.2 %collective-permute-start.1 = (bf16[64,256]{1,0:T(8,128)(2,1)S(1)}, bf16[64,256]{1,0:T(8,128)(2,1)S(1)}, u32[]{:S(2)}, u32[]{:S(2)}) collective-permute-start(bf16[64,256]{1,0:T(8,128)(2,1)S(1)} %get-tuple-element.39.refs_0_), channel_id=1, source_target_pairs={{0,65},{1,64},{2,67},{3,66},{4,69},{5,68},{6,71},{7,70},{8,73},{9,... | collective-permute-start | bytes 98312 | tf_op jit(solution)/shard_map/ppermute | solution.py:39
  8.5 3.6 %collective-permute-done.2.refs_3_ = bf16[64,256]{1,0:T(8,128)(2,1)S(1)} collective-permute-done((bf16[64,256]{1,0:T(8,128)(2,1)S(1)}, bf16[64,256]{1,0:T(8,128)(2,1)S(1)}, u32[]{:S(2)}, u32[]{:S(2)}) %collective-permute-start.2) | collective-permute-done | bytes 32800 | tf_op jit(solution)/shard_map/ppermute | solution.py:39
  17.4 2.4 %collective-permute-done.3.refs_1_ = bf16[256,256]{1,0:T(8,128)(2,1)S(1)} collective-permute-done((bf16[256,256]{1,0:T(8,128)(2,1)S(1)}, bf16[256,256]{1,0:T(8,128)(2,1)S(1)}, u32[]{:S(2)}, u32[]{:S(2)}) %collective-permute-start.3) | collective-permute-done | bytes 131104 | tf_op jit(solution)/shard_map/ppermute | solution.py:39
  19.7 2.1 %collective-permute-done.5.refs_3_ = bf16[256,256]{1,0:T(8,128)(2,1)S(1)} collective-permute-done((bf16[256,256]{1,0:T(8,128)(2,1)S(1)}, bf16[256,256]{1,0:T(8,128)(2,1)S(1)}, u32[]{:S(2)}, u32[]{:S(2)}) %collective-permute-start.5) | collective-permute-done | bytes 131104 | tf_op jit(solution)/shard_map/ppermute | solution.py:39
  27.0 3.7 %collective-permute-start.8 = (bf16[8,768]{1,0:T(8,128)(2,1)S(1)}, bf16[8,768]{1,0:T(8,128)(2,1)S(1)}, u32[]{:S(2)}, u32[]{:S(2)}) collective-permute-start(bf16[8,768]{1,0:T(8,128)(2,1)S(1)} %get-tuple-element.40), channel_id=1, source_target_pairs={{0,1},{1,2},{2,3},{3,4},{4,5},{5,6},{6,7},{7,8},{8,9},{9,10},{10,1... | collective-permute-start | bytes 36872 | tf_op jit(solution)/shard_map/ppermute | solution.py:422
  33.4 6.1 %collective-permute-done.9.after_ref = bf16[8,768]{1,0:T(8,128)(2,1)S(1)} collective-permute-done((bf16[8,768]{1,0:T(8,128)(2,1)S(1)}, bf16[8,768]{1,0:T(8,128)(2,1)S(1)}, u32[]{:S(2)}, u32[]{:S(2)}) %collective-permute-start.9) | collective-permute-done | bytes 12320 | tf_op jit(solution)/shard_map/ppermute | solution.py:423
  39.4 3.0 %collective-permute-start.13 = (bf16[1024,256]{1,0:T(8,128)(2,1)S(1)}, bf16[1024,256]{1,0:T(8,128)(2,1)}, u32[]{:S(2)}, u32[]{:S(2)}) collective-permute-start(bf16[1024,256]{1,0:T(8,128)(2,1)S(1)} %collective-permute-done.7.refs_3_), channel_id=1, source_target_pairs={{0,8},{1,9},{2,10},{3,11},{4,12},{5,13},{6,14},{7,15},{8,0},{9,1},... | collective-permute-start | bytes 1572872 | tf_op jit(solution)/shard_map/ppermute | solution.py:39
  49.3 2.6 %attend.7 = (f32[528,128]{1,0:T(8,128)S(1)}, f32[528,128]{1,0:T(8,128)S(1)}) custom-call(bf16[64,1024]{1,0:T(8,128)(2,1)S(1)} %get-tuple-element.46.refs_0_, bf16[16,128]{1,0:T(8,128)(2,1)S(1)} %get-tuple-element.47.refs_1_, bf16[1024,256]{1,0:T(8,128)(2,1)} %collective-permute-done.13.refs_2_, bf16[1024,256]{1,0:T(8,128)(2,1)S(1)} %collective-permute-done.6.refs_3_, ...), custom_call_target="tpu_custom_call" | custom-call | flops 1107296256 | bytes 1048576 | tf_op jit(solution)/shard_map/attend/pallas_call | solution.py:188
  52.0 2.6 %attend.8 = (f32[528,128]{1,0:T(8,128)S(1)}, f32[528,128]{1,0:T(8,128)S(1)}) custom-call(bf16[64,1024]{1,0:T(8,128)(2,1)S(1)} %get-tuple-element.46.refs_0_, bf16[16,128]{1,0:T(8,128)(2,1)S(1)} %get-tuple-element.47.refs_1_, bf16[1024,256]{1,0:T(8,128)(2,1)} %collective-permute-done.12.refs_2_, bf16[1024,256]{1,0:T(8,128)(2,1)S(1)} %collective-permute-done.10.refs_3_, ...), custom_call_target="tpu_custom_call" | custom-call | flops 1107296256 | bytes 1048576 | tf_op jit(solution)/shard_map/attend/pallas_call | solution.py:188
  56.6 3.7 %finish.1.refs_0_ = bf16[256,768]{1,0:T(8,128)(2,1)S(1)} custom-call(s32[2]{0:T(128)S(1)} %pad_add_fusion.2.at_ref, f32[528,128]{1,0:T(8,128)S(1)} %get-tuple-element.58.num_ref, f32[528,128]{1,0:T(8,128)S(1)} %get-tuple-element.59.den_ref, bf16[64,1536]{1,0:T(8,128)(2,1)S(1)} %copy-done.4, bf16[8,768]{1,0:T(8,128)(2,1)S(1)} %collective-permute-done.8.before_ref, ...), custom_call_target="tpu_custom_call" | custom-call | flops 1862270976 | bytes 11403264 | tf_op jit(solution)/shard_map/finish/pallas_call | solution.py:260
  60.3 2.1 %collective-permute-start.16 = (bf16[256,768]{1,0:T(8,128)(2,1)S(1)}, bf16[256,768]{1,0:T(8,128)(2,1)S(1)}, u32[]{:S(2)}, u32[]{:S(2)}) collective-permute-start(bf16[256,768]{1,0:T(8,128)(2,1)S(1)} %finish.1.refs_0_), channel_id=1, source_target_pairs={{0,4},{1,5},{2,6},{3,7},{4,0},{5,1},{6,2},{7,3},{8,12},{9,13},{10,... | collective-permute-start | bytes 1179656 | tf_op jit(solution)/shard_map/ppermute | solution.py:39
  63.3 2.7 %collective-permute-start.19 = (bf16[256,768]{1,0:T(8,128)(2,1)S(1)}, bf16[256,768]{1,0:T(8,128)(2,1)S(1)}, u32[]{:S(2)}, u32[]{:S(2)}) collective-permute-start(bf16[256,768]{1,0:T(8,128)(2,1)S(1)} %finish.1.refs_0_), channel_id=1, source_target_pairs={{0,6},{1,7},{2,0},{3,1},{4,2},{5,3},{6,4},{7,5},{8,14},{9,15},{10,... | collective-permute-start | bytes 1179656 | tf_op jit(solution)/shard_map/ppermute | solution.py:39
  66.0 7.9 %collective-permute-done.16.refs_0_ = bf16[256,768]{1,0:T(8,128)(2,1)S(1)} collective-permute-done((bf16[256,768]{1,0:T(8,128)(2,1)S(1)}, bf16[256,768]{1,0:T(8,128)(2,1)S(1)}, u32[]{:S(2)}, u32[]{:S(2)}) %collective-permute-start.16) | collective-permute-done | bytes 393248 | tf_op jit(solution)/shard_map/ppermute | solution.py:39
  75.4 6.5 %collective-permute-done.21.refs_0_ = bf16[256,768]{1,0:T(8,128)(2,1)S(1)} collective-permute-done((bf16[256,768]{1,0:T(8,128)(2,1)S(1)}, bf16[256,768]{1,0:T(8,128)(2,1)S(1)}, u32[]{:S(2)}, u32[]{:S(2)}) %collective-permute-start.21) | collective-permute-done | bytes 393248 | tf_op jit(solution)/shard_map/ppermute | solution.py:39
  83.2 4.9 %collective-permute-start.20 = (bf16[256,768]{1,0:T(8,128)(2,1)S(1)}, bf16[256,768]{1,0:T(8,128)(2,1)S(1)}, u32[]{:S(2)}, u32[]{:S(2)}) collective-permute-start(bf16[256,768]{1,0:T(8,128)(2,1)S(1)} %collective-permute-done.19.refs_0_), channel_id=1, source_target_pairs={{0,1},{1,0},{2,3},{3,2},{4,5},{5,4},{6,7},{7,6},{8,9},{9,8},{10,11... | collective-permute-start | bytes 1179656 | tf_op jit(solution)/shard_map/ppermute | solution.py:39
  88.1 6.4 %head_pass.4 = (bf16[2048,768]{1,0:T(8,128)(2,1)}, bf16[512,768]{1,0:T(8,128)(2,1)S(1)}, f32[768,768]{1,0:T(8,128)S(1)}) custom-call(s32[3]{0:T(128)S(1)} %get-tuple-element.78.at_ref, bf16[256,768]{1,0:T(8,128)(2,1)S(1)} %collective-permute-done.16.refs_0_, bf16[256,768]{1,0:T(8,128)(2,1)S(1)} %collective-permute-done.17.refs_1_, ...), custom_call_target="tpu_custom_call" | custom-call | flops 1811939328 | bytes 6291456 | tf_op jit(solution)/shard_map/head_pass/pallas_call | solution.py:367
  96.0 6.6 %head_pass.5 = (bf16[2048,768]{1,0:T(8,128)(2,1)}, bf16[512,768]{1,0:T(8,128)(2,1)S(1)}, f32[768,768]{1,0:T(8,128)S(1)}) custom-call(s32[3]{0:T(128)S(1)} %get-tuple-element.75.at_ref, bf16[256,768]{1,0:T(8,128)(2,1)S(1)} %collective-permute-done.21.refs_0_, bf16[256,768]{1,0:T(8,128)(2,1)S(1)} %collective-permute-done.22.refs_1_, ...), custom_call_target="tpu_custom_call", output_to_operand_aliasing={{0}: (8, {})} | custom-call | flops 1811939328 | bytes 6291456 | tf_op jit(solution)/shard_map/head_pass/pallas_call | solution.py:367
  103.8 6.6 %head_pass.6 = (bf16[2048,768]{1,0:T(8,128)(2,1)}, bf16[512,768]{1,0:T(8,128)(2,1)S(1)}, f32[768,768]{1,0:T(8,128)S(1)}) custom-call(s32[3]{0:T(128)S(1)} %get-tuple-element.77.at_ref, bf16[256,768]{1,0:T(8,128)(2,1)S(1)} %collective-permute-done.19.refs_0_, bf16[256,768]{1,0:T(8,128)(2,1)S(1)} %collective-permute-done.20.refs_1_, ...), custom_call_target="tpu_custom_call", output_to_operand_aliasing={{0}: (8, {})} | custom-call | flops 1811939328 | bytes 6291456 | tf_op jit(solution)/shard_map/head_pass/pallas_call | solution.py:367
  110.4 6.7 %collective-permute-start.25 = (bf16[512,768]{1,0:T(8,128)(2,1)S(1)}, bf16[512,768]{1,0:T(8,128)(2,1)S(1)}, u32[]{:S(2)}, u32[]{:S(2)}) collective-permute-start(bf16[512,768]{1,0:T(8,128)(2,1)S(1)} %get-tuple-element.73), channel_id=1, source_target_pairs={{0,2},{1,3},{2,4},{3,5},{4,6},{5,7},{6,0},{7,1},{8,10},{9,11},{10,... | collective-permute-start | bytes 2359304 | tf_op jit(solution)/shard_map/ppermute | solution.py:39
  117.1 6.7 %head_pass.7 = (bf16[2048,768]{1,0:T(8,128)(2,1)}, bf16[512,768]{1,0:T(8,128)(2,1)S(1)}, f32[384,768]{1,0:T(8,128)S(1)}, bf16[384,768]{1,0:T(8,128)(2,1)S(1)}) custom-call(s32[3]{0:T(128)S(1)} %get-tuple-element.79.at_ref, bf16[256,768]{1,0:T(8,128)(2,1)S(1)} %finish.1.refs_0_, ...), custom_call_target="tpu_custom_call", output_to_operand_aliasing={{0}: (8, {})} | custom-call | flops 1811939328 | bytes 6291456 | tf_op jit(solution)/shard_map/head_pass/pallas_call | solution.py:367
  123.9 7.6 %collective-permute-done.25 = bf16[512,768]{1,0:T(8,128)(2,1)S(1)} collective-permute-done((bf16[512,768]{1,0:T(8,128)(2,1)S(1)}, bf16[512,768]{1,0:T(8,128)(2,1)S(1)}, u32[]{:S(2)}, u32[]{:S(2)}) %collective-permute-start.25) | collective-permute-done | bytes 786464 | tf_op jit(solution)/shard_map/ppermute | solution.py:39
  135.2 6.5 %all-to-all-start = ((bf16[8,48,768]{2,1,0:T(8,128)(2,1)}), bf16[8,48,768]{2,1,0:T(8,128)(2,1)S(1)}, u32[]{:S(2)}, u32[]{:S(2)}) async-start(bf16[8,48,768]{2,1,0:T(8,128)(2,1)} %bitcast.9), calls=%async_computation | async-start | bytes 1179648 | tf_op jit(solution)/shard_map/all_to_all | solution.py:483
  142.6 8.2 %all-to-all-done = bf16[8,48,768]{2,1,0:T(8,128)(2,1)S(1)} async-done(((bf16[8,48,768]{2,1,0:T(8,128)(2,1)}), bf16[8,48,768]{2,1,0:T(8,128)(2,1)S(1)}, u32[]{:S(2)}, u32[]{:S(2)}) %all-to-all-start) | async-done | bytes 589856 | tf_op jit(solution)/shard_map/all_to_all | solution.py:483
  (89 shorter events, 37.1 us)
Async XLA Ops:
  2.4 6.1 %collective-permute-start = (bf16[64,256]{1,0:T(8,128)(2,1)S(1)}, bf16[64,256]{1,0:T(8,128)(2,1)S(1)}, u32[]{:S(2)}, u32[]{:S(2)}) collective-permute-start(bf16[64,256]{1,0:T(8,128)(2,1)S(1)} %get-tuple-element.39.refs_0_), channel_id=1, source_target_pairs={{0,64},{1,65},{2,66},{3,67},{4,68},{5,69},{6,70},{7,71},{8,72},{9,... | collective-permute-start | bytes 98312 | tf_op jit(solution)/shard_map/ppermute | solution.py:39
  12.1 7.7 %collective-permute-start.3 = (bf16[256,256]{1,0:T(8,128)(2,1)S(1)}, bf16[256,256]{1,0:T(8,128)(2,1)S(1)}, u32[]{:S(2)}, u32[]{:S(2)}) collective-permute-start(bf16[256,256]{1,0:T(8,128)(2,1)S(1)} %join.2.refs_0_), channel_id=1, source_target_pairs={{0,2},{1,3},{2,4},{3,5},{4,6},{5,7},{6,0},{7,1},{8,10},{9,11},{10,... | collective-permute-start | bytes 393224 | tf_op jit(solution)/shard_map/ppermute | solution.py:39
  15.4 6.5 %collective-permute-start.5 = (bf16[256,256]{1,0:T(8,128)(2,1)S(1)}, bf16[256,256]{1,0:T(8,128)(2,1)S(1)}, u32[]{:S(2)}, u32[]{:S(2)}) collective-permute-start(bf16[256,256]{1,0:T(8,128)(2,1)S(1)} %join.2.refs_0_), channel_id=1, source_target_pairs={{0,4},{1,5},{2,6},{3,7},{4,0},{5,1},{6,2},{7,3},{8,12},{9,13},{10,... | collective-permute-start | bytes 393224 | tf_op jit(solution)/shard_map/ppermute | solution.py:39
  21.9 17.6 %collective-permute-start.7 = (bf16[1024,256]{1,0:T(8,128)(2,1)S(1)}, bf16[1024,256]{1,0:T(8,128)(2,1)S(1)}, u32[]{:S(2)}, u32[]{:S(2)}) collective-permute-start(bf16[1024,256]{1,0:T(8,128)(2,1)S(1)} %join.3.refs_2_), channel_id=1, source_target_pairs={{0,16},{1,17},{2,18},{3,19},{4,20},{5,21},{6,22},{7,23},{8,24},{9,... | collective-permute-start | bytes 1572872 | tf_op jit(solution)/shard_map/ppermute | solution.py:39
  23.4 21.7 %collective-permute-start.6 = (bf16[1024,256]{1,0:T(8,128)(2,1)S(1)}, bf16[1024,256]{1,0:T(8,128)(2,1)S(1)}, u32[]{:S(2)}, u32[]{:S(2)}) collective-permute-start(bf16[1024,256]{1,0:T(8,128)(2,1)S(1)} %join.3.refs_2_), channel_id=1, source_target_pairs={{0,48},{1,49},{2,50},{3,51},{4,52},{5,53},{6,54},{7,55},{8,56},{9,... | collective-permute-start | bytes 1572872 | tf_op jit(solution)/shard_map/ppermute | solution.py:39
  25.2 21.6 %collective-permute-start.10 = (bf16[1024,256]{1,0:T(8,128)(2,1)S(1)}, bf16[1024,256]{1,0:T(8,128)(2,1)S(1)}, u32[]{:S(2)}, u32[]{:S(2)}) collective-permute-start(bf16[1024,256]{1,0:T(8,128)(2,1)S(1)} %join.3.refs_2_), channel_id=1, source_target_pairs={{0,32},{1,33},{2,34},{3,35},{4,36},{5,37},{6,38},{7,39},{8,40},{9,... | collective-permute-start | bytes 1572872 | tf_op jit(solution)/shard_map/ppermute | solution.py:39
  27.0 20.9 %collective-permute-start.14 = (bf16[1024,256]{1,0:T(8,128)(2,1)S(1)}, bf16[1024,256]{1,0:T(8,128)(2,1)S(1)}, u32[]{:S(2)}, u32[]{:S(2)}) collective-permute-start(bf16[1024,256]{1,0:T(8,128)(2,1)S(1)} %join.3.refs_2_), channel_id=1, source_target_pairs={{0,8},{1,9},{2,10},{3,11},{4,12},{5,13},{6,14},{7,15},{8,0},{9,1},... | collective-permute-start | bytes 1572872 | tf_op jit(solution)/shard_map/ppermute | solution.py:39
  32.1 7.4 %collective-permute-start.9 = (bf16[8,768]{1,0:T(8,128)(2,1)S(1)}, bf16[8,768]{1,0:T(8,128)(2,1)S(1)}, u32[]{:S(2)}, u32[]{:S(2)}) collective-permute-start(bf16[8,768]{1,0:T(8,128)(2,1)S(1)} %get-tuple-element.41), channel_id=1, source_target_pairs={{1,0},{2,1},{3,2},{4,3},{5,4},{6,5},{7,6},{8,7},{9,8},{10,9},{11,1... | collective-permute-start | bytes 36872 | tf_op jit(solution)/shard_map/ppermute | solution.py:423
  39.4 9.9 %collective-permute-start.13 = (bf16[1024,256]{1,0:T(8,128)(2,1)S(1)}, bf16[1024,256]{1,0:T(8,128)(2,1)}, u32[]{:S(2)}, u32[]{:S(2)}) collective-permute-start(bf16[1024,256]{1,0:T(8,128)(2,1)S(1)} %collective-permute-done.7.refs_3_), channel_id=1, source_target_pairs={{0,8},{1,9},{2,10},{3,11},{4,12},{5,13},{6,14},{7,15},{8,0},{9,1},... | collective-permute-start | bytes 1572872 | tf_op jit(solution)/shard_map/ppermute | solution.py:39
  45.1 6.8 %collective-permute-start.12 = (bf16[1024,256]{1,0:T(8,128)(2,1)S(1)}, bf16[1024,256]{1,0:T(8,128)(2,1)}, u32[]{:S(2)}, u32[]{:S(2)}) collective-permute-start(bf16[1024,256]{1,0:T(8,128)(2,1)S(1)} %collective-permute-done.6.refs_3_), channel_id=1, source_target_pairs={{0,8},{1,9},{2,10},{3,11},{4,12},{5,13},{6,14},{7,15},{8,0},{9,1},... | collective-permute-start | bytes 1572872 | tf_op jit(solution)/shard_map/ppermute | solution.py:39
  46.8 7.8 %collective-permute-start.11 = (bf16[1024,256]{1,0:T(8,128)(2,1)S(1)}, bf16[1024,256]{1,0:T(8,128)(2,1)}, u32[]{:S(2)}, u32[]{:S(2)}) collective-permute-start(bf16[1024,256]{1,0:T(8,128)(2,1)S(1)} %collective-permute-done.10.refs_3_), channel_id=1, source_target_pairs={{0,8},{1,9},{2,10},{3,11},{4,12},{5,13},{6,14},{7,15},{8,0},{9,1},... | collective-permute-start | bytes 1572872 | tf_op jit(solution)/shard_map/ppermute | solution.py:39
  60.3 13.5 %collective-permute-start.16 = (bf16[256,768]{1,0:T(8,128)(2,1)S(1)}, bf16[256,768]{1,0:T(8,128)(2,1)S(1)}, u32[]{:S(2)}, u32[]{:S(2)}) collective-permute-start(bf16[256,768]{1,0:T(8,128)(2,1)S(1)} %finish.1.refs_0_), channel_id=1, source_target_pairs={{0,4},{1,5},{2,6},{3,7},{4,0},{5,1},{6,2},{7,3},{8,12},{9,13},{10,... | collective-permute-start | bytes 1179656 | tf_op jit(solution)/shard_map/ppermute | solution.py:39
  62.6 19.2 %collective-permute-start.21 = (bf16[256,768]{1,0:T(8,128)(2,1)S(1)}, bf16[256,768]{1,0:T(8,128)(2,1)S(1)}, u32[]{:S(2)}, u32[]{:S(2)}) collective-permute-start(bf16[256,768]{1,0:T(8,128)(2,1)S(1)} %finish.1.refs_0_), channel_id=1, source_target_pairs={{0,2},{1,3},{2,4},{3,5},{4,6},{5,7},{6,0},{7,1},{8,10},{9,11},{10,... | collective-permute-start | bytes 1179656 | tf_op jit(solution)/shard_map/ppermute | solution.py:39
  63.3 19.8 %collective-permute-start.19 = (bf16[256,768]{1,0:T(8,128)(2,1)S(1)}, bf16[256,768]{1,0:T(8,128)(2,1)S(1)}, u32[]{:S(2)}, u32[]{:S(2)}) collective-permute-start(bf16[256,768]{1,0:T(8,128)(2,1)S(1)} %finish.1.refs_0_), channel_id=1, source_target_pairs={{0,6},{1,7},{2,0},{3,1},{4,2},{5,3},{6,4},{7,5},{8,14},{9,15},{10,... | collective-permute-start | bytes 1179656 | tf_op jit(solution)/shard_map/ppermute | solution.py:39
  73.9 14.2 %collective-permute-start.17 = (bf16[256,768]{1,0:T(8,128)(2,1)S(1)}, bf16[256,768]{1,0:T(8,128)(2,1)S(1)}, u32[]{:S(2)}, u32[]{:S(2)}) collective-permute-start(bf16[256,768]{1,0:T(8,128)(2,1)S(1)} %collective-permute-done.16.refs_0_), channel_id=1, source_target_pairs={{0,1},{1,0},{2,3},{3,2},{4,5},{5,4},{6,7},{7,6},{8,9},{9,8},{10,11... | collective-permute-start | bytes 1179656 | tf_op jit(solution)/shard_map/ppermute | solution.py:39
  81.9 14.1 %collective-permute-start.22 = (bf16[256,768]{1,0:T(8,128)(2,1)S(1)}, bf16[256,768]{1,0:T(8,128)(2,1)S(1)}, u32[]{:S(2)}, u32[]{:S(2)}) collective-permute-start(bf16[256,768]{1,0:T(8,128)(2,1)S(1)} %collective-permute-done.21.refs_0_), channel_id=1, source_target_pairs={{0,1},{1,0},{2,3},{3,2},{4,5},{5,4},{6,7},{7,6},{8,9},{9,8},{10,11... | collective-permute-start | bytes 1179656 | tf_op jit(solution)/shard_map/ppermute | solution.py:39
  83.2 20.6 %collective-permute-start.20 = (bf16[256,768]{1,0:T(8,128)(2,1)S(1)}, bf16[256,768]{1,0:T(8,128)(2,1)S(1)}, u32[]{:S(2)}, u32[]{:S(2)}) collective-permute-start(bf16[256,768]{1,0:T(8,128)(2,1)S(1)} %collective-permute-done.19.refs_0_), channel_id=1, source_target_pairs={{0,1},{1,0},{2,3},{3,2},{4,5},{5,4},{6,7},{7,6},{8,9},{9,8},{10,11... | collective-permute-start | bytes 1179656 | tf_op jit(solution)/shard_map/ppermute | solution.py:39
  94.5 22.6 %collective-permute-start.18 = (bf16[512,768]{1,0:T(8,128)(2,1)S(1)}, bf16[512,768]{1,0:T(8,128)(2,1)S(1)}, u32[]{:S(2)}, u32[]{:S(2)}) collective-permute-start(bf16[512,768]{1,0:T(8,128)(2,1)S(1)} %get-tuple-element.60), channel_id=1, source_target_pairs={{0,4},{1,5},{2,6},{3,7},{4,0},{5,1},{6,2},{7,3},{8,12},{9,13},{10,... | collective-permute-start | bytes 2359304 | tf_op jit(solution)/shard_map/ppermute | solution.py:39
  95.4 21.7 %collective-permute-start.15 = (bf16[256,768]{1,0:T(8,128)(2,1)S(1)}, bf16[256,768]{1,0:T(8,128)(2,1)S(1)}, u32[]{:S(2)}, u32[]{:S(2)}) collective-permute-start(bf16[256,768]{1,0:T(8,128)(2,1)S(1)} %finish.1.refs_0_), channel_id=1, source_target_pairs={{0,1},{1,0},{2,3},{3,2},{4,5},{5,4},{6,7},{7,6},{8,9},{9,8},{10,11... | collective-permute-start | bytes 1179656 | tf_op jit(solution)/shard_map/ppermute | solution.py:39
  110.4 21.1 %collective-permute-start.25 = (bf16[512,768]{1,0:T(8,128)(2,1)S(1)}, bf16[512,768]{1,0:T(8,128)(2,1)S(1)}, u32[]{:S(2)}, u32[]{:S(2)}) collective-permute-start(bf16[512,768]{1,0:T(8,128)(2,1)S(1)} %get-tuple-element.73), channel_id=1, source_target_pairs={{0,2},{1,3},{2,4},{3,5},{4,6},{5,7},{6,0},{7,1},{8,10},{9,11},{10,... | collective-permute-start | bytes 2359304 | tf_op jit(solution)/shard_map/ppermute | solution.py:39
  117.1 14.9 %collective-permute-start.24 = (bf16[512,768]{1,0:T(8,128)(2,1)S(1)}, bf16[512,768]{1,0:T(8,128)(2,1)S(1)}, u32[]{:S(2)}, u32[]{:S(2)}) collective-permute-start(bf16[512,768]{1,0:T(8,128)(2,1)S(1)} %get-tuple-element.72), channel_id=1, source_target_pairs={{0,6},{1,7},{2,0},{3,1},{4,2},{5,3},{6,4},{7,5},{8,14},{9,15},{10,... | collective-permute-start | bytes 2359304 | tf_op jit(solution)/shard_map/ppermute | solution.py:39
  123.8 10.4 %collective-permute-start.23 = (bf16[384,768]{1,0:T(8,128)(2,1)S(1)}, bf16[384,768]{1,0:T(8,128)(2,1)S(1)}, u32[]{:S(2)}, u32[]{:S(2)}) collective-permute-start(bf16[384,768]{1,0:T(8,128)(2,1)S(1)} %get-tuple-element.70), channel_id=1, source_target_pairs={{0,8},{8,0},{1,9},{9,1},{2,10},{10,2},{3,11},{11,3},{4,12},{12,4},... | collective-permute-start | bytes 1769480 | tf_op jit(solution)/shard_map/ppermute | solution.py:481
  132.4 9.4 %collective-permute-start.26 = (bf16[256,768]{1,0:T(8,128)(2,1)S(1)}, bf16[256,768]{1,0:T(8,128)(2,1)S(1)}, u32[]{:S(2)}, u32[]{:S(2)}) collective-permute-start(bf16[256,768]{1,0:T(8,128)(2,1)S(1)} %slice.15), channel_id=1, source_target_pairs={{0,1},{1,0},{2,3},{3,2},{4,5},{5,4},{6,7},{7,6},{8,9},{9,8},{10,11... | collective-permute-start | bytes 1179656 | tf_op jit(solution)/shard_map/ppermute | solution.py:39
  135.2 15.6 %all-to-all-start = ((bf16[8,48,768]{2,1,0:T(8,128)(2,1)}), bf16[8,48,768]{2,1,0:T(8,128)(2,1)S(1)}, u32[]{:S(2)}, u32[]{:S(2)}) async-start(bf16[8,48,768]{2,1,0:T(8,128)(2,1)} %bitcast.9), calls=%async_computation | async-start | bytes 1179648 | tf_op jit(solution)/shard_map/all_to_all | solution.py:483
  (17 other events, 201.6 us)
